TPU v7x, 128 devices: a whole 4x4x4 slice. The times are simulated.
128 devices in a mesh: circ: 8 (over z_lo, x), axial: 16 (over y, z_hi, core).
Axes of the slice: x: 4, y: 4, z: 4 (z_hi: 2, z_lo: 2; z = z_hi * 2 + z_lo), core: 2. Of those that a mesh axis runs over, the one named last changes fastest.
Arguments:
- calcium: float32 [2, 1024, 4096], P(None, 'circ', 'axial'), may hold values from 0.1 to 3
- voltage: float32 [2, 1024, 4096], P(None, 'circ', 'axial'), may hold values from -1.5 to 0.5
- conductance: float32 [1024, 4096], P('circ', 'axial'), may hold values from 0.5 to 2
- fluid_blocks: float32 [24576, 2, 256], P(('circ', 'axial')), may hold values from -9 to 9
- target_device: int32 [24576, 1], P(('circ', 'axial')), may hold values from 0 to 127; in each aligned block of 192 rows (0 to 191, 192 to 383, ...) at most 2 rows name the same one
- target_row: int32 [24576], P(('circ', 'axial')), may hold values from 0 to 127
- block_counts: int32 [128], P(('circ', 'axial')), may hold values from 96 to 192
- port_cells: int32 [1024], P(('circ', 'axial')), may hold values from 0 to 32767
- partner: int32 [1024], P(('circ', 'axial')), may hold values from 0 to 1023, each once
Outputs:
- calcium_out: float32 [2, 1024, 4096], P(None, 'circ', 'axial')
- voltage_out: float32 [2, 1024, 4096], P(None, 'circ', 'axial')
Inputs may be any that keep to these rules, and one draw needn't show every extreme that they name: `target_device`: among the 192 slots of one device, used or not, no device number appears more than 2 times, and some number appears exactly 2 times. Only a device's first block_counts slots are used. `port_cells`: ports may share a cell.
All inputs are finite; a program needn't handle non-finite values.
Results may differ from a plain program's by a relative error of at most 0.00002.
Values sent between devices are 32-bit elements; how exact they have to be, the bound alone decides.
No kernel may reach another device: no remote copies, remote signals or barrier semaphores. Data moves between devices by JAX's collectives and lax.ppermute only.
A program may use at most 64 MiB of HBM per device.

v0:
```python
import jax
import jax.numpy as jnp
from jax import lax
from jax.sharding import PartitionSpec as P

ITERS = 8
SLOT = 2


rate_step = 0.1
couple_step = 0.05
junction_step = 0.2


def padded(block, sides, width, periodic):
    for axis, dim in sides:
        count = lax.axis_size(axis)
        forward = [(i, i + 1) for i in range(count - 1)]
        if periodic:
            forward.append((count - 1, 0))
        backward = [(target, source) for source, target in forward]
        low = lax.ppermute(
            lax.slice_in_dim(block, block.shape[dim] - width, None, axis=dim), axis, forward
        )
        high = lax.ppermute(lax.slice_in_dim(block, 0, width, axis=dim), axis, backward)
        block = jnp.concatenate([low, block, high], axis=dim)
    return block


def split_up(value, dim, size):
    before, after = (value.shape[:dim], value.shape[dim + 1 :])
    return jnp.moveaxis(value.reshape(*before, size, -1, *after), dim, 0)


def joined_along(pieces, dim):
    pieces = jnp.moveaxis(pieces, 0, dim)
    shape = pieces.shape
    return pieces.reshape(*shape[:dim], shape[dim] * shape[dim + 1], *shape[dim + 2 :])


def one_exchange(value, axis, axes, splits, concats):
    sizes = [lax.axis_size(a) for a in axes]
    pieces = split_up(value, splits[0], sizes[0])
    pieces = jnp.moveaxis(split_up(pieces, splits[1] + 1, sizes[1]), 0, 1)
    inside = pieces.shape[2:]
    pieces = pieces.reshape(-1, *inside)
    pieces = lax.all_to_all(pieces, axis, split_axis=0, concat_axis=0, tiled=True)
    pieces = joined_along(pieces.reshape(*sizes, *inside), concats[0] + 1)
    return joined_along(pieces, concats[1])


def advance(calcium, voltage, near_calcium, near_voltage, spread, stress, stimulus):
    smc_ca = calcium[0]
    end_ca = calcium[1]
    smc_volt = voltage[0]
    end_volt = voltage[1]
    new_smc_ca = (
        smc_ca
        + rate_step
        * (
            0.8 * jax.nn.sigmoid(2.0 * (smc_volt + 0.3))
            + stimulus
            - 1.2 * smc_ca / (smc_ca + 0.5)
            + 0.3 * (end_ca - smc_ca)
        )
        + spread * (near_calcium[0] - 4.0 * smc_ca)
    )
    new_end_ca = (
        end_ca
        + rate_step * (0.2 + 1.5 * stress + 0.4 * stimulus - 0.9 * end_ca + 0.3 * (smc_ca - end_ca))
        + spread * (near_calcium[1] - 4.0 * end_ca)
    )
    new_smc_volt = (
        smc_volt
        + rate_step
        * (
            -(smc_volt + 0.5)
            - 1.5 * smc_ca / (smc_ca + 1.0) * (smc_volt + 1.2)
            + 0.4 * (end_volt - smc_volt)
        )
        + spread * (near_voltage[0] - 4.0 * smc_volt)
    )
    new_end_volt = (
        end_volt
        + rate_step
        * (
            -0.8 * (end_volt + 0.4)
            - end_ca / (end_ca + 1.0) * (end_volt + 1.2)
            + 0.4 * (smc_volt - end_volt)
        )
        + spread * (near_voltage[1] - 4.0 * end_volt)
    )
    return (jnp.stack([new_smc_ca, new_end_ca]), jnp.stack([new_smc_volt, new_end_volt]))


def neighbours(fields):
    cycle_pad = padded(fields, (("circ", 1),), 1, True)
    strip_pad = padded(fields, (("axial", 2),), 1, False)
    first = lax.axis_index("axial") == 0
    final = lax.axis_index("axial") == lax.axis_size("axial") - 1
    left_side = strip_pad[:, :, :-2]
    right_side = strip_pad[:, :, 2:]
    left_side = left_side.at[:, :, 0].set(jnp.where(first, fields[:, :, 0], left_side[:, :, 0]))
    right_side = right_side.at[:, :, -1].set(
        jnp.where(final, fields[:, :, -1], right_side[:, :, -1])
    )
    return cycle_pad[:, :-2] + cycle_pad[:, 2:] + left_side + right_side


def local(
    calcium,
    voltage,
    conductance,
    fluid_blocks,
    target_device,
    target_row,
    block_counts,
    port_cells,
    partner,
):
    cycle_count = lax.axis_size("circ")
    strip_count = lax.axis_size("axial")
    devices = cycle_count * strip_count
    slot_count = fluid_blocks.shape[0]
    width = fluid_blocks.shape[2]
    row_count = conductance.shape[0]
    order_idx = jnp.arange(slot_count, dtype=jnp.int32)
    active = order_idx < block_counts[0]
    target = target_device[:, 0]
    earlier = (
        (target[:, None] == target[None, :])
        & active[None, :]
        & (order_idx[None, :] < order_idx[:, None])
    )
    slot_rank = jnp.sum(earlier.astype(jnp.int32), axis=1)
    position = jnp.where(active, target * SLOT + slot_rank, devices * SLOT)
    outgoing = (
        jnp.zeros((devices * SLOT, 2, width), jnp.float32)
        .at[position]
        .set(fluid_blocks, mode="drop")
    )
    row_tags = (
        jnp.full((devices * SLOT,), row_count, jnp.int32).at[position].set(target_row, mode="drop")
    )
    received, recv_rows = (
        one_exchange(
            outgoing.reshape(cycle_count, strip_count, SLOT, 2, width),
            ("circ", "axial"),
            ("circ", "axial"),
            (0, 1),
            (0, 1),
        ),
        one_exchange(
            row_tags.reshape(cycle_count, strip_count, SLOT),
            ("circ", "axial"),
            ("circ", "axial"),
            (0, 1),
            (0, 1),
        ),
    )
    received = received.reshape(devices * SLOT, 2, width)
    recv_rows = recv_rows.reshape(devices * SLOT)
    forcing = jnp.zeros((row_count, 2, width), jnp.float32).at[recv_rows].add(received, mode="drop")
    shear = forcing[:, 0]
    agonist = forcing[:, 1]
    stress = shear * shear / (1.0 + shear * shear)
    stimulus = jax.nn.sigmoid(agonist)
    spread = couple_step * conductance
    for substep in range(ITERS):
        flat_volt = voltage[0].reshape(-1)
        port_values = flat_volt[port_cells]
        all_ports = lax.all_gather(port_values, ("circ", "axial"), axis=0, tiled=True)
        gain_term = junction_step * (all_ports[partner] - port_values)
        calcium_new, voltage_new = advance(
            calcium, voltage, neighbours(calcium), neighbours(voltage), spread, stress, stimulus
        )
        smc_volt = (
            voltage_new[0].reshape(-1).at[port_cells].add(gain_term).reshape(voltage_new[0].shape)
        )
        voltage = jnp.stack([smc_volt, voltage_new[1]])
        calcium = calcium_new
    return (calcium, voltage)


def solution(mesh):
    return jax.shard_map(
        local,
        mesh=mesh,
        in_specs=(
            P(None, "circ", "axial"),
            P(None, "circ", "axial"),
            P("circ", "axial"),
            P(("circ", "axial"), None, None),
            P(("circ", "axial"), None),
            P(("circ", "axial")),
            P(("circ", "axial")),
            P(("circ", "axial")),
            P(("circ", "axial")),
        ),
        out_specs=(P(None, "circ", "axial"), P(None, "circ", "axial")),
        check_vma=False,
    )
```

profile of v0, /device:TPU:1, one launch (start us, length us, event | category | flops | bytes accessed | tf_op | source)
XLA Modules:
  0.0 836.0 jit_solution(10530676364718597587)
XLA Ops:
  1.8 6.9 collective-permute-start.6
  13.7 6.0 collective-permute-start.2
  23.4 8.4 %all-to-all-start = ((s32[128,1,1,2]{3,2,1,0:T(1,128)}), s32[128,1,1,2]{3,2,1,0:T(1,128)S(1)}, u32[]{:S(2)}, u32[]{:S(2)}) async-start(s32[128,1,1,2]{3,2,1,0:T(1,128)} %bitcast.6), calls=%async_computation | async-start | bytes 131072 | tf_op jit(solution)/shard_map/all_to_all | solution.py:47
  33.6 67.1 %all-reduce = f32[1024]{0:T(1024)S(1)} all-reduce(f32[1024]{0:T(1024)S(1)} %dynamic-update-slice.96), channel_id=2, replica_groups=mesh['circ'=8,'axial'=16] {'circ','axial'}, use_global_device_ids=true, to_apply=%add | all-reduce | flops 1024 | bytes 8192
  102.4 18.7 %scatter_fusion = f32[256,2,256]{2,1,0:T(2,128)} fusion(f32[256,2,256]{2,1,0:T(2,128)} %broadcast_in_dim.14, s32[192]{0:T(256)S(1)} %bitcast.653, f32[192,2,256]{2,1,0:T(2,128)S(1)} %copy-done.3), kind=kCustom, calls=%fused_computation.17 | custom fusion | bytes 1180416 | tf_op jit(solution)/shard_map/scatter | solution.py:140
  132.3 5.0 collective-permute-done.3
  144.0 65.0 %all-reduce.1 = f32[1024]{0:T(1024)S(1)} all-reduce(f32[1024]{0:T(1024)S(1)} %dynamic-update-slice.97), channel_id=3, replica_groups=mesh['circ'=8,'axial'=16] {'circ','axial'}, use_global_device_ids=true, to_apply=%add.1 | all-reduce | flops 1024 | bytes 8192
  219.3 9.3 %scatter_fusion.1 = f32[128,2,256]{2,1,0:T(2,128)S(1)} fusion(f32[128,2,256]{2,1,0:T(2,128)S(1)} %broadcast_in_dim.12, s32[256]{0:T(256)S(1)} %bitcast.654, f32[256,2,256]{2,1,0:T(2,128)S(1)} %bitcast.648), kind=kCustom, calls=%fused_computation.18 | custom fusion | flops 131072 | bytes 1573888 | tf_op jit(solution)/shard_map/scatter-add | solution.py:163
  230.7 5.7 collective-permute-start.22
  238.7 64.4 %all-reduce.2 = f32[1024]{0:T(1024)S(1)} all-reduce(f32[1024]{0:T(1024)S(1)} %dynamic-update-slice.98), channel_id=4, replica_groups=mesh['circ'=8,'axial'=16] {'circ','axial'}, use_global_device_ids=true, to_apply=%add.2 | all-reduce | flops 1024 | bytes 8192
  312.4 4.6 collective-permute-done.23
  318.9 5.8 collective-permute-done.11
  330.9 6.0 collective-permute-start.18
  337.2 63.5 %all-reduce.3 = f32[1024]{0:T(1024)S(1)} all-reduce(f32[1024]{0:T(1024)S(1)} %dynamic-update-slice.99), channel_id=5, replica_groups=mesh['circ'=8,'axial'=16] {'circ','axial'}, use_global_device_ids=true, to_apply=%add.3 | all-reduce | flops 1024 | bytes 8192
  409.6 4.9 collective-permute-done.31
  416.5 5.8 collective-permute-done.19
  428.7 6.0 collective-permute-start.26
  434.9 64.6 %all-reduce.4 = f32[1024]{0:T(1024)S(1)} all-reduce(f32[1024]{0:T(1024)S(1)} %dynamic-update-slice.100), channel_id=6, replica_groups=mesh['circ'=8,'axial'=16] {'circ','axial'}, use_global_device_ids=true, to_apply=%add.4 | all-reduce | flops 1024 | bytes 8192
  515.3 5.8 collective-permute-done.27
  527.3 5.9 collective-permute-start.34
  533.5 63.7 %all-reduce.5 = f32[1024]{0:T(1024)S(1)} all-reduce(f32[1024]{0:T(1024)S(1)} %dynamic-update-slice.101), channel_id=7, replica_groups=mesh['circ'=8,'axial'=16] {'circ','axial'}, use_global_device_ids=true, to_apply=%add.5 | all-reduce | flops 1024 | bytes 8192
  606.4 4.7 collective-permute-done.47
  613.0 5.8 collective-permute-done.35
  625.3 5.9 collective-permute-start.42
  631.5 64.4 %all-reduce.6 = f32[1024]{0:T(1024)S(1)} all-reduce(f32[1024]{0:T(1024)S(1)} %dynamic-update-slice.102), channel_id=8, replica_groups=mesh['circ'=8,'axial'=16] {'circ','axial'}, use_global_device_ids=true, to_apply=%add.6 | all-reduce | flops 1024 | bytes 8192
  705.0 4.7 collective-permute-done.55
  711.7 5.8 collective-permute-done.43
  723.7 5.9 collective-permute-start.50
  729.9 63.7 %all-reduce.7 = f32[1024]{0:T(1024)S(1)} all-reduce(f32[1024]{0:T(1024)S(1)} %dynamic-update-slice.103), channel_id=9, replica_groups=mesh['circ'=8,'axial'=16] {'circ','axial'}, use_global_device_ids=true, to_apply=%add.7 | all-reduce | flops 1024 | bytes 8192
  802.8 4.7 collective-permute-done.63
  809.4 5.8 collective-permute-done.51
  827.7 5.8 collective-permute-done.59
  (348 shorter events, 161.8 us)
Async XLA Ops:
  1.8 124.0 %collective-permute-start.6 = (f32[2,128,1]{2,1,0:T(8,128)S(1)}, f32[2,128,1]{2,1,0:T(8,128)S(1)}, u32[]{:S(2)}, u32[]{:S(2)}) collective-permute-start(f32[2,128,1]{2,1,0:T(8,128)S(1)} %get-tuple-element.533), channel_id=1, source_target_pairs={{0,1},{1,2},{2,3},{3,4},{4,5},{5,6},{6,7},{7,8},{8,9},{9,10},{10,1... | collective-permute-start | bytes 3080 | tf_op jit(solution)/shard_map/ppermute | solution.py:22
  8.7 120.1 %collective-permute-start.7 = (f32[2,128,1]{2,1,0:T(8,128)S(1)}, f32[2,128,1]{2,1,0:T(8,128)S(1)}, u32[]{:S(2)}, u32[]{:S(2)}) collective-permute-start(f32[2,128,1]{2,1,0:T(8,128)S(1)} %get-tuple-element.534), channel_id=1, source_target_pairs={{1,0},{2,1},{3,2},{4,3},{5,4},{6,5},{7,6},{8,7},{9,8},{10,9},{11,1... | collective-permute-start | bytes 3080 | tf_op jit(solution)/shard_map/ppermute | solution.py:25
  10.6 128.6 %collective-permute-start.5 = (f32[2,1,256]{2,1,0:T(1,128)S(1)}, f32[2,1,256]{2,1,0:T(1,128)S(1)}, u32[]{:S(2)}, u32[]{:S(2)}) collective-permute-start(f32[2,1,256]{2,1,0:T(1,128)S(1)} %get-tuple-element.528), channel_id=1, source_target_pairs={{16,0},{32,16},{48,32},{64,48},{80,64},{96,80},{112,96},{0,112},{1... | collective-permute-start | bytes 6152 | tf_op jit(solution)/shard_map/ppermute | solution.py:25
  13.6 125.6 %collective-permute-start.4 = (f32[2,1,256]{2,1,0:T(1,128)S(1)}, f32[2,1,256]{2,1,0:T(1,128)S(1)}, u32[]{:S(2)}, u32[]{:S(2)}) collective-permute-start(f32[2,1,256]{2,1,0:T(1,128)S(1)} %get-tuple-element.527), channel_id=1, source_target_pairs={{0,16},{16,32},{32,48},{48,64},{64,80},{80,96},{96,112},{112,0},{1... | collective-permute-start | bytes 6152 | tf_op jit(solution)/shard_map/ppermute | solution.py:22
  13.7 118.5 %collective-permute-start.2 = (f32[2,128,1]{2,1,0:T(8,128)S(1)}, f32[2,128,1]{2,1,0:T(8,128)S(1)}, u32[]{:S(2)}, u32[]{:S(2)}) collective-permute-start(f32[2,128,1]{2,1,0:T(8,128)S(1)} %get-tuple-element.521), channel_id=1, source_target_pairs={{0,1},{1,2},{2,3},{3,4},{4,5},{5,6},{6,7},{7,8},{8,9},{9,10},{10,1... | collective-permute-start | bytes 3080 | tf_op jit(solution)/shard_map/ppermute | solution.py:22
  23.4 97.6 %all-to-all-start = ((s32[128,1,1,2]{3,2,1,0:T(1,128)}), s32[128,1,1,2]{3,2,1,0:T(1,128)S(1)}, u32[]{:S(2)}, u32[]{:S(2)}) async-start(s32[128,1,1,2]{3,2,1,0:T(1,128)} %bitcast.6), calls=%async_computation | async-start | bytes 131072 | tf_op jit(solution)/shard_map/all_to_all | solution.py:47
  121.1 98.1 %all-to-all-start.1 = ((f32[128,1,1,2,2,256]{5,4,3,2,1,0:T(2,128)}), f32[128,1,1,2,2,256]{5,4,3,2,1,0:T(2,128)S(1)}, u32[]{:S(2)}, u32[]{:S(2)}) async-start(f32[128,1,1,2,2,256]{5,4,3,2,1,0:T(2,128)} %bitcast.13), calls=%async_computation.1 | async-start | bytes 1048576 | tf_op jit(solution)/shard_map/all_to_all | solution.py:47
  128.8 80.9 %collective-permute-start.1 = (f32[2,1,256]{2,1,0:T(1,128)S(1)}, f32[2,1,256]{2,1,0:T(1,128)S(1)}, u32[]{:S(2)}, u32[]{:S(2)}) collective-permute-start(f32[2,1,256]{2,1,0:T(1,128)S(1)} %get-tuple-element.516), channel_id=1, source_target_pairs={{16,0},{32,16},{48,32},{64,48},{80,64},{96,80},{112,96},{0,112},{1... | collective-permute-start | bytes 6152 | tf_op jit(solution)/shard_map/ppermute | solution.py:25
  132.2 77.5 %collective-permute-start = (f32[2,1,256]{2,1,0:T(1,128)S(1)}, f32[2,1,256]{2,1,0:T(1,128)S(1)}, u32[]{:S(2)}, u32[]{:S(2)}) collective-permute-start(f32[2,1,256]{2,1,0:T(1,128)S(1)} %get-tuple-element.515), channel_id=1, source_target_pairs={{0,16},{16,32},{32,48},{48,64},{64,80},{80,96},{96,112},{112,0},{1... | collective-permute-start | bytes 6152 | tf_op jit(solution)/shard_map/ppermute | solution.py:22
  141.8 67.9 %collective-permute-start.14 = (f32[2,128,1]{2,1,0:T(8,128)S(1)}, f32[2,128,1]{2,1,0:T(8,128)S(1)}, u32[]{:S(2)}, u32[]{:S(2)}) collective-permute-start(f32[2,128,1]{2,1,0:T(8,128)S(1)} %fusion.112), channel_id=1, source_target_pairs={{0,1},{1,2},{2,3},{3,4},{4,5},{5,6},{6,7},{7,8},{8,9},{9,10},{10,1... | collective-permute-start | bytes 3080 | tf_op jit(solution)/shard_map/ppermute | solution.py:22
  230.7 77.9 %collective-permute-start.22 = (f32[2,128,1]{2,1,0:T(8,128)S(1)}, f32[2,128,1]{2,1,0:T(8,128)S(1)}, u32[]{:S(2)}, u32[]{:S(2)}) collective-permute-start(f32[2,128,1]{2,1,0:T(8,128)S(1)} %fusion.110), channel_id=1, source_target_pairs={{0,1},{1,2},{2,3},{3,4},{4,5},{5,6},{6,7},{7,8},{8,9},{9,10},{10,1... | collective-permute-start | bytes 3080 | tf_op jit(solution)/shard_map/ppermute | solution.py:22
  236.5 72.2 %collective-permute-start.10 = (f32[2,128,1]{2,1,0:T(8,128)S(1)}, f32[2,128,1]{2,1,0:T(8,128)S(1)}, u32[]{:S(2)}, u32[]{:S(2)}) collective-permute-start(f32[2,128,1]{2,1,0:T(8,128)S(1)} %fusion.113), channel_id=1, source_target_pairs={{0,1},{1,2},{2,3},{3,4},{4,5},{5,6},{6,7},{7,8},{8,9},{9,10},{10,1... | collective-permute-start | bytes 3080 | tf_op jit(solution)/shard_map/ppermute | solution.py:22
  303.8 22.0 %collective-permute-start.21 = (f32[2,1,256]{2,1,0:T(1,128)S(1)}, f32[2,1,256]{2,1,0:T(1,128)S(1)}, u32[]{:S(2)}, u32[]{:S(2)}) collective-permute-start(f32[2,1,256]{2,1,0:T(1,128)S(1)} %get-tuple-element.510), channel_id=1, source_target_pairs={{16,0},{32,16},{48,32},{64,48},{80,64},{96,80},{112,96},{0,112},{1... | collective-permute-start | bytes 6152 | tf_op jit(solution)/shard_map/ppermute | solution.py:25
  328.9 77.5 %collective-permute-start.30 = (f32[2,128,1]{2,1,0:T(8,128)S(1)}, f32[2,128,1]{2,1,0:T(8,128)S(1)}, u32[]{:S(2)}, u32[]{:S(2)}) collective-permute-start(f32[2,128,1]{2,1,0:T(8,128)S(1)} %fusion.108), channel_id=1, source_target_pairs={{0,1},{1,2},{2,3},{3,4},{4,5},{5,6},{6,7},{7,8},{8,9},{9,10},{10,1... | collective-permute-start | bytes 3080 | tf_op jit(solution)/shard_map/ppermute | solution.py:22
  330.9 75.5 %collective-permute-start.18 = (f32[2,128,1]{2,1,0:T(8,128)S(1)}, f32[2,128,1]{2,1,0:T(8,128)S(1)}, u32[]{:S(2)}, u32[]{:S(2)}) collective-permute-start(f32[2,128,1]{2,1,0:T(8,128)S(1)} %fusion.111), channel_id=1, source_target_pairs={{0,1},{1,2},{2,3},{3,4},{4,5},{5,6},{6,7},{7,8},{8,9},{9,10},{10,1... | collective-permute-start | bytes 3080 | tf_op jit(solution)/shard_map/ppermute | solution.py:22
  401.4 22.2 %collective-permute-start.29 = (f32[2,1,256]{2,1,0:T(1,128)S(1)}, f32[2,1,256]{2,1,0:T(1,128)S(1)}, u32[]{:S(2)}, u32[]{:S(2)}) collective-permute-start(f32[2,1,256]{2,1,0:T(1,128)S(1)} %get-tuple-element.502), channel_id=1, source_target_pairs={{16,0},{32,16},{48,32},{64,48},{80,64},{96,80},{112,96},{0,112},{1... | collective-permute-start | bytes 6152 | tf_op jit(solution)/shard_map/ppermute | solution.py:25
  402.9 21.7 %collective-permute-start.17 = (f32[2,1,256]{2,1,0:T(1,128)S(1)}, f32[2,1,256]{2,1,0:T(1,128)S(1)}, u32[]{:S(2)}, u32[]{:S(2)}) collective-permute-start(f32[2,1,256]{2,1,0:T(1,128)S(1)} %get-tuple-element.498), channel_id=1, source_target_pairs={{16,0},{32,16},{48,32},{64,48},{80,64},{96,80},{112,96},{0,112},{1... | collective-permute-start | bytes 6152 | tf_op jit(solution)/shard_map/ppermute | solution.py:25
  426.6 78.3 %collective-permute-start.38 = (f32[2,128,1]{2,1,0:T(8,128)S(1)}, f32[2,128,1]{2,1,0:T(8,128)S(1)}, u32[]{:S(2)}, u32[]{:S(2)}) collective-permute-start(f32[2,128,1]{2,1,0:T(8,128)S(1)} %fusion.106), channel_id=1, source_target_pairs={{0,1},{1,2},{2,3},{3,4},{4,5},{5,6},{6,7},{7,8},{8,9},{9,10},{10,1... | collective-permute-start | bytes 3080 | tf_op jit(solution)/shard_map/ppermute | solution.py:22
  428.7 76.3 %collective-permute-start.26 = (f32[2,128,1]{2,1,0:T(8,128)S(1)}, f32[2,128,1]{2,1,0:T(8,128)S(1)}, u32[]{:S(2)}, u32[]{:S(2)}) collective-permute-start(f32[2,128,1]{2,1,0:T(8,128)S(1)} %fusion.109), channel_id=1, source_target_pairs={{0,1},{1,2},{2,3},{3,4},{4,5},{5,6},{6,7},{7,8},{8,9},{9,10},{10,1... | collective-permute-start | bytes 3080 | tf_op jit(solution)/shard_map/ppermute | solution.py:22
  500.2 22.0 %collective-permute-start.37 = (f32[2,1,256]{2,1,0:T(1,128)S(1)}, f32[2,1,256]{2,1,0:T(1,128)S(1)}, u32[]{:S(2)}, u32[]{:S(2)}) collective-permute-start(f32[2,1,256]{2,1,0:T(1,128)S(1)} %get-tuple-element.494), channel_id=1, source_target_pairs={{16,0},{32,16},{48,32},{64,48},{80,64},{96,80},{112,96},{0,112},{1... | collective-permute-start | bytes 6152 | tf_op jit(solution)/shard_map/ppermute | solution.py:25
  501.7 21.6 %collective-permute-start.25 = (f32[2,1,256]{2,1,0:T(1,128)S(1)}, f32[2,1,256]{2,1,0:T(1,128)S(1)}, u32[]{:S(2)}, u32[]{:S(2)}) collective-permute-start(f32[2,1,256]{2,1,0:T(1,128)S(1)} %get-tuple-element.490), channel_id=1, source_target_pairs={{16,0},{32,16},{48,32},{64,48},{80,64},{96,80},{112,96},{0,112},{1... | collective-permute-start | bytes 6152 | tf_op jit(solution)/shard_map/ppermute | solution.py:25
  525.3 77.4 %collective-permute-start.46 = (f32[2,128,1]{2,1,0:T(8,128)S(1)}, f32[2,128,1]{2,1,0:T(8,128)S(1)}, u32[]{:S(2)}, u32[]{:S(2)}) collective-permute-start(f32[2,128,1]{2,1,0:T(8,128)S(1)} %fusion.104), channel_id=1, source_target_pairs={{0,1},{1,2},{2,3},{3,4},{4,5},{5,6},{6,7},{7,8},{8,9},{9,10},{10,1... | collective-permute-start | bytes 3080 | tf_op jit(solution)/shard_map/ppermute | solution.py:22
  527.3 75.4 %collective-permute-start.34 = (f32[2,128,1]{2,1,0:T(8,128)S(1)}, f32[2,128,1]{2,1,0:T(8,128)S(1)}, u32[]{:S(2)}, u32[]{:S(2)}) collective-permute-start(f32[2,128,1]{2,1,0:T(8,128)S(1)} %fusion.107), channel_id=1, source_target_pairs={{0,1},{1,2},{2,3},{3,4},{4,5},{5,6},{6,7},{7,8},{8,9},{9,10},{10,1... | collective-permute-start | bytes 3080 | tf_op jit(solution)/shard_map/ppermute | solution.py:22
  597.9 22.2 %collective-permute-start.45 = (f32[2,1,256]{2,1,0:T(1,128)S(1)}, f32[2,1,256]{2,1,0:T(1,128)S(1)}, u32[]{:S(2)}, u32[]{:S(2)}) collective-permute-start(f32[2,1,256]{2,1,0:T(1,128)S(1)} %get-tuple-element.486), channel_id=1, source_target_pairs={{16,0},{32,16},{48,32},{64,48},{80,64},{96,80},{112,96},{0,112},{1... | collective-permute-start | bytes 6152 | tf_op jit(solution)/shard_map/ppermute | solution.py:25
  599.4 21.8 %collective-permute-start.33 = (f32[2,1,256]{2,1,0:T(1,128)S(1)}, f32[2,1,256]{2,1,0:T(1,128)S(1)}, u32[]{:S(2)}, u32[]{:S(2)}) collective-permute-start(f32[2,1,256]{2,1,0:T(1,128)S(1)} %get-tuple-element.482), channel_id=1, source_target_pairs={{16,0},{32,16},{48,32},{64,48},{80,64},{96,80},{112,96},{0,112},{1... | collective-permute-start | bytes 6152 | tf_op jit(solution)/shard_map/ppermute | solution.py:25
  623.2 78.1 %collective-permute-start.54 = (f32[2,128,1]{2,1,0:T(8,128)S(1)}, f32[2,128,1]{2,1,0:T(8,128)S(1)}, u32[]{:S(2)}, u32[]{:S(2)}) collective-permute-start(f32[2,128,1]{2,1,0:T(8,128)S(1)} %fusion.102), channel_id=1, source_target_pairs={{0,1},{1,2},{2,3},{3,4},{4,5},{5,6},{6,7},{7,8},{8,9},{9,10},{10,1... | collective-permute-start | bytes 3080 | tf_op jit(solution)/shard_map/ppermute | solution.py:22
  625.3 76.1 %collective-permute-start.42 = (f32[2,128,1]{2,1,0:T(8,128)S(1)}, f32[2,128,1]{2,1,0:T(8,128)S(1)}, u32[]{:S(2)}, u32[]{:S(2)}) collective-permute-start(f32[2,128,1]{2,1,0:T(8,128)S(1)} %fusion.105), channel_id=1, source_target_pairs={{0,1},{1,2},{2,3},{3,4},{4,5},{5,6},{6,7},{7,8},{8,9},{9,10},{10,1... | collective-permute-start | bytes 3080 | tf_op jit(solution)/shard_map/ppermute | solution.py:22
  696.6 22.0 %collective-permute-start.53 = (f32[2,1,256]{2,1,0:T(1,128)S(1)}, f32[2,1,256]{2,1,0:T(1,128)S(1)}, u32[]{:S(2)}, u32[]{:S(2)}) collective-permute-start(f32[2,1,256]{2,1,0:T(1,128)S(1)} %get-tuple-element.478), channel_id=1, source_target_pairs={{16,0},{32,16},{48,32},{64,48},{80,64},{96,80},{112,96},{0,112},{1... | collective-permute-start | bytes 6152 | tf_op jit(solution)/shard_map/ppermute | solution.py:25
  721.7 77.4 %collective-permute-start.62 = (f32[2,128,1]{2,1,0:T(8,128)S(1)}, f32[2,128,1]{2,1,0:T(8,128)S(1)}, u32[]{:S(2)}, u32[]{:S(2)}) collective-permute-start(f32[2,128,1]{2,1,0:T(8,128)S(1)} %fusion.100), channel_id=1, source_target_pairs={{0,1},{1,2},{2,3},{3,4},{4,5},{5,6},{6,7},{7,8},{8,9},{9,10},{10,1... | collective-permute-start | bytes 3080 | tf_op jit(solution)/shard_map/ppermute | solution.py:22
  723.7 75.4 %collective-permute-start.50 = (f32[2,128,1]{2,1,0:T(8,128)S(1)}, f32[2,128,1]{2,1,0:T(8,128)S(1)}, u32[]{:S(2)}, u32[]{:S(2)}) collective-permute-start(f32[2,128,1]{2,1,0:T(8,128)S(1)} %fusion.103), channel_id=1, source_target_pairs={{0,1},{1,2},{2,3},{3,4},{4,5},{5,6},{6,7},{7,8},{8,9},{9,10},{10,1... | collective-permute-start | bytes 3080 | tf_op jit(solution)/shard_map/ppermute | solution.py:22
  794.3 22.2 %collective-permute-start.61 = (f32[2,1,256]{2,1,0:T(1,128)S(1)}, f32[2,1,256]{2,1,0:T(1,128)S(1)}, u32[]{:S(2)}, u32[]{:S(2)}) collective-permute-start(f32[2,1,256]{2,1,0:T(1,128)S(1)} %get-tuple-element.470), channel_id=1, source_target_pairs={{16,0},{32,16},{48,32},{64,48},{80,64},{96,80},{112,96},{0,112},{1... | collective-permute-start | bytes 6152 | tf_op jit(solution)/shard_map/ppermute | solution.py:25
  795.8 21.8 %collective-permute-start.49 = (f32[2,1,256]{2,1,0:T(1,128)S(1)}, f32[2,1,256]{2,1,0:T(1,128)S(1)}, u32[]{:S(2)}, u32[]{:S(2)}) collective-permute-start(f32[2,1,256]{2,1,0:T(1,128)S(1)} %get-tuple-element.466), channel_id=1, source_target_pairs={{16,0},{32,16},{48,32},{64,48},{80,64},{96,80},{112,96},{0,112},{1... | collective-permute-start | bytes 6152 | tf_op jit(solution)/shard_map/ppermute | solution.py:25
  (41 other events, 540.2 us)
where the time goes:
time: 847 us; the launch traced here: 836 us
  blocking collectives  516 us (61%)
  starting transfers between devices  160 us (19%)
  waiting for transfers between devices  77.6 us (9%)
  local copies, waits for them, and re-layouts  51.9 us (6%)
  other arithmetic  26.6 us (3%)
    unnamed x8, blocking collectives  516 us
    ppermute x32, starting transfers between devices, padded(): lax.ppermute(lax.slice_in_dim(block, 0, width, axis=dim), axis, backward)  81.2 us
    ppermute x32, waiting for transfers between devices, padded(): lax.ppermute(lax.slice_in_dim(block, 0, width, axis=dim), axis, backward)  77.5 us
    ppermute x32, starting transfers between devices, padded(): lax.ppermute(lax.slice_in_dim(block, block.shape[dim] - width, None, axis...  65.6 us
    scatter x1, local copies, waits for them, and re-layouts, local(): outgoing = jnp.zeros((devices * SLOT, 2, width), jnp.float32).at[position...  18.7 us
  transfers between devices with their start and end apart: 66, of which 15 were waited for; matrix products, arithmetic and copies ran while one was open for 6% of the time, Pallas kernels for 0%

commit v1 on v0

v1 whole, which is shorter than its diff:
```python
import functools

import jax
import jax.numpy as jnp
import numpy as np
from jax import lax
from jax.experimental import pallas as pl
from jax.experimental.pallas import tpu as pltpu
from jax.sharding import PartitionSpec as P

AXES = ("circ", "axial")
HALO = 8
LANES = 128
WIDE = 384
TOP = 16
EXT = 160
NEAR_LANES = (0, 1, -1, 16, -16, 15, -15, 17, -17)
ROW_KEY = 8192
KEY_MASK = 1024 * ROW_KEY - 1
HIGH = lax.Precision.HIGHEST
VMEM = pl.BlockSpec(memory_space=pltpu.VMEM)
SMEM = pl.BlockSpec(memory_space=pltpu.SMEM)


def diamond(radius):
    if radius < 0:
        return []
    span = range(-radius, radius + 1)
    return [(a, b) for a in span for b in span if abs(a) + abs(b) <= radius]


def patch_plan(radius):
    radii = (radius, radius - 1, radius - 1, radius - 1, radius - 2, radius - 2, radius - 3)
    return [(field, cell) for field, r in enumerate(radii) for cell in diamond(r)]


def patch_tables(radius):
    plan = patch_plan(radius)
    side = 2 * radius + 1
    deep = -(-side // 8) * 8
    width = -(-len(plan) * 8 // LANES) * LANES
    table = np.full((8, width), -1, np.int32)
    for index, (field, (a, b)) in enumerate(plan):
        for slot in range(8):
            at = index * 8 + slot
            table[0, at] = field * side + b + radius
            table[1, at] = slot * deep + a + radius
    return table


def iota(shape, dim):
    return lax.broadcasted_iota(jnp.int32, shape, dim)


def call(kernel, outs, ins, name, scratch=()):
    return pl.pallas_call(
        kernel,
        out_shape=tuple(jax.ShapeDtypeStruct(s, jnp.float32) for s in outs),
        in_specs=ins,
        out_specs=tuple(VMEM for _ in outs),
        scratch_shapes=list(scratch),
        name=name,
    )


def side_strips(tiles):
    rows = tiles[0][0].shape[0]
    lane = iota((rows, LANES), 1)
    left = jnp.zeros((rows, LANES), jnp.float32)
    right = left
    for f, (first, last) in enumerate(tiles):
        mine = (lane >= f * HALO) & (lane < (f + 1) * HALO)
        left = jnp.where(mine, pltpu.roll(first, f * HALO, 1) if f else first, left)
        right = jnp.where(mine, pltpu.roll(last, f * HALO + HALO, 1), right)
    return left, right


def side_tile(from_east, from_west, f):
    lane = iota(from_east.shape, 1)
    east = pltpu.roll(from_east, (LANES - f * HALO) % LANES, 1) if f else from_east
    west = pltpu.roll(from_west, LANES - HALO - f * HALO, 1)
    return jnp.where(lane < HALO, east, jnp.where(lane >= LANES - HALO, west, 0.0))


def strips_kernel(ca, vo, co, to_west, to_east):
    fields = [ca.at[0], ca.at[1], vo.at[0], vo.at[1], co]
    left, right = side_strips([(f[:, :LANES], f[:, LANES:]) for f in fields])
    to_west[...] = left
    to_east[...] = right


def ends_kernel(ca, vo, co, from_east, from_west, to_north, to_south):
    fields = [ca.at[0], ca.at[1], vo.at[0], vo.at[1], co]
    for f, ref in enumerate(fields):
        for rows, out in ((slice(0, HALO), to_north), (slice(128 - HALO, 128), to_south)):
            out[f, :, : 2 * LANES] = ref[rows, :]
            out[f, :, 2 * LANES :] = side_tile(from_east[rows, :], from_west[rows, :], f)


def ends2_kernel(force, from_east, from_west, to_north, to_south):
    for f in range(2):
        for rows, out in ((slice(0, HALO), to_north), (slice(128 - HALO, 128), to_south)):
            out[f, :, : 2 * LANES] = force[f, rows, :]
            out[f, :, 2 * LANES :] = side_tile(from_east[rows, :], from_west[rows, :], f)


def pack_kernel(count, target, row, info, fluid, out):
    slots = fluid.shape[0]
    t_row = target[...]
    order = iota((1, slots), 1)
    used = order < count[0]
    eye = iota((slots, slots), 0) == iota((slots, slots), 1)
    t_col = jnp.sum(jnp.where(eye, t_row, 0), axis=1, keepdims=True)
    earlier = (
        (t_col == t_row)
        & (iota((slots, slots), 0) < count[0])
        & (iota((slots, slots), 0) < iota((slots, slots), 1))
    )
    rank = jnp.sum(jnp.where(earlier, 1, 0), axis=0, keepdims=True)
    place = jnp.where(used, rank * 128 + t_row, -1)
    pick = iota((256, slots), 0) == place
    tags = jnp.sum(jnp.where(pick, row[...] + 1, 0), axis=1, keepdims=True).astype(jnp.float32)
    moved = jnp.dot(
        pick.astype(jnp.float32), fluid[...], precision=HIGH, preferred_element_type=jnp.float32
    )
    out[:, :512] = moved[:128]
    out[:, 512:1024] = moved[128:]
    lane = iota((128, LANES), 1)
    tail = jnp.where(lane == 0, tags[:128], jnp.where(lane == 1, tags[128:], info[...]))
    out[:, 1024:] = tail


def force_kernel(got, force, to_west, to_east):
    tail = got[:, 1024:]
    line = iota((128, 128), 1).astype(jnp.float32) + 1.0
    dims = (((0,), (0,)), ((), ()))
    total = lax.dot_general(
        (tail[:, 0:1] == line).astype(jnp.float32),
        got[:, :512],
        dims,
        precision=HIGH,
        preferred_element_type=jnp.float32,
    ) + lax.dot_general(
        (tail[:, 1:2] == line).astype(jnp.float32),
        got[:, 512:1024],
        dims,
        precision=HIGH,
        preferred_element_type=jnp.float32,
    )
    shear = total[:, :256]
    agonist = total[:, 256:]
    stress = shear * shear / (1.0 + shear * shear)
    stimulus = 0.5 + 0.5 * jnp.tanh(0.5 * agonist)
    a_s = 0.1 * stimulus
    a_e = 0.02 + 0.15 * stress + 0.04 * stimulus
    force[0] = a_s
    force[1] = a_e
    left, right = side_strips([(a[:, :LANES], a[:, LANES:]) for a in (a_s, a_e)])
    to_west[...] = left
    to_east[...] = right


def extract(radius, refs, cells, table, tmp, out):
    side = 2 * radius + 1
    deep = -(-side // 8) * 8
    lane = iota((deep, LANES), 1)
    for slot in range(8):
        cell = cells[slot]
        row = cell // 256 + TOP - radius
        col = cell % 256 - radius
        base = pl.multiple_of(row // 8 * 8, 8)
        up = row - base
        kept = jnp.zeros((deep, LANES), jnp.float32)
        for f, ref in enumerate(refs):
            window = ref[pl.ds(base, deep + 8), :]
            window = pltpu.roll(window, (deep + 8 - up) % (deep + 8), 0)[:deep]
            window = pltpu.roll(window, (2 * WIDE - col + f * side) % WIDE, 1)[:, :LANES]
            kept = jnp.where((lane >= f * side) & (lane < (f + 1) * side), window, kept)
        tmp[slot * deep : (slot + 1) * deep, :] = kept
    pieces = tmp[: 8 * deep, :]
    width = table.shape[1]
    pick = (iota((LANES, width), 0) == table[0:1, :]).astype(jnp.float32)
    spread_out = jnp.dot(pieces, pick, precision=HIGH, preferred_element_type=jnp.float32)
    mine = iota((8 * deep, width), 0) == table[1:2, :]
    line = jnp.sum(jnp.where(mine, spread_out, 0.0), axis=0, keepdims=True)
    out[...] = jnp.broadcast_to(line, (128, width))


def build_ext(dst, centre, side, north, south):
    dst[TOP : TOP + 128, : 2 * LANES] = centre
    dst[TOP : TOP + 128, 2 * LANES :] = side
    dst[TOP - HALO : TOP, :] = north
    dst[TOP + 128 : TOP + 128 + HALO, :] = south
    clear_ends(dst)


def clear_ends(dst):
    dst[: TOP - HALO, :] = jnp.zeros((TOP - HALO, WIDE), jnp.float32)
    dst[TOP + 128 + HALO :, :] = jnp.zeros((EXT - TOP - 128 - HALO, WIDE), jnp.float32)


def first_patch_kernel(
    cells, ca, vo, co, from_east, from_west, from_north, from_south, force, table, ext, out, tmp
):
    fields = [ca.at[0], ca.at[1], vo.at[0], vo.at[1], co]
    for f, ref in enumerate(fields):
        scale = 0.05 if f == 4 else 1.0
        build_ext(
            ext.at[f],
            ref[...] * scale,
            side_tile(from_east[...], from_west[...], f) * scale,
            from_north[f] * scale,
            from_south[f] * scale,
        )
    tmp_force = ext.at[5]
    tmp_force[...] = jnp.zeros((EXT, WIDE), jnp.float32)
    tmp_force[TOP : TOP + 128, : 2 * LANES] = force[0]
    refs = [ext.at[2], ext.at[0], ext.at[3], ext.at[4], ext.at[1], ext.at[5]]
    extract(2, refs, cells, table, tmp, out)


def port_places(tail_t):
    rows = tail_t[8:16].astype(jnp.int32)
    cols = tail_t[16:24].astype(jnp.int32)
    partner = tail_t[24:32].astype(jnp.int32)
    return rows, cols, partner


def port_sim(radius, got, codes, rows, cols, partner):
    plan = patch_plan(radius)
    fields = [{} for _ in range(7)]
    for index, (field, cell) in enumerate(plan):
        fields[field][cell] = got[index * 8 : index * 8 + 8]
    v, s, u, spread, e, a_s, a_e = fields
    device = partner // 8
    slot = partner % 8

    def near(f, cell):
        a, b = cell
        left = jnp.where(cols == -b, f[cell], f[(a, b - 1)])
        right = jnp.where(cols == 4095 - b, f[cell], f[(a, b + 1)])
        return f[(a - 1, b)] + f[(a + 1, b)] + left + right

    gains = []
    for step in range(radius + 1):
        here = v[(0, 0)]
        theirs = jnp.zeros_like(here)
        for k in range(8):
            line = jnp.broadcast_to(here[k : k + 1], here.shape)
            theirs = jnp.where(slot == k, jnp.take_along_axis(line, device, axis=1), theirs)
        gain = 0.2 * (theirs - here)
        gains.append(gain)
        reach = radius - 1 - step
        if reach < 0:
            break
        cells = diamond(reach)
        added = {c: jnp.zeros_like(gain) for c in cells}
        index = 0
        for k in range(8):
            turned = pltpu.roll(gain, k, 0) if k else gain
            for shift in NEAR_LANES:
                moved = pltpu.roll(turned, (-shift) % LANES, 1) if shift else turned
                code = codes[index]
                index += 1
                for c in cells:
                    key = (c[0] * ROW_KEY + c[1]) & KEY_MASK
                    added[c] = added[c] + jnp.where(code == key, moved, 0.0)
        new_v = {}
        for c in cells:
            new_v[c] = v_step(s[c], v[c], u[c], near(v, c), spread[c]) + added[c]
        new_s, new_u, new_e = {}, {}, {}
        for c in diamond(reach - 1):
            new_s[c] = s_step(s[c], e[c], v[c], near(s, c), spread[c], a_s[c])
            new_u[c] = u_step(e[c], v[c], u[c], near(u, c), spread[c])
        for c in diamond(reach - 2):
            new_e[c] = e_step(s[c], e[c], near(e, c), spread[c], a_e[c])
        v, s, u, e = new_v, new_s, new_u, new_e
    return gains


def s_step(s, e, v, near, spread, a_s):
    return (
        s
        + (0.04 * jnp.tanh(v + 0.3) + 0.04)
        + a_s
        - 0.12 * s / (s + 0.5)
        + 0.03 * (e - s)
        + spread * (near - 4.0 * s)
    )


def e_step(s, e, near, spread, a_e):
    return e + a_e - 0.09 * e + 0.03 * (s - e) + spread * (near - 4.0 * e)


def v_step(s, v, u, near, spread):
    return (
        v
        - 0.1 * (v + 0.5)
        - 0.15 * s / (s + 1.0) * (v + 1.2)
        + 0.04 * (u - v)
        + spread * (near - 4.0 * v)
    )


def u_step(e, v, u, near, spread):
    return (
        u
        - 0.08 * (u + 0.4)
        - 0.1 * e / (e + 1.0) * (u + 1.2)
        + 0.04 * (v - u)
        + spread * (near - 4.0 * u)
    )


def make_codes(rows, cols, codes):
    key = rows * ROW_KEY + cols
    index = 0
    for k in range(8):
        turned = pltpu.roll(key, k, 0) if k else key
        for shift in NEAR_LANES:
            moved = pltpu.roll(turned, (-shift) % LANES, 1) if shift else turned
            codes[index] = (moved - key) & KEY_MASK
            index += 1


def my_column(value, lane_of):
    tiles = []
    lane = iota((8, LANES), 1)
    for shift in NEAR_LANES:
        at = (lane_of + shift) & (LANES - 1)
        tiles.append(jnp.sum(jnp.where(lane == at, value, 0.0), axis=1, keepdims=True))
    tiles.append(jnp.zeros((128 - 8 * len(tiles), 1), jnp.float32))
    return jnp.concatenate(tiles, axis=0)


def injections(place, rows, cols, gains, inject):
    i_circ = place[0]
    i_axial = place[1]
    lane_of = i_circ * 16 + i_axial
    row = my_column(rows.astype(jnp.float32), lane_of).astype(jnp.int32)
    col = my_column(cols.astype(jnp.float32), lane_of).astype(jnp.int32)
    row = ((row - i_circ * 128 + HALO) & 1023) + (TOP - HALO)
    col = col - i_axial * 256
    ok = (iota((128, 1), 0) < 72) & (col >= -HALO) & (col < 256 + HALO)
    col = jnp.where(ok, jnp.where(col < 0, col + WIDE, col), -1)
    in_row = jnp.where(row == iota((128, 256), 1), 1.0, 0.0)
    in_row = jnp.transpose(in_row)[:EXT]
    in_col = col == iota((128, WIDE), 1)
    for k, gain in enumerate(gains):
        line = jnp.where(in_col, my_column(gain, lane_of), 0.0)
        inject[k] = jnp.dot(in_row, line, precision=HIGH, preferred_element_type=jnp.float32)


def run_steps(steps, state, coef, inject, place):
    lane = iota((8, WIDE), 1)
    first = (lane == 0) & (place[1] == 0)
    last = (lane == 255) & (place[1] == 15)

    for f in range(4):
        clear_ends(state.at[1, f])

    def one(k, carry):
        now = lax.rem(k, 2)
        later = 1 - now
        for tile in range(1, EXT // 8 - 1):
            at = slice(tile * 8, tile * 8 + 8)
            mid, near = [], []
            for f in range(4):
                x = state[now, f, at, :]
                up = state[now, f, tile * 8 - 1 : tile * 8 + 7, :]
                down = state[now, f, tile * 8 + 1 : tile * 8 + 9, :]
                left = jnp.where(first, x, pltpu.roll(x, 1, 1))
                right = jnp.where(last, x, pltpu.roll(x, WIDE - 1, 1))
                mid.append(x)
                near.append(up + down + left + right)
            s, e, v, u = mid
            spread = coef[0][at, :]
            state[later, 0, at, :] = s_step(s, e, v, near[0], spread, coef[1][at, :])
            state[later, 1, at, :] = e_step(s, e, near[1], spread, coef[2][at, :])
            state[later, 2, at, :] = v_step(s, v, u, near[2], spread) + inject[k, at, :]
            state[later, 3, at, :] = u_step(e, v, u, near[3], spread)
        return carry

    lax.fori_loop(0, steps, one, 0)


def first_steps_kernel(
    place, cells, ext, force, from_east, from_west, from_north, from_south, got, tail, table,
    kept, out, state, codes, inject, tmp
):
    rows, cols, partner = port_places(jnp.transpose(tail[...]))
    make_codes(rows, cols, codes)
    gains = port_sim(2, jnp.transpose(got[...]), codes, rows, cols, partner)
    injections(place, rows, cols, gains, inject)
    for f in range(4):
        state[0, f] = ext[f]
    kept[4] = ext[4]
    for f in range(2):
        build_ext(
            kept.at[5 + f],
            force[f],
            side_tile(from_east[...], from_west[...], f),
            from_north[f],
            from_south[f],
        )
    run_steps(3, state, (kept.at[4], kept.at[5], kept.at[6]), inject, place)
    for f in range(4):
        kept[f] = state[1, f]
    refs = [kept.at[f] for f in (2, 0, 3, 4, 1, 5, 6)]
    extract(4, refs, cells, table, tmp, out)


def last_steps_kernel(place, kept, got, tail, ca_out, vo_out, state, codes, inject):
    rows, cols, partner = port_places(jnp.transpose(tail[...]))
    make_codes(rows, cols, codes)
    gains = port_sim(4, jnp.transpose(got[...]), codes, rows, cols, partner)
    injections(place, rows, cols, gains, inject)
    for f in range(4):
        state[0, f] = kept[f]
    run_steps(5, state, (kept.at[4], kept.at[5], kept.at[6]), inject, place)
    for f in range(2):
        ca_out[f] = state[1, f, TOP : TOP + 128, : 2 * LANES]
        vo_out[f] = state[1, f + 2, TOP : TOP + 128, : 2 * LANES]


def shifted(value, axis, step, periodic):
    count = lax.axis_size(axis)
    pairs = [(i, i + step) for i in range(count)]
    if periodic:
        pairs = [(i, j % count) for i, j in pairs]
    return lax.ppermute(value, axis, [(i, j) for i, j in pairs if 0 <= j < count])


def swap_axial(to_west, to_east):
    return shifted(to_west, "axial", -1, False), shifted(to_east, "axial", 1, False)


def swap_circ(to_north, to_south):
    return shifted(to_south, "circ", 1, True), shifted(to_north, "circ", -1, True)


def to_all(value):
    return lax.all_to_all(value, AXES, 0, 0, tiled=True)


def local(ca, vo, co, fluid, target, row, count, cells, partner):
    i_circ = lax.axis_index("circ")
    i_axial = lax.axis_index("axial")
    place = jnp.stack([i_circ, i_axial]).astype(jnp.int32)
    tables = [jnp.asarray(patch_tables(r)) for r in (2, 4)]
    widths = [t.shape[1] for t in tables]

    to_west, to_east = call(strips_kernel, [(128, LANES)] * 2, [VMEM] * 3, "strips")(ca, vo, co)
    from_east, from_west = swap_axial(to_west, to_east)

    info = jnp.concatenate(
        [
            jnp.zeros((8,), jnp.float32),
            (i_circ * 128 + cells // 256).astype(jnp.float32),
            (i_axial * 256 + cells % 256).astype(jnp.float32),
            partner.astype(jnp.float32),
            jnp.zeros((LANES - 32,), jnp.float32),
        ]
    )[None]
    (packed,) = call(pack_kernel, [(128, 1152)], [SMEM] + [VMEM] * 4, "pack")(
        count, target.reshape(1, -1), row.reshape(1, -1), info, fluid.reshape(192, 512)
    )
    to_north, to_south = call(ends_kernel, [(5, HALO, WIDE)] * 2, [VMEM] * 5, "ends")(
        ca, vo, co, from_east, from_west
    )
    from_north, from_south = swap_circ(to_north, to_south)
    received = to_all(packed)
    tail = received[:, 1024:]

    force, f_west, f_east = call(
        force_kernel, [(2, 128, 256), (128, LANES), (128, LANES)], [VMEM], "force"
    )(received)
    f_from_east, f_from_west = swap_axial(f_west, f_east)
    ext, patches = call(
        first_patch_kernel,
        [(6, EXT, WIDE), (128, widths[0])],
        [SMEM] + [VMEM] * 9,
        "first_patch",
        [pltpu.VMEM((128, LANES), jnp.float32)],
    )(cells, ca, vo, co, from_east, from_west, from_north, from_south, force, tables[0])
    f_north, f_south = call(ends2_kernel, [(2, HALO, WIDE)] * 2, [VMEM] * 3, "ends2")(
        force, f_from_east, f_from_west
    )
    f_from_north, f_from_south = swap_circ(f_north, f_south)
    got = to_all(patches)

    state = pltpu.VMEM((2, 4, EXT, WIDE), jnp.float32)
    codes = pltpu.VMEM((72, 8, LANES), jnp.int32)
    kept, patches = call(
        first_steps_kernel,
        [(7, EXT, WIDE), (128, widths[1])],
        [SMEM] * 2 + [VMEM] * 9,
        "first_steps",
        [state, codes, pltpu.VMEM((3, EXT, WIDE), jnp.float32), pltpu.VMEM((128, LANES), jnp.float32)],
    )(
        place, cells, ext, force, f_from_east, f_from_west, f_from_north, f_from_south, got, tail,
        tables[1],
    )
    got = to_all(patches)
    return call(
        last_steps_kernel,
        [(2, 128, 256)] * 2,
        [SMEM] + [VMEM] * 3,
        "last_steps",
        [state, codes, pltpu.VMEM((5, EXT, WIDE), jnp.float32)],
    )(place, kept, got, tail)


def solution(mesh):
    return jax.shard_map(
        local,
        mesh=mesh,
        in_specs=(
            P(None, "circ", "axial"),
            P(None, "circ", "axial"),
            P("circ", "axial"),
            P(AXES, None, None),
            P(AXES, None),
            P(AXES),
            P(AXES),
            P(AXES),
            P(AXES),
        ),
        out_specs=(P(None, "circ", "axial"), P(None, "circ", "axial")),
        check_vma=False,
    )
```

time: 847 us -> 123 us (0.15); the launches traced: 836 us -> 123 us
  blocking collectives: 516 us -> 23.9 us
  starting transfers between devices: 160 us -> 41.8 us
  waiting for transfers between devices: 77.6 us -> 3.49 us
  local copies, waits for them, and re-layouts: 51.9 us -> 15.9 us
  Pallas kernels: 0 us -> 34 us
  other arithmetic: 26.6 us -> 1.97 us
    unnamed x8 -> x0, blocking collectives: 516 us -> none
    ppermute x64 -> x8, starting transfers between devices: 147 us -> 22.1 us  [shifted(): lax.ppermute(value, axis, [(i, j) for i, j in pairs if 0 <= j < count])]
    ppermute x64 -> x8, waiting for transfers between devices: 77.6 us -> 2.27 us  [shifted(): lax.ppermute(value, axis, [(i, j) for i, j in pairs if 0 <= j < count])]
    pallas_call x0 -> x8, Pallas kernels: none -> 34 us  [the longest x1 11.5 us: local(): call(last_steps_kernel, [(2, 128, 256)] * 2, [SMEM] + [VMEM] * 3, 'last_s...]
    scatter x34 -> x0, local copies, waits for them, and re-layouts: 33.3 us -> none  [the longest x1 18.7 us: local(): outgoing = jnp.zeros((devices * SLOT, 2, width), jnp.float32).at[position...]
    all_to_all x0 -> x1, blocking collectives: none -> 23.9 us  [to_all(): return lax.all_to_all(value, AXES, 0, 0, tiled=True)]
    scatter-add x9 -> x0, other arithmetic: 15 us -> none  [the longest x1 9.28 us: local(): jnp.zeros((row_count, 2, width), jnp.float32).at[recv_rows]]
    gather x16 -> x0, local copies, waits for them, and re-layouts: 10.1 us -> none  [the longest x8 5.09 us: local(): port_values = flat_volt[port_cells]]
  transfers between devices with their start and end apart: 66 -> 10, of which waited for: 15 -> 2; matrix products, arithmetic and copies ran while one was open for 6% -> 4% of each run, Pallas kernels for 0% -> 9%
where the time goes in v1:
time: 123 us
  starting transfers between devices  41.8 us (34%)
  Pallas kernels  34 us (28%)
  blocking collectives  23.9 us (19%)
  local copies, waits for them, and re-layouts  15.9 us (13%)
  waiting for transfers between devices  3.49 us (3%)
  other arithmetic  1.97 us (2%)
  between operations  1.43 us (1%)
    all_to_all x1, blocking collectives, to_all(): return lax.all_to_all(value, AXES, 0, 0, tiled=True)  23.9 us
    ppermute x8, starting transfers between devices, shifted(): lax.ppermute(value, axis, [(i, j) for i, j in pairs if 0 <= j < count])  22.1 us
    all_to_all x2, starting transfers between devices, to_all(): return lax.all_to_all(value, AXES, 0, 0, tiled=True)  19.8 us
    pallas_call x1, Pallas kernels, local(): call(last_steps_kernel, [(2, 128, 256)] * 2, [SMEM] + [VMEM] * 3, 'last_s...  11.5 us
    pallas_call x1, Pallas kernels, local(): call(first_steps_kernel, [(7, EXT, WIDE), (128, widths[1])], [SMEM] * 2 +...  8.97 us
    unnamed x20, local copies, waits for them, and re-layouts  7.88 us
    all_to_all x3, local copies, waits for them, and re-layouts, to_all(): return lax.all_to_all(value, AXES, 0, 0, tiled=True)  5.97 us
    pallas_call x1, Pallas kernels, local(): call(first_patch_kernel, [(6, EXT, WIDE), (128, widths[0])], [SMEM] + [VM...  2.92 us
  transfers between devices with their start and end apart: 10, of which 2 were waited for; matrix products, arithmetic and copies ran while one was open for 4% of the time, Pallas kernels for 9%

profile of v1, /device:TPU:1, one launch (start us, length us, event | category | flops | bytes accessed | tf_op | source)
XLA Modules:
  0.0 122.6 jit_solution(12112344961116631710)
XLA Ops:
  1.3 0.7 convert_element_type.11
  1.9 1.8 %copy.19 = f32[24,8,2,256]{3,1,2,0:T(8,128)} copy(f32[24,8,2,256]{3,2,1,0:T(2,128)} %bitcast.26) | data formatting | bytes 786432
  3.7 0.7 fusion.1
  5.0 2.6 %pack.1 = f32[128,1152]{1,0:T(8,128)} custom-call(s32[1]{0:T(128)S(6)} %copy.26.count, s32[1,192]{1,0:T(1,128)} %bitcast.29, s32[1,192]{1,0:T(1,128)} %bitcast.30, f32[1,128]{1,0:T(1,128)} %bitcast.28, f32[192,512]{1,0:T(8,128)} %bitcast.23), custom_call_target="tpu_custom_call" | custom-call | tf_op jit(solution)/shard_map/pack/pallas_call | solution.py:466
  7.6 2.5 %copy.13 = f32[128,1,1152]{2,1,0:T(1,128)} copy(f32[128,1,1152]{2,0,1:T(8,128)} %bitcast.22) | data formatting | bytes 1179648 | tf_op jit(solution)/shard_map/all_to_all | solution.py:444
  10.1 11.5 %all-to-all-start = ((f32[128,1,1152]{2,1,0:T(1,128)}), f32[128,1,1152]{2,1,0:T(1,128)S(1)}, u32[]{:S(2)}, u32[]{:S(2)}) async-start(f32[128,1,1152]{2,1,0:T(1,128)} %copy.13), calls=%async_computation | async-start | bytes 1179648 | tf_op jit(solution)/shard_map/all_to_all | solution.py:444
  21.6 1.9 %strips.1 = (f32[128,128]{1,0:T(8,128)}, f32[128,128]{1,0:T(8,128)}) custom-call(f32[2,128,256]{2,1,0:T(8,128)} %ca.5, f32[2,128,256]{2,1,0:T(8,128)} %vo.5, f32[128,256]{1,0:T(8,128)} %co.5), custom_call_target="tpu_custom_call" | custom-call | tf_op jit(solution)/shard_map/strips/pallas_call | solution.py:454
  23.6 3.0 %collective-permute-start = (f32[128,128]{1,0:T(8,128)}, f32[128,128]{1,0:T(8,128)S(1)}, u32[]{:S(2)}, u32[]{:S(2)}) collective-permute-start(f32[128,128]{1,0:T(8,128)} %get-tuple-element.15), channel_id=1, source_target_pairs={{1,0},{2,1},{3,2},{4,3},{5,4},{6,5},{7,6},{8,7},{9,8},{10,9},{11,1... | collective-permute-start | bytes 196616 | tf_op jit(solution)/shard_map/ppermute | solution.py:432
  26.5 4.4 %collective-permute-start.1 = (f32[128,128]{1,0:T(8,128)}, f32[128,128]{1,0:T(8,128)S(1)}, u32[]{:S(2)}, u32[]{:S(2)}) collective-permute-start(f32[128,128]{1,0:T(8,128)} %get-tuple-element.16), channel_id=1, source_target_pairs={{0,1},{1,2},{2,3},{3,4},{4,5},{5,6},{6,7},{7,8},{8,9},{9,10},{10,1... | collective-permute-start | bytes 196616 | tf_op jit(solution)/shard_map/ppermute | solution.py:432
  30.9 2.3 %collective-permute-done.from_east = f32[128,128]{1,0:T(8,128)S(1)} collective-permute-done((f32[128,128]{1,0:T(8,128)}, f32[128,128]{1,0:T(8,128)S(1)}, u32[]{:S(2)}, u32[]{:S(2)}) %collective-permute-start) | collective-permute-done | bytes 65568 | tf_op jit(solution)/shard_map/ppermute | solution.py:432
  34.4 1.8 %ends.1 = (f32[5,8,384]{2,1,0:T(8,128)}, f32[5,8,384]{2,1,0:T(8,128)}) custom-call(f32[2,128,256]{2,1,0:T(8,128)} %ca.5, f32[2,128,256]{2,1,0:T(8,128)} %vo.5, f32[128,256]{1,0:T(8,128)} %co.5, f32[128,128]{1,0:T(8,128)} %copy-done, f32[128,128]{1,0:T(8,128)} %copy-done.1), custom_call_target="tpu_custom_call" | custom-call | tf_op jit(solution)/shard_map/ends/pallas_call | solution.py:469
  36.2 1.5 %collective-permute-start.2 = (f32[5,8,384]{2,1,0:T(8,128)}, f32[5,8,384]{2,1,0:T(8,128)S(1)}, u32[]{:S(2)}, u32[]{:S(2)}) collective-permute-start(f32[5,8,384]{2,1,0:T(8,128)} %get-tuple-element.17), channel_id=1, source_target_pairs={{0,16},{16,32},{32,48},{48,64},{64,80},{80,96},{96,112},{112,0},{1... | collective-permute-start | bytes 184328 | tf_op jit(solution)/shard_map/ppermute | solution.py:432
  37.8 2.1 %collective-permute-start.3 = (f32[5,8,384]{2,1,0:T(8,128)}, f32[5,8,384]{2,1,0:T(8,128)S(1)}, u32[]{:S(2)}, u32[]{:S(2)}) collective-permute-start(f32[5,8,384]{2,1,0:T(8,128)} %get-tuple-element.18), channel_id=1, source_target_pairs={{0,112},{16,0},{32,16},{48,32},{64,48},{80,64},{96,80},{112,96},{1... | collective-permute-start | bytes 184328 | tf_op jit(solution)/shard_map/ppermute | solution.py:432
  39.8 0.9 copy.24
  40.7 2.5 %force.1 = (f32[2,128,256]{2,1,0:T(8,128)}, f32[128,128]{1,0:T(8,128)}, f32[128,128]{1,0:T(8,128)}) custom-call(f32[128,1152]{1,0:T(8,128)} %bitcast.19), custom_call_target="tpu_custom_call" | custom-call | tf_op jit(solution)/shard_map/force/pallas_call | solution.py:476
  43.2 1.9 %collective-permute-start.4 = (f32[128,128]{1,0:T(8,128)}, f32[128,128]{1,0:T(8,128)S(1)}, u32[]{:S(2)}, u32[]{:S(2)}) collective-permute-start(f32[128,128]{1,0:T(8,128)} %get-tuple-element.21), channel_id=1, source_target_pairs={{1,0},{2,1},{3,2},{4,3},{5,4},{6,5},{7,6},{8,7},{9,8},{10,9},{11,1... | collective-permute-start | bytes 196616 | tf_op jit(solution)/shard_map/ppermute | solution.py:432
  45.1 5.6 %collective-permute-start.5 = (f32[128,128]{1,0:T(8,128)}, f32[128,128]{1,0:T(8,128)S(1)}, u32[]{:S(2)}, u32[]{:S(2)}) collective-permute-start(f32[128,128]{1,0:T(8,128)} %get-tuple-element.22), channel_id=1, source_target_pairs={{0,1},{1,2},{2,3},{3,4},{4,5},{5,6},{6,7},{7,8},{8,9},{9,10},{10,1... | collective-permute-start | bytes 196616 | tf_op jit(solution)/shard_map/ppermute | solution.py:432
  51.4 2.9 %first_patch.1 = (f32[6,160,384]{2,1,0:T(8,128)}, f32[128,256]{1,0:T(8,128)}) custom-call(s32[8]{0:T(128)} %cells.3, f32[2,128,256]{2,1,0:T(8,128)} %ca.5, f32[2,128,256]{2,1,0:T(8,128)} %vo.5, f32[128,256]{1,0:T(8,128)} %co.5, f32[128,128]{1,0:T(8,128)} %copy-done, f32[128,128]{1,0:T(8,128)} %copy-done.1, f32[5,8,384]{2,1,0:T(8,128)} %copy-done.4, ...), custom_call_target="tpu_custom_call" | custom-call | tf_op jit(solution)/shard_map/first_patch/pallas_call | solution.py:480
  54.3 1.7 %copy.14 = f32[128,1,256]{2,1,0:T(1,128)} copy(f32[128,1,256]{2,0,1:T(8,128)} %bitcast.27) | data formatting | bytes 262144 | tf_op jit(solution)/shard_map/all_to_all | solution.py:444
  56.0 8.3 %all-to-all-start.1 = ((f32[128,1,256]{2,1,0:T(1,128)}), f32[128,1,256]{2,1,0:T(1,128)S(1)}, u32[]{:S(2)}, u32[]{:S(2)}) async-start(f32[128,1,256]{2,1,0:T(1,128)} %copy.14), calls=%async_computation.1 | async-start | bytes 262144 | tf_op jit(solution)/shard_map/all_to_all | solution.py:444
  65.5 1.7 %ends2.1 = (f32[2,8,384]{2,1,0:T(8,128)}, f32[2,8,384]{2,1,0:T(8,128)}) custom-call(f32[2,128,256]{2,1,0:T(8,128)} %get-tuple-element.19.force, f32[128,128]{1,0:T(8,128)} %copy-done.2, f32[128,128]{1,0:T(8,128)} %copy-done.3), custom_call_target="tpu_custom_call" | custom-call | tf_op jit(solution)/shard_map/ends2/pallas_call | solution.py:487
  67.2 1.4 %collective-permute-start.6 = (f32[2,8,384]{2,1,0:T(8,128)}, f32[2,8,384]{2,1,0:T(8,128)S(1)}, u32[]{:S(2)}, u32[]{:S(2)}) collective-permute-start(f32[2,8,384]{2,1,0:T(8,128)} %get-tuple-element.23), channel_id=1, source_target_pairs={{0,16},{16,32},{32,48},{48,64},{64,80},{80,96},{96,112},{112,0},{1... | collective-permute-start | bytes 73736 | tf_op jit(solution)/shard_map/ppermute | solution.py:432
  68.6 2.3 %collective-permute-start.7 = (f32[2,8,384]{2,1,0:T(8,128)}, f32[2,8,384]{2,1,0:T(8,128)S(1)}, u32[]{:S(2)}, u32[]{:S(2)}) collective-permute-start(f32[2,8,384]{2,1,0:T(8,128)} %get-tuple-element.24), channel_id=1, source_target_pairs={{0,112},{16,0},{32,16},{48,32},{64,48},{80,64},{96,80},{112,96},{1... | collective-permute-start | bytes 73736 | tf_op jit(solution)/shard_map/ppermute | solution.py:432
  70.9 0.6 pad_add_fusion.place
  71.5 1.5 %slice.4.tail = f32[128,128]{1,0:T(8,128)} slice(f32[128,1152]{1,0:T(8,128)} %bitcast.20), slice={[0:128], [1024:1152]} | slice | bytes 131072 | tf_op jit(solution)/shard_map/slice | solution.py:474
  73.0 1.2 all-to-all-done.1
  74.2 0.7 copy.25
  75.5 9.0 %first_steps.1 = (f32[7,160,384]{2,1,0:T(8,128)}, f32[128,1280]{1,0:T(8,128)}) custom-call(s32[2]{0:T(128)} %pad_add_fusion.place, s32[8]{0:T(128)} %cells.3, f32[6,160,384]{2,1,0:T(8,128)} %get-tuple-element.20.ext, f32[2,128,256]{2,1,0:T(8,128)} %get-tuple-element.19.force, f32[128,128]{1,0:T(8,128)} %copy-done.2, f32[128,128]{1,0:T(8,128)} %copy-done.3, ...), custom_call_target="tpu_custom_call" | custom-call | tf_op jit(solution)/shard_map/first_steps/pallas_call | solution.py:495
  84.4 1.8 %copy.15 = f32[128,1,1280]{2,1,0:T(1,128)S(1)} copy(f32[128,1,1280]{2,0,1:T(8,128)} %bitcast.24) | data formatting | bytes 1310720 | tf_op jit(solution)/shard_map/all_to_all | solution.py:444
  86.2 23.9 %all_to_all.33 = f32[128,1,1280]{2,1,0:T(1,128)S(1)} all-to-all(f32[128,1,1280]{2,1,0:T(1,128)S(1)} %copy.15), channel_id=1, replica_groups=mesh['circ'=8,'axial'=16] {'circ','axial'}, dimensions={0} | all-to-all | bytes 1310720 | tf_op jit(solution)/shard_map/all_to_all | solution.py:444
  110.1 0.9 copy.23
  111.0 11.5 %last_steps.1 = (f32[2,128,256]{2,1,0:T(8,128)}, f32[2,128,256]{2,1,0:T(8,128)}) custom-call(s32[2]{0:T(128)} %pad_add_fusion.place, f32[7,160,384]{2,1,0:T(8,128)} %get-tuple-element.26.kept, f32[128,1280]{1,0:T(8,128)} %bitcast.21, f32[128,128]{1,0:T(8,128)} %slice.4.tail), custom_call_target="tpu_custom_call" | custom-call | tf_op jit(solution)/shard_map/last_steps/pallas_call | solution.py:506
  (27 shorter events, 4.3 us)
Async XLA Ops:
  10.1 29.7 %all-to-all-start = ((f32[128,1,1152]{2,1,0:T(1,128)}), f32[128,1,1152]{2,1,0:T(1,128)S(1)}, u32[]{:S(2)}, u32[]{:S(2)}) async-start(f32[128,1,1152]{2,1,0:T(1,128)} %copy.13), calls=%async_computation | async-start | bytes 1179648 | tf_op jit(solution)/shard_map/all_to_all | solution.py:444
  23.6 9.6 %collective-permute-start = (f32[128,128]{1,0:T(8,128)}, f32[128,128]{1,0:T(8,128)S(1)}, u32[]{:S(2)}, u32[]{:S(2)}) collective-permute-start(f32[128,128]{1,0:T(8,128)} %get-tuple-element.15), channel_id=1, source_target_pairs={{1,0},{2,1},{3,2},{4,3},{5,4},{6,5},{7,6},{8,7},{9,8},{10,9},{11,1... | collective-permute-start | bytes 196616 | tf_op jit(solution)/shard_map/ppermute | solution.py:432
  26.5 6.6 %collective-permute-start.1 = (f32[128,128]{1,0:T(8,128)}, f32[128,128]{1,0:T(8,128)S(1)}, u32[]{:S(2)}, u32[]{:S(2)}) collective-permute-start(f32[128,128]{1,0:T(8,128)} %get-tuple-element.16), channel_id=1, source_target_pairs={{0,1},{1,2},{2,3},{3,4},{4,5},{5,6},{6,7},{7,8},{8,9},{9,10},{10,1... | collective-permute-start | bytes 196616 | tf_op jit(solution)/shard_map/ppermute | solution.py:432
  33.2 0.6 copy-start
  33.8 0.6 copy-start.1
  36.2 14.5 %collective-permute-start.2 = (f32[5,8,384]{2,1,0:T(8,128)}, f32[5,8,384]{2,1,0:T(8,128)S(1)}, u32[]{:S(2)}, u32[]{:S(2)}) collective-permute-start(f32[5,8,384]{2,1,0:T(8,128)} %get-tuple-element.17), channel_id=1, source_target_pairs={{0,16},{16,32},{32,48},{48,64},{64,80},{80,96},{96,112},{112,0},{1... | collective-permute-start | bytes 184328 | tf_op jit(solution)/shard_map/ppermute | solution.py:432
  37.8 13.0 %collective-permute-start.3 = (f32[5,8,384]{2,1,0:T(8,128)}, f32[5,8,384]{2,1,0:T(8,128)S(1)}, u32[]{:S(2)}, u32[]{:S(2)}) collective-permute-start(f32[5,8,384]{2,1,0:T(8,128)} %get-tuple-element.18), channel_id=1, source_target_pairs={{0,112},{16,0},{32,16},{48,32},{64,48},{80,64},{96,80},{112,96},{1... | collective-permute-start | bytes 184328 | tf_op jit(solution)/shard_map/ppermute | solution.py:432
  43.2 21.1 %collective-permute-start.4 = (f32[128,128]{1,0:T(8,128)}, f32[128,128]{1,0:T(8,128)S(1)}, u32[]{:S(2)}, u32[]{:S(2)}) collective-permute-start(f32[128,128]{1,0:T(8,128)} %get-tuple-element.21), channel_id=1, source_target_pairs={{1,0},{2,1},{3,2},{4,3},{5,4},{6,5},{7,6},{8,7},{9,8},{10,9},{11,1... | collective-permute-start | bytes 196616 | tf_op jit(solution)/shard_map/ppermute | solution.py:432
  45.1 19.2 %collective-permute-start.5 = (f32[128,128]{1,0:T(8,128)}, f32[128,128]{1,0:T(8,128)S(1)}, u32[]{:S(2)}, u32[]{:S(2)}) collective-permute-start(f32[128,128]{1,0:T(8,128)} %get-tuple-element.22), channel_id=1, source_target_pairs={{0,1},{1,2},{2,3},{3,4},{4,5},{5,6},{6,7},{7,8},{8,9},{9,10},{10,1... | collective-permute-start | bytes 196616 | tf_op jit(solution)/shard_map/ppermute | solution.py:432
  50.8 0.6 copy-start.4
  50.8 0.6 copy-start.5
  56.0 18.2 %all-to-all-start.1 = ((f32[128,1,256]{2,1,0:T(1,128)}), f32[128,1,256]{2,1,0:T(1,128)S(1)}, u32[]{:S(2)}, u32[]{:S(2)}) async-start(f32[128,1,256]{2,1,0:T(1,128)} %copy.14), calls=%async_computation.1 | async-start | bytes 262144 | tf_op jit(solution)/shard_map/all_to_all | solution.py:444
  64.3 0.6 copy-start.2
  64.9 0.6 copy-start.3
  67.2 7.6 %collective-permute-start.6 = (f32[2,8,384]{2,1,0:T(8,128)}, f32[2,8,384]{2,1,0:T(8,128)S(1)}, u32[]{:S(2)}, u32[]{:S(2)}) collective-permute-start(f32[2,8,384]{2,1,0:T(8,128)} %get-tuple-element.23), channel_id=1, source_target_pairs={{0,16},{16,32},{32,48},{48,64},{64,80},{80,96},{96,112},{112,0},{1... | collective-permute-start | bytes 73736 | tf_op jit(solution)/shard_map/ppermute | solution.py:432
  68.6 6.3 %collective-permute-start.7 = (f32[2,8,384]{2,1,0:T(8,128)}, f32[2,8,384]{2,1,0:T(8,128)S(1)}, u32[]{:S(2)}, u32[]{:S(2)}) collective-permute-start(f32[2,8,384]{2,1,0:T(8,128)} %get-tuple-element.24), channel_id=1, source_target_pairs={{0,112},{16,0},{32,16},{48,32},{64,48},{80,64},{96,80},{112,96},{1... | collective-permute-start | bytes 73736 | tf_op jit(solution)/shard_map/ppermute | solution.py:432
  74.8 0.6 copy-start.6
  74.9 0.6 copy-start.7

commit v2 on v1

v2 whole, which is shorter than its diff:
```python
import functools

import jax
import jax.numpy as jnp
import numpy as np
from jax import lax
from jax.experimental import pallas as pl
from jax.experimental.pallas import tpu as pltpu
from jax.sharding import PartitionSpec as P

AXES = ("circ", "axial")
HALO = 8
LANES = 128
WIDE = 384
RADIUS = 2
SIDE = 5
BLOCK = 9
TOP = 16
EXT = 160
NEAR_LANES = (0, 1, -1, 16, -16, 15, -15, 17, -17)
ROW_KEY = 8192
KEY_MASK = 1024 * ROW_KEY - 1
VMEM = pl.BlockSpec(memory_space=pltpu.VMEM)
SMEM = pl.BlockSpec(memory_space=pltpu.SMEM)


def diamond(radius):
    if radius < 0:
        return []
    span = range(-radius, radius + 1)
    return [(a, b) for a in span for b in span if abs(a) + abs(b) <= radius]


def patch_plan():
    radii = (2, 1, 1, 1, 0, 0, 0)
    return [(field, cell) for field, r in enumerate(radii) for cell in diamond(r)]


def patch_table():
    table = np.full((8, 2 * LANES), -1, np.int32)
    for index, (field, (a, b)) in enumerate(patch_plan()):
        for slot in range(8):
            at = index * 8 + slot
            table[0, at] = field * SIDE + b + RADIUS
            table[1, at] = slot * 8 + a + RADIUS
    return table


def iota(shape, dim):
    return lax.broadcasted_iota(jnp.int32, shape, dim)


def call(kernel, outs, ins, name, scratch=()):
    return pl.pallas_call(
        kernel,
        out_shape=tuple(jax.ShapeDtypeStruct(s, jnp.float32) for s in outs),
        in_specs=ins,
        out_specs=tuple(VMEM for _ in outs),
        scratch_shapes=list(scratch),
        name=name,
    )


def side_strips(tiles):
    rows = tiles[0][0].shape[0]
    lane = iota((rows, LANES), 1)
    left = jnp.zeros((rows, LANES), jnp.float32)
    right = left
    for f, (first, last) in enumerate(tiles):
        mine = (lane >= f * HALO) & (lane < (f + 1) * HALO)
        left = jnp.where(mine, pltpu.roll(first, f * HALO, 1) if f else first, left)
        right = jnp.where(mine, pltpu.roll(last, f * HALO + HALO, 1), right)
    return left, right


def side_tile(from_east, from_west, f):
    lane = iota(from_east.shape, 1)
    east = pltpu.roll(from_east, (LANES - f * HALO) % LANES, 1) if f else from_east
    west = pltpu.roll(from_west, LANES - HALO - f * HALO, 1)
    return jnp.where(lane < HALO, east, jnp.where(lane >= LANES - HALO, west, 0.0))


def exact_pick(pick, x):
    pick = jnp.where(pick, 1.0, 0.0).astype(jnp.bfloat16)
    high = x.astype(jnp.bfloat16)
    rest = x - high.astype(jnp.float32)
    middle = rest.astype(jnp.bfloat16)
    low = (rest - middle.astype(jnp.float32)).astype(jnp.bfloat16)
    total = jnp.dot(pick, low, preferred_element_type=jnp.float32)
    total = total + jnp.dot(pick, middle, preferred_element_type=jnp.float32)
    return total + jnp.dot(pick, high, preferred_element_type=jnp.float32)


def lanes_to(x, source, target, count):
    lane = iota(x.shape, 1)
    turned = pltpu.roll(x, (target - source) % LANES, 1) if target != source else x
    return jnp.where((lane >= target) & (lane < target + count), turned, 0.0)


def pack_kernel(
    count, cells, partner, target, row, fluid, ca, vo, co, packed, to_west, to_east
):
    i_circ = lax.axis_index("circ")
    i_axial = lax.axis_index("axial")
    fields = [ca.at[0], ca.at[1], vo.at[0], vo.at[1], co]
    left, right = side_strips([(f[:, :LANES], f[:, LANES:]) for f in fields])
    to_west[...] = left
    to_east[...] = right
    slots = fluid.shape[0]
    t_row = target[...]
    order = iota((1, slots), 1)
    used = order < count[0]
    eye = iota((slots, slots), 0) == iota((slots, slots), 1)
    t_col = jnp.sum(jnp.where(eye, t_row, 0), axis=1, keepdims=True)
    earlier = (
        (t_col == t_row)
        & (iota((slots, slots), 0) < count[0])
        & (iota((slots, slots), 0) < iota((slots, slots), 1))
    )
    rank = jnp.sum(jnp.where(earlier, 1, 0), axis=0, keepdims=True)
    place = jnp.where(used, rank * 128 + t_row, -1)
    pick = iota((256, slots), 0) == place
    tags = jnp.sum(jnp.where(pick, row[...] + 1, 0), axis=1, keepdims=True).astype(jnp.float32)
    tags0, tags1 = tags[:128], tags[128:]
    moved = exact_pick(pick, fluid[...])
    for half in range(2):
        for part in range(4):
            packed[pl.ds(half * 4 + part, 128, stride=BLOCK), :] = moved[
                half * 128 : half * 128 + 128, part * LANES : part * LANES + LANES
            ]
    lane = iota((128, LANES), 1)
    tail = jnp.where(lane == 0, tags0, jnp.where(lane == 1, tags1, 0.0))
    for slot in range(8):
        cell = cells[slot]
        for base, value in (
            (8, i_circ * 128 + cell // 256),
            (16, i_axial * 256 + cell % 256),
            (24, partner[slot]),
        ):
            tail = jnp.where(lane == base + slot, value.astype(jnp.float32), tail)
    east = jnp.where(lane == 2, tags0, jnp.where(lane == 3, tags1, 0.0))
    west = jnp.where(lane == 4, tags0, jnp.where(lane == 5, tags1, 0.0))
    for half in range(2):
        rows = moved[half * 128 : half * 128 + 128]
        for k in range(2):
            first = rows[:, 2 * k * LANES : (2 * k + 1) * LANES]
            last = rows[:, (2 * k + 1) * LANES : (2 * k + 2) * LANES]
            east = east + lanes_to(first, 0, 32 + half * 16 + k * HALO, HALO)
            west = west + lanes_to(last, LANES - HALO, 64 + half * 16 + k * HALO, HALO)
    tail = tail + pltpu.roll(east, 127, 0) + pltpu.roll(west, 1, 0)
    packed[pl.ds(8, 128, stride=BLOCK), :] = tail


def force_kernel(got, ca, vo, co, from_east, from_west, force, ports, to_north, to_south):
    tail = got[pl.ds(8, 128, stride=BLOCK), :]
    tail_t = jnp.transpose(tail)
    ports[...] = tail_t[8:32]
    line = iota((128, 128), 0).astype(jnp.float32) + 1.0

    def picked(k, x):
        return exact_pick(tail_t[k : k + 1] == line, x)

    halves = []
    for half in range(2):
        parts = [got[pl.ds(half * 4 + part, 128, stride=BLOCK), :] for part in range(4)]
        halves.append(picked(half, jnp.concatenate(parts, axis=1)))
    total = halves[0] + halves[1]
    east = picked(2, tail) + pltpu.roll(picked(3, tail), LANES - 16, 1)
    west = picked(4, tail) + pltpu.roll(picked(5, tail), LANES - 16, 1)
    sides = [
        lanes_to(east, 32 + k * HALO, 0, HALO) + lanes_to(west, 64 + k * HALO, LANES - HALO, HALO)
        for k in range(2)
    ]
    shear = jnp.concatenate([total[:, :256], sides[0]], axis=1)
    agonist = jnp.concatenate([total[:, 256:], sides[1]], axis=1)
    stress = shear * shear / (1.0 + shear * shear)
    stimulus = 0.5 + 0.5 * jnp.tanh(0.5 * agonist)
    a_s = 0.1 * stimulus
    a_e = 0.02 + 0.15 * stress + 0.04 * stimulus
    force[0] = a_s
    force[1] = a_e
    fields = [ca.at[0], ca.at[1], vo.at[0], vo.at[1], co]
    for rows, out in ((slice(0, HALO), to_north), (slice(128 - HALO, 128), to_south)):
        for f, ref in enumerate(fields):
            out[f, :, : 2 * LANES] = ref[rows, :]
            out[f, :, 2 * LANES :] = side_tile(from_east[rows, :], from_west[rows, :], f)
        out[5] = a_s[rows]
        out[6] = a_e[rows]


def extract(refs, cells, table, tmp, out):
    lane = iota((8, LANES), 1)
    for slot in range(8):
        cell = cells[slot]
        row = cell // 256 + TOP - RADIUS
        col = cell % 256 - RADIUS
        base = pl.multiple_of(row // 8 * 8, 8)
        up = row - base
        kept = jnp.zeros((8, LANES), jnp.float32)
        for f, ref in enumerate(refs):
            window = ref[pl.ds(base, 16), :]
            window = pltpu.roll(window, 16 - up, 0)[:8]
            window = pltpu.roll(window, (2 * WIDE - col + f * SIDE) % WIDE, 1)[:, :LANES]
            kept = jnp.where((lane >= f * SIDE) & (lane < (f + 1) * SIDE), window, kept)
        tmp[slot * 8 : slot * 8 + 8, :] = kept
    width = 2 * LANES
    pieces = exact_take(tmp[...], iota((LANES, width), 0) == table[0:1, :])
    mine = iota((64, width), 0) == table[1:2, :]
    line = jnp.sum(jnp.where(mine, pieces, 0.0), axis=0, keepdims=True)
    for k in range(2):
        out[pl.ds(k, 128, stride=2), :] = jnp.broadcast_to(
            line[:, k * LANES : (k + 1) * LANES], (128, LANES)
        )


def exact_take(x, pick):
    pick = jnp.where(pick, 1.0, 0.0).astype(jnp.bfloat16)
    high = x.astype(jnp.bfloat16)
    rest = x - high.astype(jnp.float32)
    middle = rest.astype(jnp.bfloat16)
    low = (rest - middle.astype(jnp.float32)).astype(jnp.bfloat16)
    total = jnp.dot(low, pick, preferred_element_type=jnp.float32)
    total = total + jnp.dot(middle, pick, preferred_element_type=jnp.float32)
    return total + jnp.dot(high, pick, preferred_element_type=jnp.float32)


def build_ext(dst, centre, side, north, south):
    dst[TOP : TOP + 128, : 2 * LANES] = centre
    dst[TOP : TOP + 128, 2 * LANES :] = side
    dst[TOP - HALO : TOP, :] = north
    dst[TOP + 128 : TOP + 128 + HALO, :] = south
    clear_ends(dst)


def clear_ends(dst):
    dst[: TOP - HALO, :] = jnp.zeros((TOP - HALO, WIDE), jnp.float32)
    dst[TOP + 128 + HALO :, :] = jnp.zeros((EXT - TOP - 128 - HALO, WIDE), jnp.float32)


def first_patch_kernel(
    cells, ca, vo, co, from_east, from_west, from_north, from_south, force, table,
    kept, out, start, tmp
):
    fields = [ca.at[0], ca.at[1], vo.at[0], vo.at[1], co]
    for f, ref in enumerate(fields):
        scale = 0.05 if f == 4 else 1.0
        build_ext(
            start.at[f] if f < 4 else kept.at[4],
            ref[...] * scale,
            side_tile(from_east[...], from_west[...], f) * scale,
            from_north[f] * scale,
            from_south[f] * scale,
        )
        if f < 4:
            clear_ends(kept.at[f])
    for f in range(2):
        build_ext(
            kept.at[5 + f], force[f, :, :256], force[f, :, 256:], from_north[5 + f], from_south[5 + f]
        )
    one_step(
        [start.at[f] for f in range(4)], [kept.at[f] for f in range(4)], coefs(kept), None
    )
    take_patches(kept, kept, start.at[2], cells, table, tmp, out)


def coefs(kept):
    return [kept.at[f] for f in (4, 5, 6)]


def take_patches(after, coef, before_v, cells, table, tmp, out):
    refs = [after.at[2], after.at[0], after.at[3], coef.at[4], after.at[1], coef.at[5], before_v]
    extract(refs, cells, table, tmp, out)


def port_places(ports):
    return [ports[k * 8 : k * 8 + 8, :].astype(jnp.int32) for k in range(3)]


def port_sim(got, codes, rows, cols, partner):
    got_t = [jnp.transpose(got[pl.ds(k, 128, stride=2), :]) for k in range(2)]
    fields = [{} for _ in range(7)]
    for index, (field, cell) in enumerate(patch_plan()):
        at = index * 8 % LANES
        fields[field][cell] = got_t[index * 8 // LANES][at : at + 8]
    v, s, u, spread, e, a_s, before = fields
    device = partner // 8
    slot = partner % 8

    def near(f, cell):
        a, b = cell
        left = jnp.where(cols == -b, f[cell], f[(a, b - 1)])
        right = jnp.where(cols == 4095 - b, f[cell], f[(a, b + 1)])
        return f[(a - 1, b)] + f[(a + 1, b)] + left + right

    def gain_of(here):
        theirs = jnp.zeros_like(here)
        for k in range(8):
            line = jnp.broadcast_to(here[k : k + 1], here.shape)
            theirs = jnp.where(slot == k, jnp.take_along_axis(line, device, axis=1), theirs)
        return 0.2 * (theirs - here)

    def add_gain(f, gain, reach):
        added = dict(f)
        index = 0
        for k in range(8):
            turned = pltpu.roll(gain, k, 0) if k else gain
            for shift in NEAR_LANES:
                moved = pltpu.roll(turned, (-shift) % LANES, 1) if shift else turned
                code = codes[index]
                index += 1
                for c in diamond(reach):
                    key = (c[0] * ROW_KEY + c[1]) & KEY_MASK
                    added[c] = added[c] + jnp.where(code == key, moved, 0.0)
        return added

    gains = [gain_of(before[(0, 0)])]
    v = add_gain(v, gains[0], RADIUS)
    for step in range(RADIUS + 1):
        gains.append(gain_of(v[(0, 0)]))
        reach = RADIUS - 1 - step
        if reach < 0:
            break
        parts = {c: reciprocals(s[c], e.get(c)) for c in diamond(reach)}
        new_v = {}
        for c in diamond(reach):
            new_v[c] = v_step(parts[c], v[c], u[c], near(v, c), spread[c])
        new_s, new_u = {}, {}
        for c in diamond(reach - 1):
            new_s[c] = s_step(parts[c], s[c], e[c], v[c], near(s, c), spread[c], a_s[c])
            new_u[c] = u_step(parts[c], v[c], u[c], near(u, c), spread[c])
        v = add_gain(new_v, gains[-1], reach)
        s, u = new_s, new_u
    return gains


def reciprocals(s, e):
    half, whole = s + 0.5, s + 1.0
    both = half * whole
    if e is None:
        inv = 1.0 / both
        return inv * whole, inv * half, None
    end = e + 1.0
    inv = 1.0 / (both * end)
    rest = inv * end
    return rest * whole, rest * half, inv * both


def s_step(parts, s, e, v, near, spread, a_s):
    return (
        s * (0.97 - 4.0 * spread)
        + 0.03 * e
        + (a_s - 0.08)
        + 0.04 * jnp.tanh(v + 0.3)
        + 0.06 * parts[0]
        + spread * near
    )


def e_step(s, e, near, spread, a_e):
    return e * (0.88 - 4.0 * spread) + 0.03 * s + a_e + spread * near


def v_step(parts, v, u, near, spread):
    return (
        v * (0.71 - 4.0 * spread + 0.15 * parts[1])
        + 0.18 * parts[1]
        - 0.23
        + 0.04 * u
        + spread * near
    )


def u_step(parts, v, u, near, spread):
    return (
        u * (0.78 - 4.0 * spread + 0.1 * parts[2])
        + 0.12 * parts[2]
        - 0.152
        + 0.04 * v
        + spread * near
    )


def make_codes(rows, cols, codes):
    key = rows * ROW_KEY + cols
    index = 0
    for k in range(8):
        turned = pltpu.roll(key, k, 0) if k else key
        for shift in NEAR_LANES:
            moved = pltpu.roll(turned, (-shift) % LANES, 1) if shift else turned
            codes[index] = (moved - key) & KEY_MASK
            index += 1


def my_column(value, lane_of):
    tiles = []
    lane = iota((8, LANES), 1)
    for shift in NEAR_LANES:
        at = (lane_of + shift) & (LANES - 1)
        tiles.append(jnp.sum(jnp.where(lane == at, value, 0.0), axis=1, keepdims=True))
    tiles.append(jnp.zeros((128 - 8 * len(tiles), 1), jnp.float32))
    return jnp.concatenate(tiles, axis=0)


def injections(rows, cols, gains, inject):
    i_circ = lax.axis_index("circ")
    i_axial = lax.axis_index("axial")
    lane_of = i_circ * 16 + i_axial
    row = my_column(rows.astype(jnp.float32), lane_of).astype(jnp.int32)
    col = my_column(cols.astype(jnp.float32), lane_of).astype(jnp.int32)
    row = ((row - i_circ * 128 + HALO) & 1023) + (TOP - HALO)
    col = col - i_axial * 256
    ok = (iota((128, 1), 0) < 72) & (col >= -HALO) & (col < 256 + HALO)
    col = jnp.where(ok, jnp.where(col < 0, col + WIDE, col), -1)
    in_row = jnp.where(row == iota((128, 256), 1), 1.0, 0.0)
    in_row = jnp.transpose(in_row)[:EXT] > 0.5
    in_col = col == iota((128, WIDE), 1)
    for k, gain in enumerate(gains):
        line = jnp.where(in_col, my_column(gain, lane_of), 0.0)
        inject[k] = exact_pick(in_row, line)


def one_step(now, later, coef, inject):
    lane = iota((8, WIDE), 1)
    i_axial = lax.axis_index("axial")
    first = (lane == 0) & (i_axial == 0)
    last = (lane == 255) & (i_axial == 15)
    for tile in range(1, EXT // 8 - 1):
        at = slice(tile * 8, tile * 8 + 8)
        mid, near = [], []
        for f in range(4):
            x = now[f][at, :]
            up = now[f][tile * 8 - 1 : tile * 8 + 7, :]
            down = now[f][tile * 8 + 1 : tile * 8 + 9, :]
            left = jnp.where(first, x, pltpu.roll(x, 1, 1))
            right = jnp.where(last, x, pltpu.roll(x, WIDE - 1, 1))
            mid.append(x)
            near.append(up + down + left + right)
        s, e, v, u = mid
        spread = coef[0][at, :]
        parts = reciprocals(s, e)
        new_v = v_step(parts, v, u, near[2], spread)
        later[0][at, :] = s_step(parts, s, e, v, near[0], spread, coef[1][at, :])
        later[1][at, :] = e_step(s, e, near[1], spread, coef[2][at, :])
        later[2][at, :] = new_v if inject is None else new_v + inject[at, :]
        later[3][at, :] = u_step(parts, v, u, near[3], spread)


def coupled_steps(kept, got, ports, state, codes, inject):
    rows, cols, partner = port_places(ports)
    make_codes(rows, cols, codes)
    gains = port_sim(got, codes, rows, cols, partner)
    injections(rows, cols, gains, inject)
    for f in range(4):
        state[0, f] = kept[f] + inject[0] if f == 2 else kept[f]
        clear_ends(state.at[1, f])

    def one(k, carry):
        now = lax.rem(k, 2)
        one_step(
            [state.at[now, f] for f in range(4)],
            [state.at[1 - now, f] for f in range(4)],
            coefs(kept),
            inject.at[k + 1],
        )
        return carry

    lax.fori_loop(0, 3, one, 0)


def first_steps_kernel(cells, kept, got, ports, table, ahead, out, state, codes, inject, tmp):
    coupled_steps(kept, got, ports, state, codes, inject)
    for f in range(4):
        clear_ends(ahead.at[f])
    one_step(
        [state.at[1, f] for f in range(4)], [ahead.at[f] for f in range(4)], coefs(kept), None
    )
    take_patches(ahead, kept, state.at[1, 2], cells, table, tmp, out)


def last_steps_kernel(kept, ahead, got, ports, ca_out, vo_out, state, codes, inject):
    both = [ahead.at[f] for f in range(4)] + [kept.at[f] for f in (4, 5, 6)]
    coupled_steps(Views(both), got, ports, state, codes, inject)
    for f in range(2):
        ca_out[f] = state[1, f, TOP : TOP + 128, : 2 * LANES]
        vo_out[f] = state[1, f + 2, TOP : TOP + 128, : 2 * LANES]


class Views:
    def __init__(self, refs):
        self.refs = refs
        self.at = refs

    def __getitem__(self, k):
        return self.refs[k][...]


def shifted(value, axis, step, periodic):
    count = lax.axis_size(axis)
    pairs = [(i, i + step) for i in range(count)]
    if periodic:
        pairs = [(i, j % count) for i, j in pairs]
    return lax.ppermute(value, axis, [(i, j) for i, j in pairs if 0 <= j < count])


def swap_axial(to_west, to_east):
    return shifted(to_west, "axial", -1, False), shifted(to_east, "axial", 1, False)


def swap_circ(to_north, to_south):
    return shifted(to_south, "circ", 1, True), shifted(to_north, "circ", -1, True)


def to_all(value):
    blocks = value.reshape(128, 1, -1)
    return lax.all_to_all(blocks, AXES, 0, 0, tiled=True).reshape(value.shape)


def local(ca, vo, co, fluid, target, row, count, cells, partner):
    table = jnp.asarray(patch_table())
    packed, to_west, to_east = call(
        pack_kernel,
        [(128 * BLOCK, LANES), (128, LANES), (128, LANES)],
        [SMEM] * 3 + [VMEM] * 6,
        "pack",
    )(
        count, cells, partner, target.reshape(1, -1), row.reshape(1, -1), fluid.reshape(192, 512),
        ca, vo, co,
    )
    from_east, from_west = swap_axial(to_west, to_east)
    received = to_all(packed)
    force, ports, to_north, to_south = call(
        force_kernel,
        [(2, 128, WIDE), (24, LANES), (7, HALO, WIDE), (7, HALO, WIDE)],
        [VMEM] * 6,
        "force",
    )(received, ca, vo, co, from_east, from_west)
    from_north, from_south = swap_circ(to_north, to_south)
    tmp = pltpu.VMEM((64, LANES), jnp.float32)
    kept, patches = call(
        first_patch_kernel,
        [(7, EXT, WIDE), (256, LANES)],
        [SMEM] + [VMEM] * 9,
        "first_patch",
        [pltpu.VMEM((4, EXT, WIDE), jnp.float32), tmp],
    )(cells, ca, vo, co, from_east, from_west, from_north, from_south, force, table)
    got = to_all(patches)
    scratch = [
        pltpu.VMEM((2, 4, EXT, WIDE), jnp.float32),
        pltpu.VMEM((72, 8, LANES), jnp.int32),
        pltpu.VMEM((4, EXT, WIDE), jnp.float32),
    ]
    ahead, patches = call(
        first_steps_kernel,
        [(4, EXT, WIDE), (256, LANES)],
        [SMEM] + [VMEM] * 4,
        "first_steps",
        scratch + [tmp],
    )(cells, kept, got, ports, table)
    got = to_all(patches)
    return call(last_steps_kernel, [(2, 128, 256)] * 2, [VMEM] * 4, "last_steps", scratch)(
        kept, ahead, got, ports
    )


def solution(mesh):
    return jax.shard_map(
        local,
        mesh=mesh,
        in_specs=(
            P(None, "circ", "axial"),
            P(None, "circ", "axial"),
            P("circ", "axial"),
            P(AXES, None, None),
            P(AXES, None),
            P(AXES),
            P(AXES),
            P(AXES),
            P(AXES),
        ),
        out_specs=(P(None, "circ", "axial"), P(None, "circ", "axial")),
        check_vma=False,
    )
```

time: 123 us -> 96.5 us (0.78)
  starting transfers between devices: 41.8 us -> 22.4 us
  local copies, waits for them, and re-layouts: 15.9 us -> 3.23 us
  blocking collectives: 23.9 us -> 33.3 us
  Pallas kernels: 34 us -> 26.6 us
  waiting for transfers between devices: 3.49 us -> 9.17 us
  other arithmetic: 1.97 us -> 0 us
    ppermute x8 -> x4, starting transfers between devices: 22.1 us -> 10.9 us  [shifted(): lax.ppermute(value, axis, [(i, j) for i, j in pairs if 0 <= j < count])]
    all_to_all x1 -> x2, blocking collectives: 23.9 us -> 33.3 us  [to_all(): return lax.all_to_all(blocks, AXES, 0, 0, tiled=True).reshape(value.shape)]
    all_to_all x2 -> x1, starting transfers between devices: 19.8 us -> 11.5 us  [to_all(): return lax.all_to_all(blocks, AXES, 0, 0, tiled=True).reshape(value.shape)]
    pallas_call x8 -> x5, Pallas kernels: 34 us -> 26.6 us  [the longest x1 9.01 us: local(): call(first_steps_kernel, [(4, EXT, WIDE), (256, LANES)], [SMEM] + [VMEM]...]
    all_to_all x3 -> x0, local copies, waits for them, and re-layouts: 5.97 us -> none  [to_all(): return lax.all_to_all(value, AXES, 0, 0, tiled=True)]
    unnamed x20 -> x11, local copies, waits for them, and re-layouts: 7.88 us -> 3.23 us
    ppermute x8 -> x4, waiting for transfers between devices: 2.27 us -> 5.55 us  [shifted(): lax.ppermute(value, axis, [(i, j) for i, j in pairs if 0 <= j < count])]
    all_to_all x2 -> x1, waiting for transfers between devices: 1.22 us -> 3.62 us  [to_all(): return lax.all_to_all(blocks, AXES, 0, 0, tiled=True).reshape(value.shape)]
  transfers between devices with their start and end apart: 10 -> 5, of which waited for: 2 -> 4; matrix products, arithmetic and copies ran while one was open for 4% -> 0% of each run, Pallas kernels for 9% -> 0%
where the time goes in v2:
time: 96.5 us; the launch traced here: 96 us
  blocking collectives  33.3 us (35%)
  Pallas kernels  26.6 us (28%)
  starting transfers between devices  22.4 us (23%)
  waiting for transfers between devices  9.17 us (10%)
  local copies, waits for them, and re-layouts  3.23 us (3%)
  between operations  1.32 us (1%)
    all_to_all x2, blocking collectives, to_all(): return lax.all_to_all(blocks, AXES, 0, 0, tiled=True).reshape(value.shape)  33.3 us
    all_to_all x1, starting transfers between devices, to_all(): return lax.all_to_all(blocks, AXES, 0, 0, tiled=True).reshape(value.shape)  11.5 us
    ppermute x4, starting transfers between devices, shifted(): lax.ppermute(value, axis, [(i, j) for i, j in pairs if 0 <= j < count])  10.9 us
    pallas_call x1, Pallas kernels, local(): call(first_steps_kernel, [(4, EXT, WIDE), (256, LANES)], [SMEM] + [VMEM]...  9.01 us
    pallas_call x1, Pallas kernels, local(): call(last_steps_kernel, [(2, 128, 256)] * 2, [VMEM] * 4, 'last_steps', sc...  8.07 us
    ppermute x4, waiting for transfers between devices, shifted(): lax.ppermute(value, axis, [(i, j) for i, j in pairs if 0 <= j < count])  5.55 us
    pallas_call x1, Pallas kernels, local(): call(first_patch_kernel, [(7, EXT, WIDE), (256, LANES)], [SMEM] + [VMEM]...  4.01 us
    all_to_all x1, waiting for transfers between devices, to_all(): return lax.all_to_all(blocks, AXES, 0, 0, tiled=True).reshape(value.shape)  3.62 us
  transfers between devices with their start and end apart: 5, of which 4 were waited for; matrix products, arithmetic and copies ran while one was open for 0% of the time, Pallas kernels for 0%

profile of v2, /device:TPU:1, one launch (start us, length us, event | category | flops | bytes accessed | tf_op | source)
XLA Modules:
  0.0 96.0 jit_solution(14232122193534441007)
XLA Ops:
  1.3 1.8 %copy.15 = f32[24,8,2,256]{3,1,2,0:T(8,128)} copy(f32[24,8,2,256]{3,2,1,0:T(2,128)} %bitcast.15) | data formatting | bytes 786432
  3.0 2.7 %pack.1 = (f32[1152,128]{1,0:T(8,128)}, f32[128,128]{1,0:T(8,128)}, f32[128,128]{1,0:T(8,128)}) custom-call(s32[1]{0:T(128)S(6)} %copy.16.count, s32[8]{0:T(128)} %cells.5, s32[8]{0:T(128)} %partner.1, s32[1,192]{1,0:T(1,128)} %bitcast.18, s32[1,192]{1,0:T(1,128)} %bitcast.19, f32[192,512]{1,0:T(8,128)} %bitcast.11, f32[2,128,256]{2,1,0:T(8,128)} %ca.5, ...), custom_call_target="tpu_custom_call" | custom-call | tf_op jit(solution)/shard_map/pack/pallas_call | solution.py:520
  5.8 11.5 %all-to-all-start = ((f32[128,1,1152]{2,1,0:T(1,128)}), f32[128,1,1152]{2,1,0:T(1,128)S(1)}, u32[]{:S(2)}, u32[]{:S(2)}) async-start(f32[128,1,1152]{2,1,0:T(1,128)} %bitcast.12), calls=%async_computation | async-start | bytes 1179648 | tf_op jit(solution)/shard_map/all_to_all | solution.py:515
  17.2 3.0 %collective-permute-start = (f32[128,128]{1,0:T(8,128)}, f32[128,128]{1,0:T(8,128)S(1)}, u32[]{:S(2)}, u32[]{:S(2)}) collective-permute-start(f32[128,128]{1,0:T(8,128)} %get-tuple-element.13), channel_id=1, source_target_pairs={{1,0},{2,1},{3,2},{4,3},{5,4},{6,5},{7,6},{8,7},{9,8},{10,9},{11,1... | collective-permute-start | bytes 196616 | tf_op jit(solution)/shard_map/ppermute | solution.py:502
  20.2 4.4 %collective-permute-start.1 = (f32[128,128]{1,0:T(8,128)}, f32[128,128]{1,0:T(8,128)S(1)}, u32[]{:S(2)}, u32[]{:S(2)}) collective-permute-start(f32[128,128]{1,0:T(8,128)} %get-tuple-element.14), channel_id=1, source_target_pairs={{0,1},{1,2},{2,3},{3,4},{4,5},{5,6},{6,7},{7,8},{8,9},{9,10},{10,1... | collective-permute-start | bytes 196616 | tf_op jit(solution)/shard_map/ppermute | solution.py:502
  24.6 2.2 %collective-permute-done.from_east = f32[128,128]{1,0:T(8,128)S(1)} collective-permute-done((f32[128,128]{1,0:T(8,128)}, f32[128,128]{1,0:T(8,128)S(1)}, u32[]{:S(2)}, u32[]{:S(2)}) %collective-permute-start) | collective-permute-done | bytes 65568 | tf_op jit(solution)/shard_map/ppermute | solution.py:502
  26.9 0.0 copy-start.1
  26.9 0.9 collective-permute-done.1.from_west
  27.8 0.0 copy-start.2
  27.8 3.6 %all-to-all-done = f32[128,1,1152]{2,1,0:T(1,128)S(1)} async-done(((f32[128,1,1152]{2,1,0:T(1,128)}), f32[128,1,1152]{2,1,0:T(1,128)S(1)}, u32[]{:S(2)}, u32[]{:S(2)}) %all-to-all-start) | async-done | bytes 589856 | tf_op jit(solution)/shard_map/all_to_all | solution.py:515
  31.4 0.0 copy-start
  31.4 0.0 copy-done.1
  31.4 0.0 copy-done.2
  31.4 0.8 copy-done
  32.2 2.8 %force.1 = (f32[2,128,384]{2,1,0:T(8,128)}, f32[24,128]{1,0:T(8,128)}, f32[7,8,384]{2,1,0:T(8,128)}, f32[7,8,384]{2,1,0:T(8,128)}) custom-call(f32[1152,128]{1,0:T(8,128)} %bitcast.10, f32[2,128,256]{2,1,0:T(8,128)} %ca.5, f32[2,128,256]{2,1,0:T(8,128)} %vo.5, f32[128,256]{1,0:T(8,128)} %co.5, f32[128,128]{1,0:T(8,128)} %copy-done.1, f32[128,128]{1,0:T(8,128)} %copy-done.2), custom_call_target="tpu_custom_call" | custom-call | tf_op jit(solution)/shard_map/force/pallas_call | solution.py:531
  35.0 0.0 collective-permute-start.2
  35.0 3.6 %collective-permute-start.3 = (f32[7,8,384]{2,1,0:T(8,128)}, f32[7,8,384]{2,1,0:T(8,128)S(1)}, u32[]{:S(2)}, u32[]{:S(2)}) collective-permute-start(f32[7,8,384]{2,1,0:T(8,128)} %get-tuple-element.17), channel_id=1, source_target_pairs={{0,112},{16,0},{32,16},{48,32},{64,48},{80,64},{96,80},{112,96},{1... | collective-permute-start | bytes 258056 | tf_op jit(solution)/shard_map/ppermute | solution.py:502
  38.6 2.4 %collective-permute-done.2.from_north = f32[7,8,384]{2,1,0:T(8,128)S(1)} collective-permute-done((f32[7,8,384]{2,1,0:T(8,128)}, f32[7,8,384]{2,1,0:T(8,128)S(1)}, u32[]{:S(2)}, u32[]{:S(2)}) %collective-permute-start.2) | collective-permute-done | bytes 86048 | tf_op jit(solution)/shard_map/ppermute | solution.py:502
  41.0 0.0 copy-start.3
  41.0 0.0 collective-permute-done.3.from_south
  41.0 0.0 copy-start.4
  41.0 0.6 copy-done.3
  41.6 0.0 copy-done.4
  41.6 4.0 %first_patch.1 = (f32[7,160,384]{2,1,0:T(8,128)}, f32[256,128]{1,0:T(8,128)}) custom-call(s32[8]{0:T(128)} %cells.5, f32[2,128,256]{2,1,0:T(8,128)} %ca.5, f32[2,128,256]{2,1,0:T(8,128)} %vo.5, f32[128,256]{1,0:T(8,128)} %co.5, f32[128,128]{1,0:T(8,128)} %copy-done.1, f32[128,128]{1,0:T(8,128)} %copy-done.2, f32[7,8,384]{2,1,0:T(8,128)} %copy-done.3, ...), custom_call_target="tpu_custom_call" | custom-call | tf_op jit(solution)/shard_map/first_patch/pallas_call | solution.py:539
  45.6 18.5 %all_to_all.15 = f32[128,1,256]{2,1,0:T(1,128)} all-to-all(f32[128,1,256]{2,1,0:T(1,128)} %bitcast.16), channel_id=1, replica_groups=mesh['circ'=8,'axial'=16] {'circ','axial'}, dimensions={0} | all-to-all | bytes 262144 | tf_op jit(solution)/shard_map/all_to_all | solution.py:515
  64.1 9.0 %first_steps.1 = (f32[4,160,384]{2,1,0:T(8,128)}, f32[256,128]{1,0:T(8,128)}) custom-call(s32[8]{0:T(128)} %cells.5, f32[7,160,384]{2,1,0:T(8,128)} %get-tuple-element.19.kept, f32[256,128]{1,0:T(8,128)} %bitcast.14, f32[24,128]{1,0:T(8,128)} %get-tuple-element.21.ports, s32[8,256]{1,0:T(8,128)} %constant.2.clone.table), custom_call_target="tpu_custom_call" | custom-call | tf_op jit(solution)/shard_map/first_steps/pallas_call | solution.py:552
  73.1 14.8 %all_to_all.16 = f32[128,1,256]{2,1,0:T(1,128)} all-to-all(f32[128,1,256]{2,1,0:T(1,128)} %bitcast.17), channel_id=1, replica_groups=mesh['circ'=8,'axial'=16] {'circ','axial'}, dimensions={0} | all-to-all | bytes 262144 | tf_op jit(solution)/shard_map/all_to_all | solution.py:515
  88.0 8.1 %last_steps.1 = (f32[2,128,256]{2,1,0:T(8,128)}, f32[2,128,256]{2,1,0:T(8,128)}) custom-call(f32[7,160,384]{2,1,0:T(8,128)} %get-tuple-element.19.kept, f32[4,160,384]{2,1,0:T(8,128)} %get-tuple-element.22.ahead, f32[256,128]{1,0:T(8,128)} %bitcast.13, f32[24,128]{1,0:T(8,128)} %get-tuple-element.21.ports), custom_call_target="tpu_custom_call" | custom-call | tf_op jit(solution)/shard_map/last_steps/pallas_call | solution.py:560
Async XLA Ops:
  5.8 25.6 %all-to-all-start = ((f32[128,1,1152]{2,1,0:T(1,128)}), f32[128,1,1152]{2,1,0:T(1,128)S(1)}, u32[]{:S(2)}, u32[]{:S(2)}) async-start(f32[128,1,1152]{2,1,0:T(1,128)} %bitcast.12), calls=%async_computation | async-start | bytes 1179648 | tf_op jit(solution)/shard_map/all_to_all | solution.py:515
  17.2 9.6 %collective-permute-start = (f32[128,128]{1,0:T(8,128)}, f32[128,128]{1,0:T(8,128)S(1)}, u32[]{:S(2)}, u32[]{:S(2)}) collective-permute-start(f32[128,128]{1,0:T(8,128)} %get-tuple-element.13), channel_id=1, source_target_pairs={{1,0},{2,1},{3,2},{4,3},{5,4},{6,5},{7,6},{8,7},{9,8},{10,9},{11,1... | collective-permute-start | bytes 196616 | tf_op jit(solution)/shard_map/ppermute | solution.py:502
  20.2 7.5 %collective-permute-start.1 = (f32[128,128]{1,0:T(8,128)}, f32[128,128]{1,0:T(8,128)S(1)}, u32[]{:S(2)}, u32[]{:S(2)}) collective-permute-start(f32[128,128]{1,0:T(8,128)} %get-tuple-element.14), channel_id=1, source_target_pairs={{0,1},{1,2},{2,3},{3,4},{4,5},{5,6},{6,7},{7,8},{8,9},{9,10},{10,1... | collective-permute-start | bytes 196616 | tf_op jit(solution)/shard_map/ppermute | solution.py:502
  26.9 4.5 %copy-start.1 = (f32[128,128]{1,0:T(8,128)}, f32[128,128]{1,0:T(8,128)S(1)}, u32[]{:S(2)}) copy-start(f32[128,128]{1,0:T(8,128)S(1)} %collective-permute-done.from_east) | copy-start | bytes 196612
  27.8 3.6 %copy-start.2 = (f32[128,128]{1,0:T(8,128)}, f32[128,128]{1,0:T(8,128)S(1)}, u32[]{:S(2)}) copy-start(f32[128,128]{1,0:T(8,128)S(1)} %collective-permute-done.1.from_west) | copy-start | bytes 196612
  31.4 0.8 copy-start
  35.0 6.0 %collective-permute-start.2 = (f32[7,8,384]{2,1,0:T(8,128)}, f32[7,8,384]{2,1,0:T(8,128)S(1)}, u32[]{:S(2)}, u32[]{:S(2)}) collective-permute-start(f32[7,8,384]{2,1,0:T(8,128)} %get-tuple-element.16), channel_id=1, source_target_pairs={{0,16},{16,32},{32,48},{48,64},{64,80},{80,96},{96,112},{112,0},{1... | collective-permute-start | bytes 258056 | tf_op jit(solution)/shard_map/ppermute | solution.py:502
  35.0 6.0 %collective-permute-start.3 = (f32[7,8,384]{2,1,0:T(8,128)}, f32[7,8,384]{2,1,0:T(8,128)S(1)}, u32[]{:S(2)}, u32[]{:S(2)}) collective-permute-start(f32[7,8,384]{2,1,0:T(8,128)} %get-tuple-element.17), channel_id=1, source_target_pairs={{0,112},{16,0},{32,16},{48,32},{64,48},{80,64},{96,80},{112,96},{1... | collective-permute-start | bytes 258056 | tf_op jit(solution)/shard_map/ppermute | solution.py:502
  41.0 0.6 copy-start.3
  41.0 0.6 copy-start.4

commit v3 on v2

v3 whole, which is shorter than its diff:
```python
import functools

import jax
import jax.numpy as jnp
import numpy as np
from jax import lax
from jax.experimental import pallas as pl
from jax.experimental.pallas import tpu as pltpu
from jax.sharding import PartitionSpec as P

AXES = ("circ", "axial")
HALO = 8
LANES = 128
WIDE = 384
RADIUS = 2
SIDE = 5
BLOCK = 9
EXT = 144
STEP = 18
NEAR_PORTS = 80
NEAR_LANES = (0, 1, -1, 16, -16, 15, -15, 17, -17)
ROW_KEY = 8192
KEY_MASK = 1024 * ROW_KEY - 1
VMEM = pl.BlockSpec(memory_space=pltpu.VMEM)
SMEM = pl.BlockSpec(memory_space=pltpu.SMEM)


def diamond(radius):
    if radius < 0:
        return []
    span = range(-radius, radius + 1)
    return [(a, b) for a in span for b in span if abs(a) + abs(b) <= radius]


def patch_plan():
    radii = (2, 1, 1, 1, 0, 0, 0)
    return [(field, cell) for field, r in enumerate(radii) for cell in diamond(r)]


def patch_table():
    table = np.full((8, 2 * LANES), -1, np.int32)
    for index, (field, (a, b)) in enumerate(patch_plan()):
        for slot in range(8):
            at = index * 8 + slot
            table[0, at] = field * SIDE + b + RADIUS
            table[1, at] = slot * 8 + a + RADIUS
    return table


def iota(shape, dim):
    return lax.broadcasted_iota(jnp.int32, shape, dim)


HELD = pl.BlockSpec(memory_space=pltpu.VMEM)


def call(kernel, outs, ins, name, scratch=(), last=jnp.float32, place=pltpu.VMEM, room=20):
    types = [jnp.float32] * (len(outs) - 1) + [last]
    run = pl.pallas_call(
        kernel,
        out_shape=tuple(place(s, t) for s, t in zip(outs, types)),
        in_specs=ins,
        out_specs=tuple(VMEM for _ in outs),
        scratch_shapes=list(scratch),
        name=name,
        compiler_params=pltpu.CompilerParams(vmem_limit_bytes=room * 1024 * 1024),
    )

    def placed(*args):
        return run(
            *(
                pltpu.with_memory_space_constraint(x, pltpu.VMEM) if spec is HELD else x
                for x, spec in zip(args, ins)
            )
        )

    return placed


def side_strips(tiles):
    rows = tiles[0][0].shape[0]
    lane = iota((rows, LANES), 1)
    left = jnp.zeros((rows, LANES), jnp.float32)
    right = left
    for f, (first, last) in enumerate(tiles):
        mine = (lane >= f * HALO) & (lane < (f + 1) * HALO)
        left = jnp.where(mine, pltpu.roll(first, f * HALO, 1) if f else first, left)
        right = jnp.where(mine, pltpu.roll(last, f * HALO + HALO, 1), right)
    return left, right


def side_tile(from_east, from_west, f):
    lane = iota(from_east.shape, 1)
    east = pltpu.roll(from_east, (LANES - f * HALO) % LANES, 1) if f else from_east
    west = pltpu.roll(from_west, LANES - HALO - f * HALO, 1)
    return jnp.where(lane < HALO, east, jnp.where(lane >= LANES - HALO, west, 0.0))


def three_parts(x):
    high = x.astype(jnp.bfloat16)
    rest = x - high.astype(jnp.float32)
    middle = rest.astype(jnp.bfloat16)
    low = (rest - middle.astype(jnp.float32)).astype(jnp.bfloat16)
    return high, middle, low


def one_hot(pick):
    return jnp.where(pick, 1.0, 0.0).astype(jnp.bfloat16)


def dot(a, b):
    return jnp.dot(a, b, preferred_element_type=jnp.float32)


def exact_pick(pick, x):
    pick = one_hot(pick)
    high, middle, low = three_parts(x)
    return dot(pick, low) + dot(pick, middle) + dot(pick, high)


def all_fields(ca, vo, co):
    return [ca.at[0], ca.at[1], vo.at[0], vo.at[1], co]


def strips_kernel(ca, vo, co, to_west, to_east):
    left, right = side_strips([(f[:, :LANES], f[:, LANES:]) for f in all_fields(ca, vo, co)])
    to_west[...] = jnp.transpose(left)[: 5 * HALO]
    to_east[...] = jnp.transpose(right)[: 5 * HALO]


def sides_kernel(from_east, from_west, sides):
    blank = jnp.zeros((LANES - 5 * HALO, LANES), jnp.float32)
    east = jnp.transpose(jnp.concatenate([from_east[...], blank], axis=0))
    west = jnp.transpose(jnp.concatenate([from_west[...], blank], axis=0))
    for f in range(5):
        sides[f] = side_tile(east, west, f)


def lanes_to(x, source, target, count):
    lane = iota(x.shape, 1)
    turned = pltpu.roll(x, (target - source) % LANES, 1) if target != source else x
    return jnp.where((lane >= target) & (lane < target + count), turned, 0.0)


def pack_kernel(count, cells, partner, target, row, fluid, packed):
    i_circ = lax.axis_index("circ")
    i_axial = lax.axis_index("axial")
    slots = fluid.shape[0] // 4
    t_row = target[...]
    order = iota((1, slots), 1)
    used = order < count[0]
    eye = iota((slots, slots), 0) == iota((slots, slots), 1)
    t_col = jnp.sum(jnp.where(eye, t_row, 0), axis=1, keepdims=True)
    earlier = (
        (t_col == t_row)
        & (iota((slots, slots), 0) < count[0])
        & (iota((slots, slots), 0) < iota((slots, slots), 1))
    )
    rank = jnp.sum(jnp.where(earlier, 1, 0), axis=0, keepdims=True)
    place = jnp.where(used, rank * 128 + t_row, -1)
    pick = iota((256, slots), 0) == place
    tags = jnp.sum(jnp.where(pick, row[...] + 1, 0), axis=1, keepdims=True).astype(jnp.float32)
    tags0, tags1 = tags[:128], tags[128:]
    tiles = [fluid[pl.ds(c * 2 + k, slots, stride=4), :] for k in range(2) for c in range(2)]
    moved = exact_pick(pick, jnp.concatenate(tiles, axis=1))
    for half in range(2):
        for part in range(4):
            packed[pl.ds(half * 4 + part, 128, stride=BLOCK), :] = moved[
                half * 128 : half * 128 + 128, part * LANES : part * LANES + LANES
            ]
    lane = iota((128, LANES), 1)
    tail = jnp.where(lane == 0, tags0, jnp.where(lane == 1, tags1, 0.0))
    for slot in range(8):
        cell = cells[slot]
        for base, value in (
            (8, i_circ * 128 + cell // 256),
            (16, i_axial * 256 + cell % 256),
            (24, partner[slot]),
        ):
            tail = jnp.where(lane == base + slot, value.astype(jnp.float32), tail)
    east = jnp.where(lane == 2, tags0, jnp.where(lane == 3, tags1, 0.0))
    west = jnp.where(lane == 4, tags0, jnp.where(lane == 5, tags1, 0.0))
    for half in range(2):
        rows = moved[half * 128 : half * 128 + 128]
        for k in range(2):
            first = rows[:, 2 * k * LANES : (2 * k + 1) * LANES]
            last = rows[:, (2 * k + 1) * LANES : (2 * k + 2) * LANES]
            east = east + lanes_to(first, 0, 32 + half * 16 + k * HALO, HALO)
            west = west + lanes_to(last, LANES - HALO, 64 + half * 16 + k * HALO, HALO)
    tail = tail + pltpu.roll(east, 127, 0) + pltpu.roll(west, 1, 0)
    packed[pl.ds(8, 128, stride=BLOCK), :] = tail


def force_kernel(got, ca, vo, co, sides, force, ports, to_north, to_south):
    tail = got[pl.ds(8, 128, stride=BLOCK), :]
    tail_t = jnp.transpose(tail)
    ports[...] = tail_t[8:32]
    line = iota((128, 128), 0).astype(jnp.float32) + 1.0

    def pair(k):
        return jnp.concatenate([tail_t[k : k + 1] == line, tail_t[k + 1 : k + 2] == line], axis=1)

    blocks = [
        jnp.concatenate(
            [got[pl.ds(half * 4 + part, 128, stride=BLOCK), :] for half in range(2)], axis=0
        )
        for part in range(4)
    ]
    total = exact_pick(pair(0), jnp.concatenate(blocks, axis=1))
    both = jnp.concatenate([tail, pltpu.roll(tail, LANES - 16, 1)], axis=0)
    both = jnp.concatenate(three_parts(both), axis=1)
    east, west = dot(one_hot(pair(2)), both), dot(one_hot(pair(4)), both)
    east, west = [x[:, 256:] + x[:, 128:256] + x[:, :128] for x in (east, west)]
    for tile in range(3):
        if tile < 2:
            shear = total[:, tile * LANES : (tile + 1) * LANES]
            agonist = total[:, (tile + 2) * LANES : (tile + 3) * LANES]
        else:
            shear, agonist = [
                lanes_to(east, 32 + k * HALO, 0, HALO)
                + lanes_to(west, 64 + k * HALO, LANES - HALO, HALO)
                for k in range(2)
            ]
        stress = shear * shear / (1.0 + shear * shear)
        stimulus = 0.5 + 0.5 * jnp.tanh(0.5 * agonist)
        a_s = 0.1 * stimulus
        a_e = 0.02 + 0.15 * stress + 0.04 * stimulus
        for f, value in enumerate((a_s, a_e)):
            force[f, tile] = value
            to_north[5 + f, tile] = value[:HALO]
            to_south[5 + f, tile] = value[128 - HALO :]
    for f, ref in enumerate(all_fields(ca, vo, co)):
        for rows, out in ((slice(0, HALO), to_north), (slice(128 - HALO, 128), to_south)):
            out[f, 0] = ref[rows, :LANES]
            out[f, 1] = ref[rows, LANES:]
            out[f, 2] = sides[f, rows, :]


def extract(refs, cells, table, tmp, out):
    lane = iota((8, LANES), 1)
    long_lane = iota((16, LANES), 1)
    for slot in range(8):
        cell = cells[slot]
        row = cell // 256 + HALO - RADIUS
        col = lax.rem(cell % 256 - RADIUS + WIDE, WIDE)
        base = pl.multiple_of(row // 8 * 8, 8)
        turn = 16 - (row - base)
        tile = col // LANES
        other = lax.rem(tile + 1, 3)
        inside = col % LANES
        kept = jnp.zeros((8, LANES), jnp.float32)
        for f, ref in enumerate(refs):
            window = jnp.where(
                long_lane < inside, ref[other, pl.ds(base, 16), :], ref[tile, pl.ds(base, 16), :]
            )
            window = pltpu.roll(window, turn, 0)[:8]
            window = pltpu.roll(window, (2 * LANES - inside + f * SIDE) % LANES, 1)
            kept = jnp.where((lane >= f * SIDE) & (lane < (f + 1) * SIDE), window, kept)
        tmp[slot * 8 : slot * 8 + 8, :] = kept
    width = 2 * LANES
    at = iota((LANES, width), 0)
    wanted = table[0:1, :]
    pick = one_hot((at == wanted) | (at == wanted + 40) | (at == wanted + 80))
    high, middle, low = [x.astype(jnp.float32) for x in three_parts(tmp[...])]
    pieces = dot(
        (high + pltpu.roll(middle, 40, 1) + pltpu.roll(low, 80, 1)).astype(jnp.bfloat16), pick
    )
    mine = iota((64, width), 0) == table[1:2, :]
    line = jnp.sum(jnp.where(mine, pieces, 0.0), axis=0, keepdims=True)
    for k in range(2):
        out[pl.ds(k, 128, stride=2), :] = jnp.broadcast_to(
            line[:, k * LANES : (k + 1) * LANES], (128, LANES)
        )


def build_rows(dst, tiles, north, south):
    for tile in range(3):
        dst[tile, HALO : HALO + 128, :] = tiles[tile]
        dst[tile, :HALO, :] = north[tile]
        dst[tile, HALO + 128 :, :] = south[tile]


def rows_at(j):
    return pl.ds(j, 8, stride=STEP)


def mixed_at(j):
    return pl.ds(8 * j, 8)


def to_mixed(src, dst):
    for tile in range(3):
        for j in range(STEP):
            dst[tile, mixed_at(j), :] = src[tile, rows_at(j), :]


def tables_kernel(ports, in_row, in_col, codes):
    rows, cols, _ = port_places(ports)
    make_codes(rows, cols, codes)
    i_circ = lax.axis_index("circ")
    i_axial = lax.axis_index("axial")
    row = my_column(rows.astype(jnp.float32)).astype(jnp.int32)
    col = my_column(cols.astype(jnp.float32)).astype(jnp.int32)
    row = (row - i_circ * 128 + HALO) & 1023
    col = col - i_axial * 256
    ok = (iota((NEAR_PORTS, 1), 0) < 72) & (col >= -HALO) & (col < 256 + HALO) & (row < EXT)
    col = jnp.where(ok, jnp.where(col < 0, col + WIDE, col), -1)
    group = lax.shift_right_logical(row * 57, 10)
    place = jnp.where(ok, (row - group * STEP) * 8 + group, -1)
    in_col[...] = jnp.where(col == iota((NEAR_PORTS, WIDE), 1), 1.0, 0.0)
    place = jnp.concatenate([place, place, place, jnp.full((16, 1), -1, jnp.int32)], axis=0)
    in_row[...] = jnp.transpose(jnp.where(place == iota((256, 256), 1), 1.0, 0.0))[:EXT]


def first_patch_kernel(
    cells, ca, vo, co, sides, from_north, from_south, force, table,
    ahead, coef, spread, pulled, out, start, tmp,
):
    for f, ref in enumerate(all_fields(ca, vo, co)):
        scale = 0.05 if f == 4 else 1.0
        build_rows(
            start.at[f] if f < 4 else spread,
            [t * scale for t in (ref[:, :LANES], ref[:, LANES:], sides[f])],
            from_north[f] * scale,
            from_south[f] * scale,
        )
    for f in range(2):
        build_rows(
            pulled if f == 0 else start.at[4],
            [force[f, tile] for tile in range(3)],
            from_north[5 + f],
            from_south[5 + f],
        )
    for f, ref in enumerate((spread, pulled, start.at[4])):
        to_mixed(ref, coef.at[f])
    one_step(
        [start.at[f] for f in range(4)],
        rows_at,
        [ahead.at[f] for f in range(4)],
        rows_at,
        coef_refs(coef),
        None,
    )
    take_patches(ahead, spread, pulled, start.at[2], cells, table, tmp, out)


def coef_refs(coef):
    return [coef.at[f] for f in range(3)]


def take_patches(after, spread, a_s, before_v, cells, table, tmp, out):
    refs = [after.at[2], after.at[0], after.at[3], spread, after.at[1], a_s, before_v]
    extract(refs, cells, table, tmp, out)


def port_places(ports):
    return [ports[k * 8 : k * 8 + 8, :].astype(jnp.int32) for k in range(3)]


def port_sim(got, codes, rows, cols, partner):
    got_t = [jnp.transpose(got[pl.ds(k, 128, stride=2), :]) for k in range(2)]
    fields = [{} for _ in range(7)]
    for index, (field, cell) in enumerate(patch_plan()):
        at = index * 8 % LANES
        fields[field][cell] = got_t[index * 8 // LANES][at : at + 8]
    v, s, u, spread, e, a_s, before = fields
    device = partner // 8
    slot = partner % 8

    def near(f, cell):
        a, b = cell
        left = jnp.where(cols == -b, f[cell], f[(a, b - 1)])
        right = jnp.where(cols == 4095 - b, f[cell], f[(a, b + 1)])
        return f[(a - 1, b)] + f[(a + 1, b)] + left + right

    def gain_of(here):
        theirs = jnp.zeros_like(here)
        for k in range(8):
            line = jnp.broadcast_to(here[k : k + 1], here.shape)
            theirs = jnp.where(slot == k, jnp.take_along_axis(line, device, axis=1), theirs)
        return 0.2 * (theirs - here)

    def add_gain(f, gain, reach):
        added = dict(f)
        index = 0
        for k in range(8):
            turned = pltpu.roll(gain, k, 0) if k else gain
            for shift in NEAR_LANES:
                moved = pltpu.roll(turned, (-shift) % LANES, 1) if shift else turned
                code = codes[index]
                index += 1
                for c in diamond(reach):
                    key = (c[0] * ROW_KEY + c[1]) & KEY_MASK
                    added[c] = added[c] + jnp.where(code == key, moved, 0.0)
        return added

    gains = [gain_of(before[(0, 0)])]
    v = add_gain(v, gains[0], RADIUS)
    for step in range(RADIUS + 1):
        gains.append(gain_of(v[(0, 0)]))
        reach = RADIUS - 1 - step
        if reach < 0:
            break
        parts = {c: reciprocals(s[c], e.get(c)) for c in diamond(reach)}
        new_v = {}
        for c in diamond(reach):
            new_v[c] = v_step(parts[c], v[c], u[c], near(v, c), spread[c])
        new_s, new_u = {}, {}
        for c in diamond(reach - 1):
            new_s[c] = s_step(parts[c], s[c], e[c], v[c], near(s, c), spread[c], a_s[c])
            new_u[c] = u_step(parts[c], v[c], u[c], near(u, c), spread[c])
        v = add_gain(new_v, gains[-1], reach)
        s, u = new_s, new_u
    return gains


def reciprocals(s, e):
    half, whole = s + 0.5, s + 1.0
    both = half * whole
    if e is None:
        inv = 1.0 / both
        return inv * whole, inv * half, None
    end = e + 1.0
    inv = 1.0 / (both * end)
    rest = inv * end
    return rest * whole, rest * half, inv * both


def s_step(parts, s, e, v, near, spread, a_s):
    return (
        a_s
        + s * (0.97 - 4.0 * spread)
        + 0.03 * e
        - 0.08
        + 0.04 * jnp.tanh(v + 0.3)
        + 0.06 * parts[0]
        + spread * near
    )


def e_step(s, e, near, spread, a_e):
    return a_e + e * (0.88 - 4.0 * spread) + 0.03 * s + spread * near


def v_step(parts, v, u, near, spread):
    return (
        v * (0.71 - 4.0 * spread + 0.15 * parts[1])
        + 0.18 * parts[1]
        - 0.23
        + 0.04 * u
        + spread * near
    )


def u_step(parts, v, u, near, spread):
    return (
        u * (0.78 - 4.0 * spread + 0.1 * parts[2])
        + 0.12 * parts[2]
        - 0.152
        + 0.04 * v
        + spread * near
    )


def make_codes(rows, cols, codes):
    key = rows * ROW_KEY + cols
    index = 0
    for k in range(8):
        turned = pltpu.roll(key, k, 0) if k else key
        for shift in NEAR_LANES:
            moved = pltpu.roll(turned, (-shift) % LANES, 1) if shift else turned
            codes[index] = (moved - key) & KEY_MASK
            index += 1


def my_column(value):
    lane_of = lax.axis_index("circ") * 16 + lax.axis_index("axial")
    tiles = []
    lane = iota((8, LANES), 1)
    for shift in NEAR_LANES:
        at = (lane_of + shift) & (LANES - 1)
        tiles.append(jnp.sum(jnp.where(lane == at, value, 0.0), axis=1, keepdims=True))
    tiles.append(jnp.zeros((NEAR_PORTS - 8 * len(tiles), 1), jnp.float32))
    return jnp.concatenate(tiles, axis=0)


def injections(gains, in_row, in_col, inject):
    pick = in_row[...].astype(jnp.bfloat16)
    zero = jnp.zeros((256 - 3 * NEAR_PORTS, WIDE), jnp.bfloat16)
    for k, gain in enumerate(gains):
        parts = three_parts(in_col[...] * my_column(gain))
        total = dot(pick, jnp.concatenate(list(parts) + [zero], axis=0))
        for tile in range(3):
            inject[k, tile] = total[:, tile * LANES : (tile + 1) * LANES]


def one_step(now, now_at, later, later_at, coef, inject):
    lane = iota((8, LANES), 1)
    i_axial = lax.axis_index("axial")
    head = lane == 0
    tail = lane == LANES - 1
    is_first = (lane * 0 + i_axial) == 0
    is_last = (lane * 0 + i_axial) == 15

    def load(f, tile, j):
        if j < 0:
            return pltpu.roll(now[f][tile, now_at(STEP - 1), :], 1, 0)
        if j == STEP:
            return pltpu.roll(now[f][tile, now_at(0), :], 7, 0)
        return now[f][tile, now_at(j), :]

    for j in range(STEP):
        mid, near = [], []
        for f in range(4):
            x = [load(f, tile, j) for tile in range(3)]
            left = [pltpu.roll(y, 1, 1) for y in x]
            right = [pltpu.roll(y, LANES - 1, 1) for y in x]
            lefts = [
                jnp.where(head, jnp.where(is_first, x[0], left[2]), left[0]),
                jnp.where(head, left[0], left[1]),
                jnp.where(head, left[1], left[2]),
            ]
            rights = [
                jnp.where(tail, right[1], right[0]),
                jnp.where(tail, jnp.where(is_last, x[1], right[2]), right[1]),
                jnp.where(tail, right[0], right[2]),
            ]
            mid.append(x)
            near.append(
                [
                    (load(f, tile, j - 1) + load(f, tile, j + 1)) + (lefts[tile] + rights[tile])
                    for tile in range(3)
                ]
            )
        for tile in range(3):
            s, e, v, u = [x[tile] for x in mid]
            n = [x[tile] for x in near]
            spread = coef[0][tile, mixed_at(j), :]
            parts = reciprocals(s, e)
            new_s = s_step(parts, s, e, v, n[0], spread, coef[1][tile, mixed_at(j), :])
            new_e = e_step(s, e, n[1], spread, coef[2][tile, mixed_at(j), :])
            new_v = v_step(parts, v, u, n[2], spread)
            if inject is not None:
                new_v = new_v + inject[tile, mixed_at(j), :]
            later[0][tile, later_at(j), :] = new_s
            later[1][tile, later_at(j), :] = new_e
            later[2][tile, later_at(j), :] = new_v
            later[3][tile, later_at(j), :] = u_step(parts, v, u, n[3], spread)


def coupled_steps(ahead, coef, got, ports, in_row, in_col, codes, state, inject):
    rows, cols, partner = port_places(ports)
    gains = port_sim(got, codes, rows, cols, partner)
    injections(gains, in_row, in_col, inject)
    for f in range(4):
        to_mixed(ahead.at[f], state.at[0, f])
    state[0, 2] = state[0, 2] + inject[0]

    def one(k, carry):
        now = lax.rem(k, 2)
        one_step(
            [state.at[now, f] for f in range(4)],
            mixed_at,
            [state.at[1 - now, f] for f in range(4)],
            mixed_at,
            coef,
            inject.at[k + 1],
        )
        return carry

    lax.fori_loop(0, 3, one, 0)


def first_steps_kernel(
    cells, ahead, spread, pulled, coef, got, ports, in_row, in_col, codes, table,
    later, out, state, inject, tmp,
):
    coefs = coef_refs(coef)
    coupled_steps(ahead, coefs, got, ports, in_row, in_col, codes, state, inject)
    for tile in range(3):
        for j in range(STEP):
            later[4, tile, rows_at(j), :] = state[1, 2, tile, mixed_at(j), :]
    one_step(
        [state.at[1, f] for f in range(4)],
        mixed_at,
        [later.at[f] for f in range(4)],
        rows_at,
        coefs,
        None,
    )
    take_patches(later, spread, pulled, later.at[4], cells, table, tmp, out)


def last_steps_kernel(
    ahead, coef, got, ports, in_row, in_col, codes, ca_out, vo_out, state, inject
):
    coefs = coef_refs(coef)
    coupled_steps(ahead, coefs, got, ports, in_row, in_col, codes, state, inject)
    for f in range(4):
        out = (ca_out, vo_out)[f // 2].at[f % 2]
        for tile in range(2):
            for j in range(STEP):
                state[0, f, tile, rows_at(j), :] = state[1, f, tile, mixed_at(j), :]
            out[:, tile * LANES : (tile + 1) * LANES] = state[0, f, tile, HALO : HALO + 128, :]


def shifted(value, axis, step, periodic):
    count = lax.axis_size(axis)
    pairs = [(i, i + step) for i in range(count)]
    if periodic:
        pairs = [(i, j % count) for i, j in pairs]
    return lax.ppermute(value, axis, [(i, j) for i, j in pairs if 0 <= j < count])


def swap_axial(to_west, to_east):
    return shifted(to_west, "axial", -1, False), shifted(to_east, "axial", 1, False)


def swap_circ(to_north, to_south):
    return shifted(to_south, "circ", 1, True), shifted(to_north, "circ", -1, True)


def to_all(value):
    blocks = value.reshape(128, 1, -1)
    return lax.all_to_all(blocks, AXES, 0, 0, tiled=True).reshape(value.shape)


def local(ca, vo, co, fluid, target, row, count, cells, partner):
    table = jnp.asarray(patch_table())
    field = (3, EXT, LANES)
    lines = fluid.reshape(-1, 2, 2, LANES).transpose(0, 2, 1, 3).reshape(-1, LANES)
    (packed,) = call(pack_kernel, [(128 * BLOCK, LANES)], [SMEM] * 3 + [VMEM] * 3, "pack", room=60)(
        count, cells, partner, target.reshape(1, -1), row.reshape(1, -1), lines
    )
    received = to_all(packed)
    to_west, to_east = call(strips_kernel, [(5 * HALO, LANES)] * 2, [HELD] * 3, "strips")(
        ca, vo, co
    )
    from_east, from_west = swap_axial(to_west, to_east)
    (sides,) = call(sides_kernel, [(5, 128, LANES)], [HELD] * 2, "sides")(from_east, from_west)
    ring = (7, 3, HALO, LANES)
    force, ports, to_north, to_south = call(
        force_kernel, [(2, 3, 128, LANES), (24, LANES), ring, ring], [HELD] * 5, "force"
    )(received, ca, vo, co, sides)
    from_north, from_south = swap_circ(to_north, to_south)
    in_row, in_col, codes = call(
        tables_kernel,
        [(EXT, 256), (NEAR_PORTS, WIDE), (72, 8, LANES)],
        [HELD],
        "tables",
        last=jnp.int32,
    )(ports)
    patch_space = pltpu.VMEM((64, LANES), jnp.float32)
    ahead, coef, spread, pulled, patches = call(
        first_patch_kernel,
        [(4, *field), (3, *field), field, field, (256, LANES)],
        [SMEM] + [HELD] * 8,
        "first_patch",
        [pltpu.VMEM((5, *field), jnp.float32), patch_space],
    )(cells, ca, vo, co, sides, from_north, from_south, force, table)
    got = to_all(patches)
    scratch = [pltpu.VMEM((2, 4, *field), jnp.float32), pltpu.VMEM((4, *field), jnp.float32)]
    ahead, patches = call(
        first_steps_kernel,
        [(5, *field), (256, LANES)],
        [SMEM] + [HELD] * 10,
        "first_steps",
        scratch + [patch_space],
    )(cells, ahead, spread, pulled, coef, got, ports, in_row, in_col, codes, table)
    got = to_all(patches)
    return call(
        last_steps_kernel,
        [(2, 128, 256)] * 2,
        [HELD] * 7,
        "last_steps",
        scratch,
        place=jax.ShapeDtypeStruct,
    )(ahead, coef, got, ports, in_row, in_col, codes)


def solution(mesh):
    return jax.shard_map(
        local,
        mesh=mesh,
        in_specs=(
            P(None, "circ", "axial"),
            P(None, "circ", "axial"),
            P("circ", "axial"),
            P(AXES, None, None),
            P(AXES, None),
            P(AXES),
            P(AXES),
            P(AXES),
            P(AXES),
        ),
        out_specs=(P(None, "circ", "axial"), P(None, "circ", "axial")),
        check_vma=False,
    )
```

time: 96.5 us -> 81.5 us (0.84)
  blocking collectives: 33.3 us -> 14.1 us
  Pallas kernels: 26.6 us -> 17.3 us
  waiting for transfers between devices: 9.17 us -> 17.7 us
  starting transfers between devices: 22.4 us -> 30.6 us
  local copies, waits for them, and re-layouts: 3.23 us -> 0.02 us
    all_to_all x2 -> x1, blocking collectives: 33.3 us -> 14.1 us  [to_all(): return lax.all_to_all(blocks, AXES, 0, 0, tiled=True).reshape(value.shape)]
    all_to_all x1 -> x2, waiting for transfers between devices: 3.62 us -> 14.6 us  [to_all(): return lax.all_to_all(blocks, AXES, 0, 0, tiled=True).reshape(value.shape)]
    pallas_call x5 -> x8, Pallas kernels: 26.6 us -> 17.3 us  [placed(): run(*(pltpu.with_memory_space_constraint(x, pltpu.VMEM) if spec is HELD e...]
    all_to_all x1 -> x2, starting transfers between devices: 11.5 us -> 19.5 us  [to_all(): return lax.all_to_all(blocks, AXES, 0, 0, tiled=True).reshape(value.shape)]
    unnamed x11 -> x10, local copies, waits for them, and re-layouts: 3.23 us -> 0.02 us
    ppermute x4, waiting for transfers between devices: 5.55 us -> 3.12 us  [shifted(): lax.ppermute(value, axis, [(i, j) for i, j in pairs if 0 <= j < count])]
  transfers between devices with their start and end apart: 5 -> 6, of which waited for: 4 -> 5; matrix products, arithmetic and copies ran while one was open for 0% -> 0% of each run, Pallas kernels for 0% -> 1%
where the time goes in v3:
time: 81.5 us; the launch traced here: 81.2 us
  starting transfers between devices  30.6 us (38%)
  waiting for transfers between devices  17.7 us (22%)
  Pallas kernels  17.3 us (21%)
  blocking collectives  14.1 us (17%)
  between operations  1.47 us (2%)
    all_to_all x2, starting transfers between devices, to_all(): return lax.all_to_all(blocks, AXES, 0, 0, tiled=True).reshape(value.shape)  19.5 us
    pallas_call x8, Pallas kernels, placed(): run(*(pltpu.with_memory_space_constraint(x, pltpu.VMEM) if spec is HELD e...  17.3 us
    all_to_all x2, waiting for transfers between devices, to_all(): return lax.all_to_all(blocks, AXES, 0, 0, tiled=True).reshape(value.shape)  14.6 us
    all_to_all x1, blocking collectives, to_all(): return lax.all_to_all(blocks, AXES, 0, 0, tiled=True).reshape(value.shape)  14.1 us
    ppermute x4, starting transfers between devices, shifted(): lax.ppermute(value, axis, [(i, j) for i, j in pairs if 0 <= j < count])  11.1 us
    ppermute x4, waiting for transfers between devices, shifted(): lax.ppermute(value, axis, [(i, j) for i, j in pairs if 0 <= j < count])  3.12 us
  transfers between devices with their start and end apart: 6, of which 5 were waited for; matrix products, arithmetic and copies ran while one was open for 0% of the time, Pallas kernels for 1%

profile of v3, /device:TPU:1, one launch (start us, length us, event | category | flops | bytes accessed | tf_op | source)
XLA Modules:
  0.0 81.2 jit_solution(8179564357362370603)
XLA Ops:
  0.6 0.0 copy-start.2
  0.6 0.0 copy-start.1
  0.7 0.0 copy-start
  1.4 2.5 %pack.1 = f32[1152,128]{1,0:T(8,128)} custom-call(s32[1]{0:T(128)S(6)} %copy.17.count, s32[8]{0:T(128)} %cells.5, s32[8]{0:T(128)} %partner.1, s32[1,192]{1,0:T(1,128)} %bitcast.18, s32[1,192]{1,0:T(1,128)} %bitcast.19, f32[768,128]{1,0:T(8,128)} %bitcast.17), custom_call_target="tpu_custom_call" | custom-call | tf_op jit(solution)/shard_map/pack/pallas_call | solution.py:70
  3.9 11.5 %all-to-all-start = ((f32[128,1,1152]{2,1,0:T(1,128)}), f32[128,1,1152]{2,1,0:T(1,128)S(1)}, u32[]{:S(2)}, u32[]{:S(2)}) async-start(f32[128,1,1152]{2,1,0:T(1,128)} %bitcast.5), calls=%async_computation | async-start | bytes 1179648 | tf_op jit(solution)/shard_map/all_to_all | solution.py:625
  15.4 0.0 copy-done.2
  15.4 0.0 copy-done.1
  15.4 0.0 copy-done
  15.4 0.3 strips.1
  15.7 0.0 copy-start.3
  15.7 0.0 copy-start.4
  15.7 3.1 %collective-permute-start = (f32[40,128]{1,0:T(8,128)S(1)}, f32[40,128]{1,0:T(8,128)S(1)}, u32[]{:S(2)}, u32[]{:S(2)}) collective-permute-start(f32[40,128]{1,0:T(8,128)S(1)} %get-tuple-element.18), channel_id=1, source_target_pairs={{1,0},{2,1},{3,2},{4,3},{5,4},{6,5},{7,6},{8,7},{9,8},{10,9},{11,1... | collective-permute-start | bytes 61448 | tf_op jit(solution)/shard_map/ppermute | solution.py:612
  18.8 4.4 %collective-permute-start.1 = (f32[40,128]{1,0:T(8,128)S(1)}, f32[40,128]{1,0:T(8,128)S(1)}, u32[]{:S(2)}, u32[]{:S(2)}) collective-permute-start(f32[40,128]{1,0:T(8,128)S(1)} %get-tuple-element.19), channel_id=1, source_target_pairs={{0,1},{1,2},{2,3},{3,4},{4,5},{5,6},{6,7},{7,8},{8,9},{9,10},{10,1... | collective-permute-start | bytes 61448 | tf_op jit(solution)/shard_map/ppermute | solution.py:612
  23.2 0.5 collective-permute-done.from_east
  23.7 0.4 collective-permute-done.1.from_west
  24.1 0.3 sides.1
  24.4 5.1 %all-to-all-done = f32[128,1,1152]{2,1,0:T(1,128)S(1)} async-done(((f32[128,1,1152]{2,1,0:T(1,128)}), f32[128,1,1152]{2,1,0:T(1,128)S(1)}, u32[]{:S(2)}, u32[]{:S(2)}) %all-to-all-start) | async-done | bytes 589856 | tf_op jit(solution)/shard_map/all_to_all | solution.py:625
  29.5 0.5 force.1
  30.0 0.1 collective-permute-start.2
  30.1 3.6 %collective-permute-start.3 = (f32[7,3,8,128]{3,2,1,0:T(8,128)S(1)}, f32[7,3,8,128]{3,2,1,0:T(8,128)S(1)}, u32[]{:S(2)}, u32[]{:S(2)}) collective-permute-start(f32[7,3,8,128]{3,2,1,0:T(8,128)S(1)} %get-tuple-element.21), channel_id=1, source_target_pairs={{0,112},{16,0},{32,16},{48,32},{64,48},{80,64},{96,80},{112,96},{1... | collective-permute-start | bytes 258056 | tf_op jit(solution)/shard_map/ppermute | solution.py:612
  33.7 2.2 %collective-permute-done.2.from_north = f32[7,3,8,128]{3,2,1,0:T(8,128)S(1)} collective-permute-done((f32[7,3,8,128]{3,2,1,0:T(8,128)S(1)}, f32[7,3,8,128]{3,2,1,0:T(8,128)S(1)}, u32[]{:S(2)}, u32[]{:S(2)}) %collective-permute-start.2) | collective-permute-done | bytes 86048 | tf_op jit(solution)/shard_map/ppermute | solution.py:612
  35.9 0.0 collective-permute-done.3.from_south
  35.9 0.0 copy-done.3
  35.9 0.0 copy-done.4
  35.9 2.5 %first_patch.1 = (f32[4,3,144,128]{3,2,1,0:T(8,128)S(1)}, f32[3,3,144,128]{3,2,1,0:T(8,128)S(1)}, f32[3,144,128]{2,1,0:T(8,128)S(1)}, f32[3,144,128]{2,1,0:T(8,128)S(1)}, f32[256,128]{1,0:T(8,128)}) custom-call(s32[8]{0:T(128)S(1)} %copy-done.4, f32[2,128,256]{2,1,0:T(8,128)S(1)} %copy-done, f32[2,128,256]{2,1,0:T(8,128)S(1)} %copy-done.1, ...), custom_call_target="tpu_custom_call" | custom-call | tf_op jit(solution)/shard_map/first_patch/pallas_call | solution.py:70
  38.4 8.0 %all-to-all-start.1 = ((f32[128,1,256]{2,1,0:T(1,128)}), f32[128,1,256]{2,1,0:T(1,128)S(1)}, u32[]{:S(2)}, u32[]{:S(2)}) async-start(f32[128,1,256]{2,1,0:T(1,128)} %bitcast.7), calls=%async_computation.1 | async-start | bytes 262144 | tf_op jit(solution)/shard_map/all_to_all | solution.py:625
  46.4 0.4 tables.1
  46.8 9.5 %all-to-all-done.1 = f32[128,1,256]{2,1,0:T(1,128)S(1)} async-done(((f32[128,1,256]{2,1,0:T(1,128)}), f32[128,1,256]{2,1,0:T(1,128)S(1)}, u32[]{:S(2)}, u32[]{:S(2)}) %all-to-all-start.1) | async-done | bytes 131104 | tf_op jit(solution)/shard_map/all_to_all | solution.py:625
  56.3 5.9 %first_steps.1 = (f32[5,3,144,128]{3,2,1,0:T(8,128)S(1)}, f32[256,128]{1,0:T(8,128)S(1)}) custom-call(s32[8]{0:T(128)S(1)} %copy-done.4, f32[4,3,144,128]{3,2,1,0:T(8,128)S(1)} %get-tuple-element.23.ahead, f32[3,144,128]{2,1,0:T(8,128)S(1)} %get-tuple-element.24.spread, f32[3,144,128]{2,1,0:T(8,128)S(1)} %get-tuple-element.25.pulled, ...), custom_call_target="tpu_custom_call" | custom-call | tf_op jit(solution)/shard_map/first_steps/pallas_call | solution.py:70
  62.2 14.1 %all_to_all.15 = f32[128,1,256]{2,1,0:T(1,128)S(1)} all-to-all(f32[128,1,256]{2,1,0:T(1,128)S(1)} %bitcast.16), channel_id=1, replica_groups=mesh['circ'=8,'axial'=16] {'circ','axial'}, dimensions={0} | all-to-all | bytes 262144 | tf_op jit(solution)/shard_map/all_to_all | solution.py:625
  76.2 5.0 %last_steps.1 = (f32[2,128,256]{2,1,0:T(8,128)}, f32[2,128,256]{2,1,0:T(8,128)}) custom-call(f32[5,3,144,128]{3,2,1,0:T(8,128)S(1)} %get-tuple-element.32.ahead, f32[3,3,144,128]{3,2,1,0:T(8,128)S(1)} %get-tuple-element.26.coef, f32[256,128]{1,0:T(8,128)S(1)} %bitcast.15, f32[24,128]{1,0:T(8,128)S(1)} %get-tuple-element.28.ports, ...), custom_call_target="tpu_custom_call" | custom-call | tf_op jit(solution)/shard_map/last_steps/pallas_call | solution.py:70
Async XLA Ops:
  0.6 14.8 %copy-start.2 = (f32[128,256]{1,0:T(8,128)S(1)}, f32[128,256]{1,0:T(8,128)}, u32[]{:S(2)}) copy-start(f32[128,256]{1,0:T(8,128)} %co.5) | copy-start | bytes 393220
  0.6 14.8 %copy-start.1 = (f32[2,128,256]{2,1,0:T(8,128)S(1)}, f32[2,128,256]{2,1,0:T(8,128)}, u32[]{:S(2)}) copy-start(f32[2,128,256]{2,1,0:T(8,128)} %vo.5) | copy-start | bytes 786436
  0.7 14.8 %copy-start = (f32[2,128,256]{2,1,0:T(8,128)S(1)}, f32[2,128,256]{2,1,0:T(8,128)}, u32[]{:S(2)}) copy-start(f32[2,128,256]{2,1,0:T(8,128)} %ca.5) | copy-start | bytes 786436
  3.9 25.6 %all-to-all-start = ((f32[128,1,1152]{2,1,0:T(1,128)}), f32[128,1,1152]{2,1,0:T(1,128)S(1)}, u32[]{:S(2)}, u32[]{:S(2)}) async-start(f32[128,1,1152]{2,1,0:T(1,128)} %bitcast.5), calls=%async_computation | async-start | bytes 1179648 | tf_op jit(solution)/shard_map/all_to_all | solution.py:625
  15.7 20.2 %copy-start.3 = (s32[8,256]{1,0:T(8,128)S(1)}, s32[8,256]{1,0:T(8,128)}, u32[]{:S(2)}) copy-start(s32[8,256]{1,0:T(8,128)} %constant.2.clone.table) | copy-start | bytes 24580
  15.7 20.2 %copy-start.4 = (s32[8]{0:T(128)S(1)}, s32[8]{0:T(128)}, u32[]{:S(2)}) copy-start(s32[8]{0:T(128)} %cells.5) | copy-start | bytes 100
  15.7 8.0 %collective-permute-start = (f32[40,128]{1,0:T(8,128)S(1)}, f32[40,128]{1,0:T(8,128)S(1)}, u32[]{:S(2)}, u32[]{:S(2)}) collective-permute-start(f32[40,128]{1,0:T(8,128)S(1)} %get-tuple-element.18), channel_id=1, source_target_pairs={{1,0},{2,1},{3,2},{4,3},{5,4},{6,5},{7,6},{8,7},{9,8},{10,9},{11,1... | collective-permute-start | bytes 61448 | tf_op jit(solution)/shard_map/ppermute | solution.py:612
  18.8 5.3 %collective-permute-start.1 = (f32[40,128]{1,0:T(8,128)S(1)}, f32[40,128]{1,0:T(8,128)S(1)}, u32[]{:S(2)}, u32[]{:S(2)}) collective-permute-start(f32[40,128]{1,0:T(8,128)S(1)} %get-tuple-element.19), channel_id=1, source_target_pairs={{0,1},{1,2},{2,3},{3,4},{4,5},{5,6},{6,7},{7,8},{8,9},{9,10},{10,1... | collective-permute-start | bytes 61448 | tf_op jit(solution)/shard_map/ppermute | solution.py:612
  30.0 5.9 %collective-permute-start.2 = (f32[7,3,8,128]{3,2,1,0:T(8,128)S(1)}, f32[7,3,8,128]{3,2,1,0:T(8,128)S(1)}, u32[]{:S(2)}, u32[]{:S(2)}) collective-permute-start(f32[7,3,8,128]{3,2,1,0:T(8,128)S(1)} %get-tuple-element.20), channel_id=1, source_target_pairs={{0,16},{16,32},{32,48},{48,64},{64,80},{80,96},{96,112},{112,0},{1... | collective-permute-start | bytes 258056 | tf_op jit(solution)/shard_map/ppermute | solution.py:612
  30.1 5.8 %collective-permute-start.3 = (f32[7,3,8,128]{3,2,1,0:T(8,128)S(1)}, f32[7,3,8,128]{3,2,1,0:T(8,128)S(1)}, u32[]{:S(2)}, u32[]{:S(2)}) collective-permute-start(f32[7,3,8,128]{3,2,1,0:T(8,128)S(1)} %get-tuple-element.21), channel_id=1, source_target_pairs={{0,112},{16,0},{32,16},{48,32},{64,48},{80,64},{96,80},{112,96},{1... | collective-permute-start | bytes 258056 | tf_op jit(solution)/shard_map/ppermute | solution.py:612
  38.4 17.9 %all-to-all-start.1 = ((f32[128,1,256]{2,1,0:T(1,128)}), f32[128,1,256]{2,1,0:T(1,128)S(1)}, u32[]{:S(2)}, u32[]{:S(2)}) async-start(f32[128,1,256]{2,1,0:T(1,128)} %bitcast.7), calls=%async_computation.1 | async-start | bytes 262144 | tf_op jit(solution)/shard_map/all_to_all | solution.py:625

commit v4 on v3

--- a/solution.py
+++ b/solution.py
@@ -30,6 +30,12 @@
         return []
     span = range(-radius, radius + 1)
     return [(a, b) for a in span for b in span if abs(a) + abs(b) <= radius]
+
+
+def reachable(shift, radius):
+    down = {-17: -1, -16: -1, -15: -1, 15: 1, 16: 1, 17: 1}.get(shift, 0)
+    right = {-17: -1, -1: -1, 15: -1, -15: 1, 1: 1, 17: 1}.get(shift, 0)
+    return [(a, b) for a, b in diamond(radius) if a * down >= abs(down) and b * right >= abs(right)]
 
 
 def patch_plan():
@@ -236,7 +242,7 @@
             out[f, 2] = sides[f, rows, :]
 
 
-def extract(refs, cells, table, tmp, out):
+def extract(fields, cells, table, tmp, out):
     lane = iota((8, LANES), 1)
     long_lane = iota((16, LANES), 1)
     for slot in range(8):
@@ -249,9 +255,11 @@
         other = lax.rem(tile + 1, 3)
         inside = col % LANES
         kept = jnp.zeros((8, LANES), jnp.float32)
-        for f, ref in enumerate(refs):
+        for f, field in enumerate((2, 0, 3, 5, 1, 6, 4)):
             window = jnp.where(
-                long_lane < inside, ref[other, pl.ds(base, 16), :], ref[tile, pl.ds(base, 16), :]
+                long_lane < inside,
+                fields[other, field, pl.ds(base, 16), :],
+                fields[tile, field, pl.ds(base, 16), :],
             )
             window = pltpu.roll(window, turn, 0)[:8]
             window = pltpu.roll(window, (2 * LANES - inside + f * SIDE) % LANES, 1)
@@ -273,11 +281,26 @@
         )
 
 
+class Field:
+    def __init__(self, ref, f):
+        self.ref, self.f = ref, f
+
+    def __getitem__(self, at):
+        return self.ref[(at[0], self.f) + at[1:]]
+
+    def __setitem__(self, at, value):
+        self.ref[(at[0], self.f) + at[1:]] = value
+
+
+def fields_of(ref, count):
+    return [Field(ref, f) for f in range(count)]
+
+
 def build_rows(dst, tiles, north, south):
     for tile in range(3):
-        dst[tile, HALO : HALO + 128, :] = tiles[tile]
-        dst[tile, :HALO, :] = north[tile]
-        dst[tile, HALO + 128 :, :] = south[tile]
+        dst[tile, slice(HALO, HALO + 128), :] = tiles[tile]
+        dst[tile, slice(0, HALO), :] = north[tile]
+        dst[tile, slice(HALO + 128, EXT), :] = south[tile]
 
 
 def rows_at(j):
@@ -314,43 +337,32 @@
 
 def first_patch_kernel(
     cells, ca, vo, co, sides, from_north, from_south, force, table,
-    ahead, coef, spread, pulled, out, start, tmp,
+    ahead, coef, out, start, tmp,
 ):
+    after = fields_of(ahead, 7)
+    before = fields_of(start, 5)
     for f, ref in enumerate(all_fields(ca, vo, co)):
         scale = 0.05 if f == 4 else 1.0
         build_rows(
-            start.at[f] if f < 4 else spread,
+            before[f] if f < 4 else after[5],
             [t * scale for t in (ref[:, :LANES], ref[:, LANES:], sides[f])],
             from_north[f] * scale,
             from_south[f] * scale,
         )
     for f in range(2):
         build_rows(
-            pulled if f == 0 else start.at[4],
+            after[6] if f == 0 else before[4],
             [force[f, tile] for tile in range(3)],
             from_north[5 + f],
             from_south[5 + f],
         )
-    for f, ref in enumerate((spread, pulled, start.at[4])):
-        to_mixed(ref, coef.at[f])
-    one_step(
-        [start.at[f] for f in range(4)],
-        rows_at,
-        [ahead.at[f] for f in range(4)],
-        rows_at,
-        coef_refs(coef),
-        None,
-    )
-    take_patches(ahead, spread, pulled, start.at[2], cells, table, tmp, out)
-
-
-def coef_refs(coef):
-    return [coef.at[f] for f in range(3)]
-
-
-def take_patches(after, spread, a_s, before_v, cells, table, tmp, out):
-    refs = [after.at[2], after.at[0], after.at[3], spread, after.at[1], a_s, before_v]
-    extract(refs, cells, table, tmp, out)
+    for tile in range(3):
+        ahead[tile, 4] = start[tile, 2]
+    coefs = fields_of(coef, 3)
+    for src, dst in zip((after[5], after[6], before[4]), coefs):
+        to_mixed(src, dst)
+    one_step(before[:4], rows_at, after[:4], rows_at, coefs, None)
+    extract(ahead, cells, table, tmp, out)
 
 
 def port_places(ports):
@@ -382,14 +394,15 @@
 
     def add_gain(f, gain, reach):
         added = dict(f)
-        index = 0
         for k in range(8):
             turned = pltpu.roll(gain, k, 0) if k else gain
-            for shift in NEAR_LANES:
+            for place, shift in enumerate(NEAR_LANES):
+                cells = reachable(shift, reach)
+                if not cells:
+                    continue
                 moved = pltpu.roll(turned, (-shift) % LANES, 1) if shift else turned
-                code = codes[index]
-                index += 1
-                for c in diamond(reach):
+                code = codes[k * len(NEAR_LANES) + place]
+                for c in cells:
                     key = (c[0] * ROW_KEY + c[1]) & KEY_MASK
                     added[c] = added[c] + jnp.where(code == key, moved, 0.0)
         return added
@@ -486,10 +499,18 @@
 
 def injections(gains, in_row, in_col, inject):
     pick = in_row[...].astype(jnp.bfloat16)
-    zero = jnp.zeros((256 - 3 * NEAR_PORTS, WIDE), jnp.bfloat16)
+    lane_of = lax.axis_index("circ") * 16 + lax.axis_index("axial")
+    zero = jnp.zeros((NEAR_PORTS - 8 * len(NEAR_LANES), WIDE), jnp.float32)
+    blank = jnp.zeros((256 - 3 * NEAR_PORTS, WIDE), jnp.bfloat16)
     for k, gain in enumerate(gains):
-        parts = three_parts(in_col[...] * my_column(gain))
-        total = dot(pick, jnp.concatenate(list(parts) + [zero], axis=0))
+        lines = []
+        for place, shift in enumerate(NEAR_LANES):
+            at = jnp.zeros((8, LANES), jnp.int32) + ((lane_of + shift) & (LANES - 1))
+            mine = jnp.take_along_axis(gain, at, axis=1)
+            rows = slice(place * 8, place * 8 + 8)
+            lines.append(in_col[rows, :] * jnp.concatenate([mine] * 3, axis=1))
+        parts = three_parts(jnp.concatenate(lines + [zero], axis=0))
+        total = dot(pick, jnp.concatenate(list(parts) + [blank], axis=0))
         for tile in range(3):
             inject[k, tile] = total[:, tile * LANES : (tile + 1) * LANES]
 
@@ -548,60 +569,48 @@
             later[3][tile, later_at(j), :] = u_step(parts, v, u, n[3], spread)
 
 
-def coupled_steps(ahead, coef, got, ports, in_row, in_col, codes, state, inject):
+def coupled_steps(ahead, coef, got, ports, in_row, in_col, codes, first, second, inject):
     rows, cols, partner = port_places(ports)
     gains = port_sim(got, codes, rows, cols, partner)
     injections(gains, in_row, in_col, inject)
+    one, two = fields_of(first, 4), fields_of(second, 4)
     for f in range(4):
-        to_mixed(ahead.at[f], state.at[0, f])
-    state[0, 2] = state[0, 2] + inject[0]
-
-    def one(k, carry):
-        now = lax.rem(k, 2)
-        one_step(
-            [state.at[now, f] for f in range(4)],
-            mixed_at,
-            [state.at[1 - now, f] for f in range(4)],
-            mixed_at,
-            coef,
-            inject.at[k + 1],
-        )
-        return carry
-
-    lax.fori_loop(0, 3, one, 0)
+        for tile in range(3):
+            for j in range(STEP):
+                value = ahead[tile, f, rows_at(j), :]
+                if f == 2:
+                    value = value + inject[0, tile, mixed_at(j), :]
+                first[tile, f, mixed_at(j), :] = value
+    coefs = fields_of(coef, 3)
+    for k, (now, later) in enumerate(((one, two), (two, one), (one, two))):
+        one_step(now, mixed_at, later, mixed_at, coefs, inject.at[k + 1])
+    return two
 
 
 def first_steps_kernel(
-    cells, ahead, spread, pulled, coef, got, ports, in_row, in_col, codes, table,
-    later, out, state, inject, tmp,
+    cells, ahead, coef, got, ports, in_row, in_col, codes, table,
+    later, out, first, second, inject, tmp,
 ):
-    coefs = coef_refs(coef)
-    coupled_steps(ahead, coefs, got, ports, in_row, in_col, codes, state, inject)
+    now = coupled_steps(ahead, coef, got, ports, in_row, in_col, codes, first, second, inject)
     for tile in range(3):
         for j in range(STEP):
-            later[4, tile, rows_at(j), :] = state[1, 2, tile, mixed_at(j), :]
-    one_step(
-        [state.at[1, f] for f in range(4)],
-        mixed_at,
-        [later.at[f] for f in range(4)],
-        rows_at,
-        coefs,
-        None,
-    )
-    take_patches(later, spread, pulled, later.at[4], cells, table, tmp, out)
+            later[tile, 4, rows_at(j), :] = second[tile, 2, mixed_at(j), :]
+        later[tile, 5] = ahead[tile, 5]
+        later[tile, 6] = ahead[tile, 6]
+    one_step(now, mixed_at, fields_of(later, 4), rows_at, fields_of(coef, 3), None)
+    extract(later, cells, table, tmp, out)
 
 
 def last_steps_kernel(
-    ahead, coef, got, ports, in_row, in_col, codes, ca_out, vo_out, state, inject
+    ahead, coef, got, ports, in_row, in_col, codes, ca_out, vo_out, first, second, inject
 ):
-    coefs = coef_refs(coef)
-    coupled_steps(ahead, coefs, got, ports, in_row, in_col, codes, state, inject)
+    coupled_steps(ahead, coef, got, ports, in_row, in_col, codes, first, second, inject)
     for f in range(4):
         out = (ca_out, vo_out)[f // 2].at[f % 2]
         for tile in range(2):
             for j in range(STEP):
-                state[0, f, tile, rows_at(j), :] = state[1, f, tile, mixed_at(j), :]
-            out[:, tile * LANES : (tile + 1) * LANES] = state[0, f, tile, HALO : HALO + 128, :]
+                first[tile, f, rows_at(j), :] = second[tile, f, mixed_at(j), :]
+            out[:, tile * LANES : (tile + 1) * LANES] = first[tile, f, HALO : HALO + 128, :]
 
 
 def shifted(value, axis, step, periodic):
@@ -620,6 +629,10 @@
     return shifted(to_south, "circ", 1, True), shifted(to_north, "circ", -1, True)
 
 
+def stack(count):
+    return (3, count, EXT, LANES)
+
+
 def to_all(value):
     blocks = value.reshape(128, 1, -1)
     return lax.all_to_all(blocks, AXES, 0, 0, tiled=True).reshape(value.shape)
@@ -627,7 +640,6 @@
 
 def local(ca, vo, co, fluid, target, row, count, cells, partner):
     table = jnp.asarray(patch_table())
-    field = (3, EXT, LANES)
     lines = fluid.reshape(-1, 2, 2, LANES).transpose(0, 2, 1, 3).reshape(-1, LANES)
     (packed,) = call(pack_kernel, [(128 * BLOCK, LANES)], [SMEM] * 3 + [VMEM] * 3, "pack", room=60)(
         count, cells, partner, target.reshape(1, -1), row.reshape(1, -1), lines
@@ -651,22 +663,22 @@
         last=jnp.int32,
     )(ports)
     patch_space = pltpu.VMEM((64, LANES), jnp.float32)
-    ahead, coef, spread, pulled, patches = call(
+    ahead, coef, patches = call(
         first_patch_kernel,
-        [(4, *field), (3, *field), field, field, (256, LANES)],
+        [stack(7), stack(3), (256, LANES)],
         [SMEM] + [HELD] * 8,
         "first_patch",
-        [pltpu.VMEM((5, *field), jnp.float32), patch_space],
+        [pltpu.VMEM(stack(5), jnp.float32), patch_space],
     )(cells, ca, vo, co, sides, from_north, from_south, force, table)
     got = to_all(patches)
-    scratch = [pltpu.VMEM((2, 4, *field), jnp.float32), pltpu.VMEM((4, *field), jnp.float32)]
+    scratch = [pltpu.VMEM(stack(4), jnp.float32)] * 2 + [pltpu.VMEM((4, 3, EXT, LANES), jnp.float32)]
     ahead, patches = call(
         first_steps_kernel,
-        [(5, *field), (256, LANES)],
-        [SMEM] + [HELD] * 10,
+        [stack(7), (256, LANES)],
+        [SMEM] + [HELD] * 8,
         "first_steps",
         scratch + [patch_space],
-    )(cells, ahead, spread, pulled, coef, got, ports, in_row, in_col, codes, table)
+    )(cells, ahead, coef, got, ports, in_row, in_col, codes, table)
     got = to_all(patches)
     return call(
         last_steps_kernel,

time: 81.5 us -> 77.9 us (0.956)
  Pallas kernels: 17.3 us -> 13.8 us
    pallas_call x8, Pallas kernels: 17.3 us -> 13.8 us  [placed(): run(*(pltpu.with_memory_space_constraint(x, pltpu.VMEM) if spec is HELD e...]
where the time goes in v4:
time: 77.9 us; the launch traced here: 77.6 us
  starting transfers between devices  30.4 us (39%)
  waiting for transfers between devices  17.9 us (23%)
  blocking collectives  14 us (18%)
  Pallas kernels  13.8 us (18%)
  between operations  1.48 us (2%)
    all_to_all x2, starting transfers between devices, to_all(): return lax.all_to_all(blocks, AXES, 0, 0, tiled=True).reshape(value.shape)  19.4 us
    all_to_all x2, waiting for transfers between devices, to_all(): return lax.all_to_all(blocks, AXES, 0, 0, tiled=True).reshape(value.shape)  14.7 us
    all_to_all x1, blocking collectives, to_all(): return lax.all_to_all(blocks, AXES, 0, 0, tiled=True).reshape(value.shape)  14 us
    pallas_call x8, Pallas kernels, placed(): run(*(pltpu.with_memory_space_constraint(x, pltpu.VMEM) if spec is HELD e...  13.8 us
    ppermute x4, starting transfers between devices, shifted(): lax.ppermute(value, axis, [(i, j) for i, j in pairs if 0 <= j < count])  11 us
    ppermute x4, waiting for transfers between devices, shifted(): lax.ppermute(value, axis, [(i, j) for i, j in pairs if 0 <= j < count])  3.12 us
  transfers between devices with their start and end apart: 6, of which 5 were waited for; matrix products, arithmetic and copies ran while one was open for 0% of the time, Pallas kernels for 1%

profile of v4, /device:TPU:1, one launch (start us, length us, event | category | flops | bytes accessed | tf_op | source)
XLA Modules:
  0.0 77.6 jit_solution(14576625787317944155)
XLA Ops:
  0.6 0.0 copy-start.2
  0.6 0.0 copy-start.1
  0.7 0.0 copy-start
  1.4 2.5 %pack.1 = f32[1152,128]{1,0:T(8,128)} custom-call(s32[1]{0:T(128)S(6)} %copy.17.count, s32[8]{0:T(128)} %cells.5, s32[8]{0:T(128)} %partner.1, s32[1,192]{1,0:T(1,128)} %bitcast.18, s32[1,192]{1,0:T(1,128)} %bitcast.19, f32[768,128]{1,0:T(8,128)} %bitcast.17), custom_call_target="tpu_custom_call" | custom-call | tf_op jit(solution)/shard_map/pack/pallas_call | solution.py:76
  3.9 11.5 %all-to-all-start = ((f32[128,1,1152]{2,1,0:T(1,128)}), f32[128,1,1152]{2,1,0:T(1,128)S(1)}, u32[]{:S(2)}, u32[]{:S(2)}) async-start(f32[128,1,1152]{2,1,0:T(1,128)} %bitcast.5), calls=%async_computation | async-start | bytes 1179648 | tf_op jit(solution)/shard_map/all_to_all | solution.py:638
  15.4 0.0 copy-done.2
  15.4 0.0 copy-done.1
  15.4 0.0 copy-done
  15.4 0.0 copy-start.3
  15.4 0.0 copy-start.4
  15.4 0.3 strips.1
  15.7 3.0 %collective-permute-start = (f32[40,128]{1,0:T(8,128)S(1)}, f32[40,128]{1,0:T(8,128)S(1)}, u32[]{:S(2)}, u32[]{:S(2)}) collective-permute-start(f32[40,128]{1,0:T(8,128)S(1)} %get-tuple-element.16), channel_id=1, source_target_pairs={{1,0},{2,1},{3,2},{4,3},{5,4},{6,5},{7,6},{8,7},{9,8},{10,9},{11,1... | collective-permute-start | bytes 61448 | tf_op jit(solution)/shard_map/ppermute | solution.py:621
  18.7 4.4 %collective-permute-start.1 = (f32[40,128]{1,0:T(8,128)S(1)}, f32[40,128]{1,0:T(8,128)S(1)}, u32[]{:S(2)}, u32[]{:S(2)}) collective-permute-start(f32[40,128]{1,0:T(8,128)S(1)} %get-tuple-element.17), channel_id=1, source_target_pairs={{0,1},{1,2},{2,3},{3,4},{4,5},{5,6},{6,7},{7,8},{8,9},{9,10},{10,1... | collective-permute-start | bytes 61448 | tf_op jit(solution)/shard_map/ppermute | solution.py:621
  23.1 0.6 collective-permute-done.from_east
  23.7 0.3 collective-permute-done.1.from_west
  24.0 0.3 sides.1
  24.3 5.3 %all-to-all-done = f32[128,1,1152]{2,1,0:T(1,128)S(1)} async-done(((f32[128,1,1152]{2,1,0:T(1,128)}), f32[128,1,1152]{2,1,0:T(1,128)S(1)}, u32[]{:S(2)}, u32[]{:S(2)}) %all-to-all-start) | async-done | bytes 589856 | tf_op jit(solution)/shard_map/all_to_all | solution.py:638
  29.5 0.5 force.1
  30.0 0.1 collective-permute-start.2
  30.1 3.6 %collective-permute-start.3 = (f32[7,3,8,128]{3,2,1,0:T(8,128)S(1)}, f32[7,3,8,128]{3,2,1,0:T(8,128)S(1)}, u32[]{:S(2)}, u32[]{:S(2)}) collective-permute-start(f32[7,3,8,128]{3,2,1,0:T(8,128)S(1)} %get-tuple-element.19), channel_id=1, source_target_pairs={{0,112},{16,0},{32,16},{48,32},{64,48},{80,64},{96,80},{112,96},{1... | collective-permute-start | bytes 258056 | tf_op jit(solution)/shard_map/ppermute | solution.py:621
  33.7 2.2 %collective-permute-done.2.from_north = f32[7,3,8,128]{3,2,1,0:T(8,128)S(1)} collective-permute-done((f32[7,3,8,128]{3,2,1,0:T(8,128)S(1)}, f32[7,3,8,128]{3,2,1,0:T(8,128)S(1)}, u32[]{:S(2)}, u32[]{:S(2)}) %collective-permute-start.2) | collective-permute-done | bytes 86048 | tf_op jit(solution)/shard_map/ppermute | solution.py:621
  35.9 0.0 collective-permute-done.3.from_south
  35.9 0.0 copy-done.3
  35.9 0.0 copy-done.4
  35.9 2.5 %first_patch.1 = (f32[3,7,144,128]{3,2,1,0:T(8,128)S(1)}, f32[3,3,144,128]{3,2,1,0:T(8,128)S(1)}, f32[256,128]{1,0:T(8,128)}) custom-call(s32[8]{0:T(128)S(1)} %copy-done.4, f32[2,128,256]{2,1,0:T(8,128)S(1)} %copy-done, f32[2,128,256]{2,1,0:T(8,128)S(1)} %copy-done.1, f32[128,256]{1,0:T(8,128)S(1)} %copy-done.2, f32[5,128,128]{2,1,0:T(8,128)S(1)} %sides.1, ...), custom_call_target="tpu_custom_call" | custom-call | tf_op jit(solution)/shard_map/first_patch/pallas_call | solution.py:76
  38.4 7.9 %all-to-all-start.1 = ((f32[128,1,256]{2,1,0:T(1,128)}), f32[128,1,256]{2,1,0:T(1,128)S(1)}, u32[]{:S(2)}, u32[]{:S(2)}) async-start(f32[128,1,256]{2,1,0:T(1,128)} %bitcast.7), calls=%async_computation.1 | async-start | bytes 262144 | tf_op jit(solution)/shard_map/all_to_all | solution.py:638
  46.3 0.4 tables.1
  46.7 9.5 %all-to-all-done.1 = f32[128,1,256]{2,1,0:T(1,128)S(1)} async-done(((f32[128,1,256]{2,1,0:T(1,128)}), f32[128,1,256]{2,1,0:T(1,128)S(1)}, u32[]{:S(2)}, u32[]{:S(2)}) %all-to-all-start.1) | async-done | bytes 131104 | tf_op jit(solution)/shard_map/all_to_all | solution.py:638
  56.2 4.2 %first_steps.1 = (f32[3,7,144,128]{3,2,1,0:T(8,128)S(1)}, f32[256,128]{1,0:T(8,128)S(1)}) custom-call(s32[8]{0:T(128)S(1)} %copy-done.4, f32[3,7,144,128]{3,2,1,0:T(8,128)S(1)} %get-tuple-element.21.ahead, f32[3,3,144,128]{3,2,1,0:T(8,128)S(1)} %get-tuple-element.22.coef, f32[256,128]{1,0:T(8,128)S(1)} %bitcast.14, f32[24,128]{1,0:T(8,128)S(1)} %get-tuple-element.24.ports, ...), custom_call_target="tpu_custom_call" | custom-call | tf_op jit(solution)/shard_map/first_steps/pallas_call | solution.py:76
  60.4 14.0 %all_to_all.15 = f32[128,1,256]{2,1,0:T(1,128)S(1)} all-to-all(f32[128,1,256]{2,1,0:T(1,128)S(1)} %bitcast.16), channel_id=1, replica_groups=mesh['circ'=8,'axial'=16] {'circ','axial'}, dimensions={0} | all-to-all | bytes 262144 | tf_op jit(solution)/shard_map/all_to_all | solution.py:638
  74.4 3.1 %last_steps.1 = (f32[2,128,256]{2,1,0:T(8,128)}, f32[2,128,256]{2,1,0:T(8,128)}) custom-call(f32[3,7,144,128]{3,2,1,0:T(8,128)S(1)} %get-tuple-element.28.ahead, f32[3,3,144,128]{3,2,1,0:T(8,128)S(1)} %get-tuple-element.22.coef, f32[256,128]{1,0:T(8,128)S(1)} %bitcast.15, f32[24,128]{1,0:T(8,128)S(1)} %get-tuple-element.24.ports, ...), custom_call_target="tpu_custom_call" | custom-call | tf_op jit(solution)/shard_map/last_steps/pallas_call | solution.py:76
Async XLA Ops:
  0.6 14.8 %copy-start.2 = (f32[128,256]{1,0:T(8,128)S(1)}, f32[128,256]{1,0:T(8,128)}, u32[]{:S(2)}) copy-start(f32[128,256]{1,0:T(8,128)} %co.5) | copy-start | bytes 393220
  0.6 14.8 %copy-start.1 = (f32[2,128,256]{2,1,0:T(8,128)S(1)}, f32[2,128,256]{2,1,0:T(8,128)}, u32[]{:S(2)}) copy-start(f32[2,128,256]{2,1,0:T(8,128)} %vo.5) | copy-start | bytes 786436
  0.7 14.8 %copy-start = (f32[2,128,256]{2,1,0:T(8,128)S(1)}, f32[2,128,256]{2,1,0:T(8,128)}, u32[]{:S(2)}) copy-start(f32[2,128,256]{2,1,0:T(8,128)} %ca.5) | copy-start | bytes 786436
  3.9 25.6 %all-to-all-start = ((f32[128,1,1152]{2,1,0:T(1,128)}), f32[128,1,1152]{2,1,0:T(1,128)S(1)}, u32[]{:S(2)}, u32[]{:S(2)}) async-start(f32[128,1,1152]{2,1,0:T(1,128)} %bitcast.5), calls=%async_computation | async-start | bytes 1179648 | tf_op jit(solution)/shard_map/all_to_all | solution.py:638
  15.4 20.5 %copy-start.3 = (s32[8,256]{1,0:T(8,128)S(1)}, s32[8,256]{1,0:T(8,128)}, u32[]{:S(2)}) copy-start(s32[8,256]{1,0:T(8,128)} %constant.2.clone.table) | copy-start | bytes 24580
  15.4 20.5 %copy-start.4 = (s32[8]{0:T(128)S(1)}, s32[8]{0:T(128)}, u32[]{:S(2)}) copy-start(s32[8]{0:T(128)} %cells.5) | copy-start | bytes 100
  15.7 8.0 %collective-permute-start = (f32[40,128]{1,0:T(8,128)S(1)}, f32[40,128]{1,0:T(8,128)S(1)}, u32[]{:S(2)}, u32[]{:S(2)}) collective-permute-start(f32[40,128]{1,0:T(8,128)S(1)} %get-tuple-element.16), channel_id=1, source_target_pairs={{1,0},{2,1},{3,2},{4,3},{5,4},{6,5},{7,6},{8,7},{9,8},{10,9},{11,1... | collective-permute-start | bytes 61448 | tf_op jit(solution)/shard_map/ppermute | solution.py:621
  18.7 5.3 %collective-permute-start.1 = (f32[40,128]{1,0:T(8,128)S(1)}, f32[40,128]{1,0:T(8,128)S(1)}, u32[]{:S(2)}, u32[]{:S(2)}) collective-permute-start(f32[40,128]{1,0:T(8,128)S(1)} %get-tuple-element.17), channel_id=1, source_target_pairs={{0,1},{1,2},{2,3},{3,4},{4,5},{5,6},{6,7},{7,8},{8,9},{9,10},{10,1... | collective-permute-start | bytes 61448 | tf_op jit(solution)/shard_map/ppermute | solution.py:621
  30.0 5.9 %collective-permute-start.2 = (f32[7,3,8,128]{3,2,1,0:T(8,128)S(1)}, f32[7,3,8,128]{3,2,1,0:T(8,128)S(1)}, u32[]{:S(2)}, u32[]{:S(2)}) collective-permute-start(f32[7,3,8,128]{3,2,1,0:T(8,128)S(1)} %get-tuple-element.18), channel_id=1, source_target_pairs={{0,16},{16,32},{32,48},{48,64},{64,80},{80,96},{96,112},{112,0},{1... | collective-permute-start | bytes 258056 | tf_op jit(solution)/shard_map/ppermute | solution.py:621
  30.1 5.8 %collective-permute-start.3 = (f32[7,3,8,128]{3,2,1,0:T(8,128)S(1)}, f32[7,3,8,128]{3,2,1,0:T(8,128)S(1)}, u32[]{:S(2)}, u32[]{:S(2)}) collective-permute-start(f32[7,3,8,128]{3,2,1,0:T(8,128)S(1)} %get-tuple-element.19), channel_id=1, source_target_pairs={{0,112},{16,0},{32,16},{48,32},{64,48},{80,64},{96,80},{112,96},{1... | collective-permute-start | bytes 258056 | tf_op jit(solution)/shard_map/ppermute | solution.py:621
  38.4 17.8 %all-to-all-start.1 = ((f32[128,1,256]{2,1,0:T(1,128)}), f32[128,1,256]{2,1,0:T(1,128)S(1)}, u32[]{:S(2)}, u32[]{:S(2)}) async-start(f32[128,1,256]{2,1,0:T(1,128)} %bitcast.7), calls=%async_computation.1 | async-start | bytes 262144 | tf_op jit(solution)/shard_map/all_to_all | solution.py:638

commit v5 on v4

--- a/solution.py
+++ b/solution.py
@@ -156,7 +156,9 @@
     order = iota((1, slots), 1)
     used = order < count[0]
     eye = iota((slots, slots), 0) == iota((slots, slots), 1)
-    t_col = jnp.sum(jnp.where(eye, t_row, 0), axis=1, keepdims=True)
+    both = jnp.sum(jnp.where(eye, t_row * 256 + row[...], 0), axis=1, keepdims=True)
+    t_col = lax.shift_right_logical(both, 8)
+    row_col = ((both & 255) + 1).astype(jnp.float32).astype(jnp.bfloat16)
     earlier = (
         (t_col == t_row)
         & (iota((slots, slots), 0) < count[0])
@@ -165,7 +167,7 @@
     rank = jnp.sum(jnp.where(earlier, 1, 0), axis=0, keepdims=True)
     place = jnp.where(used, rank * 128 + t_row, -1)
     pick = iota((256, slots), 0) == place
-    tags = jnp.sum(jnp.where(pick, row[...] + 1, 0), axis=1, keepdims=True).astype(jnp.float32)
+    tags = dot(one_hot(pick), jnp.broadcast_to(row_col, (slots, LANES)))
     tags0, tags1 = tags[:128], tags[128:]
     tiles = [fluid[pl.ds(c * 2 + k, slots, stride=4), :] for k in range(2) for c in range(2)]
     moved = exact_pick(pick, jnp.concatenate(tiles, axis=1))
@@ -217,6 +219,7 @@
     both = jnp.concatenate(three_parts(both), axis=1)
     east, west = dot(one_hot(pair(2)), both), dot(one_hot(pair(4)), both)
     east, west = [x[:, 256:] + x[:, 128:256] + x[:, :128] for x in (east, west)]
+    coefs = []
     for tile in range(3):
         if tile < 2:
             shear = total[:, tile * LANES : (tile + 1) * LANES]
@@ -231,38 +234,55 @@
         stimulus = 0.5 + 0.5 * jnp.tanh(0.5 * agonist)
         a_s = 0.1 * stimulus
         a_e = 0.02 + 0.15 * stress + 0.04 * stimulus
-        for f, value in enumerate((a_s, a_e)):
-            force[f, tile] = value
-            to_north[5 + f, tile] = value[:HALO]
-            to_south[5 + f, tile] = value[128 - HALO :]
-    for f, ref in enumerate(all_fields(ca, vo, co)):
-        for rows, out in ((slice(0, HALO), to_north), (slice(128 - HALO, 128), to_south)):
-            out[f, 0] = ref[rows, :LANES]
-            out[f, 1] = ref[rows, LANES:]
-            out[f, 2] = sides[f, rows, :]
+        coefs.append((a_s, a_e))
+        for f in range(2):
+            force[f, tile] = coefs[tile][f]
+    refs = all_fields(ca, vo, co)
+    for rows, out in ((slice(0, HALO), to_north), (slice(128 - HALO, 128), to_south)):
+        ends = jnp.zeros((HALO, LANES), jnp.float32)
+        for f in range(7):
+            for tile in range(2):
+                out[2 * f + tile] = (
+                    refs[f][rows, tile * LANES : (tile + 1) * LANES]
+                    if f < 5
+                    else coefs[tile][f - 5][rows]
+                )
+            side = sides[f, rows, :] if f < 5 else coefs[2][f - 5][rows]
+            ends = ends + lanes_to(side, 0, f * 16, HALO)
+            ends = ends + lanes_to(side, LANES - HALO, f * 16 + HALO, HALO)
+        out[14] = ends
+
+
+def strip_tiles(strip, f):
+    ends = strip[14]
+    side = lanes_to(ends, f * 16, 0, HALO) + lanes_to(ends, f * 16 + HALO, LANES - HALO, HALO)
+    return [strip[2 * f], strip[2 * f + 1], side]
 
 
 def extract(fields, cells, table, tmp, out):
     lane = iota((8, LANES), 1)
     long_lane = iota((16, LANES), 1)
+    flat = fields.reshape(3 * 7 * EXT, LANES)
     for slot in range(8):
         cell = cells[slot]
-        row = cell // 256 + HALO - RADIUS
-        col = lax.rem(cell % 256 - RADIUS + WIDE, WIDE)
-        base = pl.multiple_of(row // 8 * 8, 8)
-        turn = 16 - (row - base)
-        tile = col // LANES
-        other = lax.rem(tile + 1, 3)
-        inside = col % LANES
+        row = lax.shift_right_logical(cell, 8) + (HALO - RADIUS)
+        col = (cell & 255) - RADIUS
+        col = jnp.where(col < 0, col + WIDE, col)
+        base = pl.multiple_of(row & -8, 8)
+        turn = 16 - (row & 7)
+        tile = lax.shift_right_logical(col, 7)
+        other = jnp.where(tile == 2, 0, tile + 1)
+        inside = col & (LANES - 1)
         kept = jnp.zeros((8, LANES), jnp.float32)
+        span = 6 * EXT + 16
+        here = flat.at[pl.ds(pl.multiple_of(tile * (7 * EXT) + base, 8), span), :]
+        there = flat.at[pl.ds(pl.multiple_of(other * (7 * EXT) + base, 8), span), :]
+        back = (LANES - inside) & (LANES - 1)
         for f, field in enumerate((2, 0, 3, 5, 1, 6, 4)):
-            window = jnp.where(
-                long_lane < inside,
-                fields[other, field, pl.ds(base, 16), :],
-                fields[tile, field, pl.ds(base, 16), :],
-            )
-            window = pltpu.roll(window, turn, 0)[:8]
-            window = pltpu.roll(window, (2 * LANES - inside + f * SIDE) % LANES, 1)
+            rows = slice(field * EXT, field * EXT + 16)
+            window = jnp.where(long_lane < inside, there[rows, :], here[rows, :])
+            window = pltpu.roll(pltpu.roll(window, turn, 0)[:8], back, 1)
+            window = pltpu.roll(window, f * SIDE, 1) if f else window
             kept = jnp.where((lane >= f * SIDE) & (lane < (f + 1) * SIDE), window, kept)
         tmp[slot * 8 : slot * 8 + 8, :] = kept
     width = 2 * LANES
@@ -346,15 +366,15 @@
         build_rows(
             before[f] if f < 4 else after[5],
             [t * scale for t in (ref[:, :LANES], ref[:, LANES:], sides[f])],
-            from_north[f] * scale,
-            from_south[f] * scale,
+            [t * scale for t in strip_tiles(from_north, f)],
+            [t * scale for t in strip_tiles(from_south, f)],
         )
     for f in range(2):
         build_rows(
             after[6] if f == 0 else before[4],
             [force[f, tile] for tile in range(3)],
-            from_north[5 + f],
-            from_south[5 + f],
+            strip_tiles(from_north, 5 + f),
+            strip_tiles(from_south, 5 + f),
         )
     for tile in range(3):
         ahead[tile, 4] = start[tile, 2]
@@ -650,7 +670,7 @@
     )
     from_east, from_west = swap_axial(to_west, to_east)
     (sides,) = call(sides_kernel, [(5, 128, LANES)], [HELD] * 2, "sides")(from_east, from_west)
-    ring = (7, 3, HALO, LANES)
+    ring = (15, HALO, LANES)
     force, ports, to_north, to_south = call(
         force_kernel, [(2, 3, 128, LANES), (24, LANES), ring, ring], [HELD] * 5, "force"
     )(received, ca, vo, co, sides)

time: 77.9 us -> 77.6 us (level)
  no operation moved by 1% of the time
where the time goes in v5:
time: 77.6 us; the launch traced here: 77.3 us
  starting transfers between devices  30.8 us (40%)
  waiting for transfers between devices  17.2 us (22%)
  blocking collectives  14 us (18%)
  Pallas kernels  13.8 us (18%)
  between operations  1.48 us (2%)
    all_to_all x2, starting transfers between devices, to_all(): return lax.all_to_all(blocks, AXES, 0, 0, tiled=True).reshape(value.shape)  19.8 us
    all_to_all x2, waiting for transfers between devices, to_all(): return lax.all_to_all(blocks, AXES, 0, 0, tiled=True).reshape(value.shape)  14.7 us
    all_to_all x1, blocking collectives, to_all(): return lax.all_to_all(blocks, AXES, 0, 0, tiled=True).reshape(value.shape)  14 us
    pallas_call x8, Pallas kernels, placed(): run(*(pltpu.with_memory_space_constraint(x, pltpu.VMEM) if spec is HELD e...  13.8 us
    ppermute x4, starting transfers between devices, shifted(): lax.ppermute(value, axis, [(i, j) for i, j in pairs if 0 <= j < count])  11 us
    ppermute x4, waiting for transfers between devices, shifted(): lax.ppermute(value, axis, [(i, j) for i, j in pairs if 0 <= j < count])  2.49 us
  transfers between devices with their start and end apart: 6, of which 5 were waited for; matrix products, arithmetic and copies ran while one was open for 0% of the time, Pallas kernels for 1%

profile of v5, /device:TPU:1, one launch (start us, length us, event | category | flops | bytes accessed | tf_op | source)
XLA Modules:
  0.0 77.3 jit_solution(13255273766222553664)
XLA Ops:
  0.6 0.0 copy-start.2
  0.6 0.0 copy-start.1
  0.7 0.0 copy-start
  1.4 2.6 %pack.1 = f32[1152,128]{1,0:T(8,128)} custom-call(s32[1]{0:T(128)S(6)} %copy.17.count, s32[8]{0:T(128)} %cells.5, s32[8]{0:T(128)} %partner.1, s32[1,192]{1,0:T(1,128)} %bitcast.18, s32[1,192]{1,0:T(1,128)} %bitcast.19, f32[768,128]{1,0:T(8,128)} %bitcast.17), custom_call_target="tpu_custom_call" | custom-call | tf_op jit(solution)/shard_map/pack/pallas_call | solution.py:76
  4.0 11.5 %all-to-all-start = ((f32[128,1,1152]{2,1,0:T(1,128)}), f32[128,1,1152]{2,1,0:T(1,128)S(1)}, u32[]{:S(2)}, u32[]{:S(2)}) async-start(f32[128,1,1152]{2,1,0:T(1,128)} %bitcast.5), calls=%async_computation | async-start | bytes 1179648 | tf_op jit(solution)/shard_map/all_to_all | solution.py:658
  15.5 0.0 copy-done.2
  15.5 0.0 copy-done.1
  15.5 0.0 copy-done
  15.5 0.0 copy-start.3
  15.5 0.0 copy-start.4
  15.5 0.3 strips.1
  15.8 3.0 %collective-permute-start = (f32[40,128]{1,0:T(8,128)S(1)}, f32[40,128]{1,0:T(8,128)S(1)}, u32[]{:S(2)}, u32[]{:S(2)}) collective-permute-start(f32[40,128]{1,0:T(8,128)S(1)} %get-tuple-element.16), channel_id=1, source_target_pairs={{1,0},{2,1},{3,2},{4,3},{5,4},{6,5},{7,6},{8,7},{9,8},{10,9},{11,1... | collective-permute-start | bytes 61448 | tf_op jit(solution)/shard_map/ppermute | solution.py:641
  18.8 4.4 %collective-permute-start.1 = (f32[40,128]{1,0:T(8,128)S(1)}, f32[40,128]{1,0:T(8,128)S(1)}, u32[]{:S(2)}, u32[]{:S(2)}) collective-permute-start(f32[40,128]{1,0:T(8,128)S(1)} %get-tuple-element.17), channel_id=1, source_target_pairs={{0,1},{1,2},{2,3},{3,4},{4,5},{5,6},{6,7},{7,8},{8,9},{9,10},{10,1... | collective-permute-start | bytes 61448 | tf_op jit(solution)/shard_map/ppermute | solution.py:641
  23.1 0.6 collective-permute-done.from_east
  23.8 0.3 collective-permute-done.1.from_west
  24.0 0.3 sides.1
  24.3 5.3 %all-to-all-done = f32[128,1,1152]{2,1,0:T(1,128)S(1)} async-done(((f32[128,1,1152]{2,1,0:T(1,128)}), f32[128,1,1152]{2,1,0:T(1,128)S(1)}, u32[]{:S(2)}, u32[]{:S(2)}) %all-to-all-start) | async-done | bytes 589856 | tf_op jit(solution)/shard_map/all_to_all | solution.py:658
  29.6 0.5 force.1
  30.1 0.1 collective-permute-start.2
  30.2 3.6 %collective-permute-start.3 = (f32[15,8,128]{2,1,0:T(8,128)S(1)}, f32[15,8,128]{2,1,0:T(8,128)S(1)}, u32[]{:S(2)}, u32[]{:S(2)}) collective-permute-start(f32[15,8,128]{2,1,0:T(8,128)S(1)} %get-tuple-element.19), channel_id=1, source_target_pairs={{0,112},{16,0},{32,16},{48,32},{64,48},{80,64},{96,80},{112,96},{1... | collective-permute-start | bytes 184328 | tf_op jit(solution)/shard_map/ppermute | solution.py:641
  33.8 1.6 %collective-permute-done.2.from_north = f32[15,8,128]{2,1,0:T(8,128)S(1)} collective-permute-done((f32[15,8,128]{2,1,0:T(8,128)S(1)}, f32[15,8,128]{2,1,0:T(8,128)S(1)}, u32[]{:S(2)}, u32[]{:S(2)}) %collective-permute-start.2) | collective-permute-done | bytes 61472 | tf_op jit(solution)/shard_map/ppermute | solution.py:641
  35.4 0.0 collective-permute-done.3.from_south
  35.4 0.0 copy-done.3
  35.4 0.0 copy-done.4
  35.4 2.4 %first_patch.1 = (f32[3,7,144,128]{3,2,1,0:T(8,128)S(1)}, f32[3,3,144,128]{3,2,1,0:T(8,128)S(1)}, f32[256,128]{1,0:T(8,128)}) custom-call(s32[8]{0:T(128)S(1)} %copy-done.4, f32[2,128,256]{2,1,0:T(8,128)S(1)} %copy-done, f32[2,128,256]{2,1,0:T(8,128)S(1)} %copy-done.1, f32[128,256]{1,0:T(8,128)S(1)} %copy-done.2, f32[5,128,128]{2,1,0:T(8,128)S(1)} %sides.1, ...), custom_call_target="tpu_custom_call" | custom-call | tf_op jit(solution)/shard_map/first_patch/pallas_call | solution.py:76
  37.8 8.3 %all-to-all-start.1 = ((f32[128,1,256]{2,1,0:T(1,128)}), f32[128,1,256]{2,1,0:T(1,128)S(1)}, u32[]{:S(2)}, u32[]{:S(2)}) async-start(f32[128,1,256]{2,1,0:T(1,128)} %bitcast.7), calls=%async_computation.1 | async-start | bytes 262144 | tf_op jit(solution)/shard_map/all_to_all | solution.py:658
  46.1 0.4 tables.1
  46.5 9.5 %all-to-all-done.1 = f32[128,1,256]{2,1,0:T(1,128)S(1)} async-done(((f32[128,1,256]{2,1,0:T(1,128)}), f32[128,1,256]{2,1,0:T(1,128)S(1)}, u32[]{:S(2)}, u32[]{:S(2)}) %all-to-all-start.1) | async-done | bytes 131104 | tf_op jit(solution)/shard_map/all_to_all | solution.py:658
  56.0 4.1 %first_steps.1 = (f32[3,7,144,128]{3,2,1,0:T(8,128)S(1)}, f32[256,128]{1,0:T(8,128)S(1)}) custom-call(s32[8]{0:T(128)S(1)} %copy-done.4, f32[3,7,144,128]{3,2,1,0:T(8,128)S(1)} %get-tuple-element.21.ahead, f32[3,3,144,128]{3,2,1,0:T(8,128)S(1)} %get-tuple-element.22.coef, f32[256,128]{1,0:T(8,128)S(1)} %bitcast.14, f32[24,128]{1,0:T(8,128)S(1)} %get-tuple-element.24.ports, ...), custom_call_target="tpu_custom_call" | custom-call | tf_op jit(solution)/shard_map/first_steps/pallas_call | solution.py:76
  60.1 14.0 %all_to_all.15 = f32[128,1,256]{2,1,0:T(1,128)S(1)} all-to-all(f32[128,1,256]{2,1,0:T(1,128)S(1)} %bitcast.16), channel_id=1, replica_groups=mesh['circ'=8,'axial'=16] {'circ','axial'}, dimensions={0} | all-to-all | bytes 262144 | tf_op jit(solution)/shard_map/all_to_all | solution.py:658
  74.1 3.1 %last_steps.1 = (f32[2,128,256]{2,1,0:T(8,128)}, f32[2,128,256]{2,1,0:T(8,128)}) custom-call(f32[3,7,144,128]{3,2,1,0:T(8,128)S(1)} %get-tuple-element.28.ahead, f32[3,3,144,128]{3,2,1,0:T(8,128)S(1)} %get-tuple-element.22.coef, f32[256,128]{1,0:T(8,128)S(1)} %bitcast.15, f32[24,128]{1,0:T(8,128)S(1)} %get-tuple-element.24.ports, ...), custom_call_target="tpu_custom_call" | custom-call | tf_op jit(solution)/shard_map/last_steps/pallas_call | solution.py:76
Async XLA Ops:
  0.6 14.8 %copy-start.2 = (f32[128,256]{1,0:T(8,128)S(1)}, f32[128,256]{1,0:T(8,128)}, u32[]{:S(2)}) copy-start(f32[128,256]{1,0:T(8,128)} %co.5) | copy-start | bytes 393220
  0.6 14.8 %copy-start.1 = (f32[2,128,256]{2,1,0:T(8,128)S(1)}, f32[2,128,256]{2,1,0:T(8,128)}, u32[]{:S(2)}) copy-start(f32[2,128,256]{2,1,0:T(8,128)} %vo.5) | copy-start | bytes 786436
  0.7 14.8 %copy-start = (f32[2,128,256]{2,1,0:T(8,128)S(1)}, f32[2,128,256]{2,1,0:T(8,128)}, u32[]{:S(2)}) copy-start(f32[2,128,256]{2,1,0:T(8,128)} %ca.5) | copy-start | bytes 786436
  4.0 25.6 %all-to-all-start = ((f32[128,1,1152]{2,1,0:T(1,128)}), f32[128,1,1152]{2,1,0:T(1,128)S(1)}, u32[]{:S(2)}, u32[]{:S(2)}) async-start(f32[128,1,1152]{2,1,0:T(1,128)} %bitcast.5), calls=%async_computation | async-start | bytes 1179648 | tf_op jit(solution)/shard_map/all_to_all | solution.py:658
  15.5 19.9 %copy-start.3 = (s32[8,256]{1,0:T(8,128)S(1)}, s32[8,256]{1,0:T(8,128)}, u32[]{:S(2)}) copy-start(s32[8,256]{1,0:T(8,128)} %constant.2.clone.table) | copy-start | bytes 24580
  15.5 19.9 %copy-start.4 = (s32[8]{0:T(128)S(1)}, s32[8]{0:T(128)}, u32[]{:S(2)}) copy-start(s32[8]{0:T(128)} %cells.5) | copy-start | bytes 100
  15.8 8.0 %collective-permute-start = (f32[40,128]{1,0:T(8,128)S(1)}, f32[40,128]{1,0:T(8,128)S(1)}, u32[]{:S(2)}, u32[]{:S(2)}) collective-permute-start(f32[40,128]{1,0:T(8,128)S(1)} %get-tuple-element.16), channel_id=1, source_target_pairs={{1,0},{2,1},{3,2},{4,3},{5,4},{6,5},{7,6},{8,7},{9,8},{10,9},{11,1... | collective-permute-start | bytes 61448 | tf_op jit(solution)/shard_map/ppermute | solution.py:641
  18.8 5.3 %collective-permute-start.1 = (f32[40,128]{1,0:T(8,128)S(1)}, f32[40,128]{1,0:T(8,128)S(1)}, u32[]{:S(2)}, u32[]{:S(2)}) collective-permute-start(f32[40,128]{1,0:T(8,128)S(1)} %get-tuple-element.17), channel_id=1, source_target_pairs={{0,1},{1,2},{2,3},{3,4},{4,5},{5,6},{6,7},{7,8},{8,9},{9,10},{10,1... | collective-permute-start | bytes 61448 | tf_op jit(solution)/shard_map/ppermute | solution.py:641
  30.1 5.3 %collective-permute-start.2 = (f32[15,8,128]{2,1,0:T(8,128)S(1)}, f32[15,8,128]{2,1,0:T(8,128)S(1)}, u32[]{:S(2)}, u32[]{:S(2)}) collective-permute-start(f32[15,8,128]{2,1,0:T(8,128)S(1)} %get-tuple-element.18), channel_id=1, source_target_pairs={{0,16},{16,32},{32,48},{48,64},{64,80},{80,96},{96,112},{112,0},{1... | collective-permute-start | bytes 184328 | tf_op jit(solution)/shard_map/ppermute | solution.py:641
  30.2 5.2 %collective-permute-start.3 = (f32[15,8,128]{2,1,0:T(8,128)S(1)}, f32[15,8,128]{2,1,0:T(8,128)S(1)}, u32[]{:S(2)}, u32[]{:S(2)}) collective-permute-start(f32[15,8,128]{2,1,0:T(8,128)S(1)} %get-tuple-element.19), channel_id=1, source_target_pairs={{0,112},{16,0},{32,16},{48,32},{64,48},{80,64},{96,80},{112,96},{1... | collective-permute-start | bytes 184328 | tf_op jit(solution)/shard_map/ppermute | solution.py:641
  37.8 18.2 %all-to-all-start.1 = ((f32[128,1,256]{2,1,0:T(1,128)}), f32[128,1,256]{2,1,0:T(1,128)S(1)}, u32[]{:S(2)}, u32[]{:S(2)}) async-start(f32[128,1,256]{2,1,0:T(1,128)} %bitcast.7), calls=%async_computation.1 | async-start | bytes 262144 | tf_op jit(solution)/shard_map/all_to_all | solution.py:658

commit v6 on v5

--- a/solution.py
+++ b/solution.py
@@ -13,6 +13,7 @@
 LANES = 128
 WIDE = 384
 RADIUS = 2
+REACH = 3
 SIDE = 5
 BLOCK = 9
 EXT = 144
@@ -49,7 +50,7 @@
         for slot in range(8):
             at = index * 8 + slot
             table[0, at] = field * SIDE + b + RADIUS
-            table[1, at] = slot * 8 + a + RADIUS
+            table[1, at] = slot * 8 + a + REACH
     return table
 
 
@@ -259,37 +260,68 @@
     return [strip[2 * f], strip[2 * f + 1], side]
 
 
-def extract(fields, cells, table, tmp, out):
-    lane = iota((8, LANES), 1)
+def extract(sources, cells, table, tmp, out):
+    i_axial = lax.axis_index("axial")
     long_lane = iota((16, LANES), 1)
-    flat = fields.reshape(3 * 7 * EXT, LANES)
+    lane = iota((64, LANES), 1)
+    flats = {id(ref): ref.reshape(3 * n * EXT, LANES) for ref, n, _ in sources}
+    marks = []
     for slot in range(8):
         cell = cells[slot]
-        row = lax.shift_right_logical(cell, 8) + (HALO - RADIUS)
-        col = (cell & 255) - RADIUS
-        col = jnp.where(col < 0, col + WIDE, col)
+        row = lax.shift_right_logical(cell, 8) + (HALO - REACH)
+        own = cell & 255
+        col = jnp.where(own < REACH, own + (WIDE - REACH), own - REACH)
         base = pl.multiple_of(row & -8, 8)
         turn = 16 - (row & 7)
         tile = lax.shift_right_logical(col, 7)
         other = jnp.where(tile == 2, 0, tile + 1)
         inside = col & (LANES - 1)
-        kept = jnp.zeros((8, LANES), jnp.float32)
-        span = 6 * EXT + 16
-        here = flat.at[pl.ds(pl.multiple_of(tile * (7 * EXT) + base, 8), span), :]
-        there = flat.at[pl.ds(pl.multiple_of(other * (7 * EXT) + base, 8), span), :]
         back = (LANES - inside) & (LANES - 1)
-        for f, field in enumerate((2, 0, 3, 5, 1, 6, 4)):
+        marks.append(jnp.zeros((8, LANES), jnp.int32) + own)
+        views = {}
+        for ref, n, _ in sources:
+            if id(ref) not in views:
+                span = (n - 1) * EXT + 16
+                views[id(ref)] = [
+                    flats[id(ref)].at[pl.ds(pl.multiple_of(t * (n * EXT) + base, 8), span), :]
+                    for t in (tile, other)
+                ]
+        for f, (ref, _, field) in enumerate(sources):
+            here, there = views[id(ref)]
             rows = slice(field * EXT, field * EXT + 16)
             window = jnp.where(long_lane < inside, there[rows, :], here[rows, :])
-            window = pltpu.roll(pltpu.roll(window, turn, 0)[:8], back, 1)
-            window = pltpu.roll(window, f * SIDE, 1) if f else window
-            kept = jnp.where((lane >= f * SIDE) & (lane < (f + 1) * SIDE), window, kept)
-        tmp[slot * 8 : slot * 8 + 8, :] = kept
+            tmp[f, slot * 8 : slot * 8 + 8, :] = pltpu.roll(
+                pltpu.roll(window, turn, 0)[:8], back, 1
+            )
+    column = jnp.concatenate(marks, axis=0) + lane - REACH
+    first = (column == 0) & ((lane * 0 + i_axial) == 0)
+    last = (column == 255) & ((lane * 0 + i_axial) == 15)
+    v, s, u, spread, e, a_s, a_e = [tmp[f] for f in range(7)]
+
+    def near(x):
+        left = jnp.where(first, x, pltpu.roll(x, 1, 1))
+        right = jnp.where(last, x, pltpu.roll(x, LANES - 1, 1))
+        return pltpu.roll(x, 1, 0) + pltpu.roll(x, 63, 0) + left + right
+
+    parts = reciprocals(s, e)
+    sent = [
+        v_step(parts, v, u, near(v), spread),
+        s_step(parts, s, e, v, near(s), spread, a_s),
+        u_step(parts, v, u, near(u), spread),
+        spread,
+        e_step(s, e, near(e), spread, a_e),
+        a_s,
+        v,
+    ]
+    kept = jnp.zeros((64, LANES), jnp.float32)
+    for f, value in enumerate(sent):
+        moved = pltpu.roll(value, (f * SIDE + RADIUS - REACH) % LANES, 1)
+        kept = jnp.where((lane >= f * SIDE) & (lane < (f + 1) * SIDE), moved, kept)
     width = 2 * LANES
     at = iota((LANES, width), 0)
     wanted = table[0:1, :]
     pick = one_hot((at == wanted) | (at == wanted + 40) | (at == wanted + 80))
-    high, middle, low = [x.astype(jnp.float32) for x in three_parts(tmp[...])]
+    high, middle, low = [x.astype(jnp.float32) for x in three_parts(kept)]
     pieces = dot(
         (high + pltpu.roll(middle, 40, 1) + pltpu.roll(low, 80, 1)).astype(jnp.bfloat16), pick
     )
@@ -355,34 +387,41 @@
     in_row[...] = jnp.transpose(jnp.where(place == iota((256, 256), 1), 1.0, 0.0))[:EXT]
 
 
+ORDER = (2, 0, 3, 4, 1, 5, 6)
+
+
 def first_patch_kernel(
-    cells, ca, vo, co, sides, from_north, from_south, force, table,
-    ahead, coef, out, start, tmp,
+    cells, ca, vo, co, sides, from_north, from_south, force, table, start, rest, out, tmp
 ):
-    after = fields_of(ahead, 7)
-    before = fields_of(start, 5)
-    for f, ref in enumerate(all_fields(ca, vo, co)):
+    for f in range(7):
         scale = 0.05 if f == 4 else 1.0
+        if f < 5:
+            ref = all_fields(ca, vo, co)[f]
+            tiles = [ref[:, :LANES], ref[:, LANES:], sides[f]]
+        else:
+            tiles = [force[f - 5, tile] for tile in range(3)]
         build_rows(
-            before[f] if f < 4 else after[5],
-            [t * scale for t in (ref[:, :LANES], ref[:, LANES:], sides[f])],
+            Field(start, f) if f < 4 else Field(rest, f - 4),
+            [t * scale for t in tiles],
             [t * scale for t in strip_tiles(from_north, f)],
             [t * scale for t in strip_tiles(from_south, f)],
         )
-    for f in range(2):
-        build_rows(
-            after[6] if f == 0 else before[4],
-            [force[f, tile] for tile in range(3)],
-            strip_tiles(from_north, 5 + f),
-            strip_tiles(from_south, 5 + f),
-        )
-    for tile in range(3):
-        ahead[tile, 4] = start[tile, 2]
+    extract(patch_sources(start, rest), cells, table, tmp, out)
+
+
+def patch_sources(state, rest):
+    return [(state, 4, f) if f < 4 else (rest, 3, f - 4) for f in ORDER]
+
+
+def first_step_kernel(start, rest, ahead, coef):
     coefs = fields_of(coef, 3)
-    for src, dst in zip((after[5], after[6], before[4]), coefs):
+    for src, dst in zip(fields_of(rest, 3), coefs):
         to_mixed(src, dst)
-    one_step(before[:4], rows_at, after[:4], rows_at, coefs, None)
-    extract(ahead, cells, table, tmp, out)
+    one_step(fields_of(start, 4), rows_at, fields_of(ahead, 4), mixed_at, coefs, None)
+
+
+def free_step_kernel(state, coef, ahead):
+    one_step(fields_of(state, 4), mixed_at, fields_of(ahead, 4), mixed_at, fields_of(coef, 3), None)
 
 
 def port_places(ports):
@@ -594,31 +633,26 @@
     gains = port_sim(got, codes, rows, cols, partner)
     injections(gains, in_row, in_col, inject)
     one, two = fields_of(first, 4), fields_of(second, 4)
+    now = fields_of(ahead, 4)
+    for tile in range(3):
+        first[tile, 2] = ahead[tile, 2] + inject[0, tile]
+    now[2] = one[2]
+    coefs = fields_of(coef, 3)
+    one_step(now, mixed_at, two, mixed_at, coefs, inject.at[1])
+    one_step(two, mixed_at, one, mixed_at, coefs, inject.at[2])
+    one_step(one, mixed_at, two, mixed_at, coefs, inject.at[3])
+
+
+def first_steps_kernel(
+    cells, ahead, coef, rest, got, ports, in_row, in_col, codes, table,
+    second, out, first, inject, tmp,
+):
+    coupled_steps(ahead, coef, got, ports, in_row, in_col, codes, first, second, inject)
     for f in range(4):
         for tile in range(3):
             for j in range(STEP):
-                value = ahead[tile, f, rows_at(j), :]
-                if f == 2:
-                    value = value + inject[0, tile, mixed_at(j), :]
-                first[tile, f, mixed_at(j), :] = value
-    coefs = fields_of(coef, 3)
-    for k, (now, later) in enumerate(((one, two), (two, one), (one, two))):
-        one_step(now, mixed_at, later, mixed_at, coefs, inject.at[k + 1])
-    return two
-
-
-def first_steps_kernel(
-    cells, ahead, coef, got, ports, in_row, in_col, codes, table,
-    later, out, first, second, inject, tmp,
-):
-    now = coupled_steps(ahead, coef, got, ports, in_row, in_col, codes, first, second, inject)
-    for tile in range(3):
-        for j in range(STEP):
-            later[tile, 4, rows_at(j), :] = second[tile, 2, mixed_at(j), :]
-        later[tile, 5] = ahead[tile, 5]
-        later[tile, 6] = ahead[tile, 6]
-    one_step(now, mixed_at, fields_of(later, 4), rows_at, fields_of(coef, 3), None)
-    extract(later, cells, table, tmp, out)
+                first[tile, f, rows_at(j), :] = second[tile, f, mixed_at(j), :]
+    extract(patch_sources(first, rest), cells, table, tmp, out)
 
 
 def last_steps_kernel(
@@ -682,30 +716,35 @@
         "tables",
         last=jnp.int32,
     )(ports)
-    patch_space = pltpu.VMEM((64, LANES), jnp.float32)
-    ahead, coef, patches = call(
+    patch_space = pltpu.VMEM((7, 64, LANES), jnp.float32)
+    start, rest, patches = call(
         first_patch_kernel,
-        [stack(7), stack(3), (256, LANES)],
+        [stack(4), stack(3), (256, LANES)],
         [SMEM] + [HELD] * 8,
         "first_patch",
-        [pltpu.VMEM(stack(5), jnp.float32), patch_space],
+        [patch_space],
     )(cells, ca, vo, co, sides, from_north, from_south, force, table)
     got = to_all(patches)
-    scratch = [pltpu.VMEM(stack(4), jnp.float32)] * 2 + [pltpu.VMEM((4, 3, EXT, LANES), jnp.float32)]
-    ahead, patches = call(
+    ahead, coef = call(first_step_kernel, [stack(4), stack(3)], [HELD] * 2, "first_step")(
+        start, rest
+    )
+    moved = pltpu.VMEM(stack(4), jnp.float32)
+    inject = pltpu.VMEM((4, 3, EXT, LANES), jnp.float32)
+    state, patches = call(
         first_steps_kernel,
-        [stack(7), (256, LANES)],
-        [SMEM] + [HELD] * 8,
+        [stack(4), (256, LANES)],
+        [SMEM] + [HELD] * 7 + [VMEM] * 2,
         "first_steps",
-        scratch + [patch_space],
-    )(cells, ahead, coef, got, ports, in_row, in_col, codes, table)
+        [moved, inject, patch_space],
+    )(cells, ahead, coef, rest, got, ports, in_row, in_col, codes, table)
     got = to_all(patches)
+    (ahead,) = call(free_step_kernel, [stack(4)], [HELD] * 2, "free_step")(state, coef)
     return call(
         last_steps_kernel,
         [(2, 128, 256)] * 2,
         [HELD] * 7,
         "last_steps",
-        scratch,
+        [moved, moved, inject],
         place=jax.ShapeDtypeStruct,
     )(ahead, coef, got, ports, in_row, in_col, codes)
 

time: 77.6 us -> 78.6 us (1.013)
  blocking collectives: 14 us -> 0 us
  waiting for transfers between devices: 17.2 us -> 24.8 us
  starting transfers between devices: 30.8 us -> 35 us
  local copies, waits for them, and re-layouts: 0.03 us -> 2.11 us
  Pallas kernels: 13.8 us -> 14.9 us
    all_to_all x1 -> x0, blocking collectives: 14 us -> none  [to_all(): return lax.all_to_all(blocks, AXES, 0, 0, tiled=True).reshape(value.shape)]
    all_to_all x2 -> x3, waiting for transfers between devices: 14.7 us -> 22.3 us  [to_all(): return lax.all_to_all(blocks, AXES, 0, 0, tiled=True).reshape(value.shape)]
    all_to_all x2 -> x3, starting transfers between devices: 19.8 us -> 24.1 us  [to_all(): return lax.all_to_all(blocks, AXES, 0, 0, tiled=True).reshape(value.shape)]
    unnamed x10 -> x14, local copies, waits for them, and re-layouts: 0.03 us -> 2.11 us
    pallas_call x8 -> x10, Pallas kernels: 13.8 us -> 14.9 us  [placed(): run(*(pltpu.with_memory_space_constraint(x, pltpu.VMEM) if spec is HELD e...]
  transfers between devices with their start and end apart: 6 -> 7, of which waited for: 5 -> 6; matrix products, arithmetic and copies ran while one was open for 0% -> 0% of each run, Pallas kernels for 1% -> 3%
where the time goes in v6:
time: 78.6 us; the launch traced here: 78.3 us
  starting transfers between devices  35 us (45%)
  waiting for transfers between devices  24.8 us (32%)
  Pallas kernels  14.9 us (19%)
  local copies, waits for them, and re-layouts  2.11 us (3%)
  between operations  1.41 us (2%)
    all_to_all x3, starting transfers between devices, to_all(): return lax.all_to_all(blocks, AXES, 0, 0, tiled=True).reshape(value.shape)  24.1 us
    all_to_all x3, waiting for transfers between devices, to_all(): return lax.all_to_all(blocks, AXES, 0, 0, tiled=True).reshape(value.shape)  22.3 us
    pallas_call x10, Pallas kernels, placed(): run(*(pltpu.with_memory_space_constraint(x, pltpu.VMEM) if spec is HELD e...  14.9 us
    ppermute x4, starting transfers between devices, shifted(): lax.ppermute(value, axis, [(i, j) for i, j in pairs if 0 <= j < count])  11 us
    ppermute x4, waiting for transfers between devices, shifted(): lax.ppermute(value, axis, [(i, j) for i, j in pairs if 0 <= j < count])  2.49 us
    unnamed x14, local copies, waits for them, and re-layouts  2.11 us
  transfers between devices with their start and end apart: 7, of which 6 were waited for; matrix products, arithmetic and copies ran while one was open for 0% of the time, Pallas kernels for 3%

profile of v6, /device:TPU:1, one launch (start us, length us, event | category | flops | bytes accessed | tf_op | source)
XLA Modules:
  0.0 78.3 jit_solution(17345856332187622183)
XLA Ops:
  1.3 2.6 %pack.1 = f32[1152,128]{1,0:T(8,128)} custom-call(s32[1]{0:T(128)S(6)} %copy.17.count, s32[8]{0:T(128)} %cells.5, s32[8]{0:T(128)} %partner.1, s32[1,192]{1,0:T(1,128)} %bitcast.17, s32[1,192]{1,0:T(1,128)} %bitcast.18, f32[768,128]{1,0:T(8,128)} %bitcast.16), custom_call_target="tpu_custom_call" | custom-call | tf_op jit(solution)/shard_map/pack/pallas_call | solution.py:77
  3.9 11.5 %all-to-all-start = ((f32[128,1,1152]{2,1,0:T(1,128)}), f32[128,1,1152]{2,1,0:T(1,128)S(1)}, u32[]{:S(2)}, u32[]{:S(2)}) async-start(f32[128,1,1152]{2,1,0:T(1,128)} %bitcast.5), calls=%async_computation | async-start | bytes 1179648 | tf_op jit(solution)/shard_map/all_to_all | solution.py:692
  15.4 0.0 copy-done
  15.4 0.0 copy-done.1
  15.4 0.0 copy-done.2
  15.4 0.3 strips.1
  15.7 3.0 %collective-permute-start = (f32[40,128]{1,0:T(8,128)S(1)}, f32[40,128]{1,0:T(8,128)S(1)}, u32[]{:S(2)}, u32[]{:S(2)}) collective-permute-start(f32[40,128]{1,0:T(8,128)S(1)} %get-tuple-element.18), channel_id=1, source_target_pairs={{1,0},{2,1},{3,2},{4,3},{5,4},{6,5},{7,6},{8,7},{9,8},{10,9},{11,1... | collective-permute-start | bytes 61448 | tf_op jit(solution)/shard_map/ppermute | solution.py:675
  18.6 4.4 %collective-permute-start.1 = (f32[40,128]{1,0:T(8,128)S(1)}, f32[40,128]{1,0:T(8,128)S(1)}, u32[]{:S(2)}, u32[]{:S(2)}) collective-permute-start(f32[40,128]{1,0:T(8,128)S(1)} %get-tuple-element.19), channel_id=1, source_target_pairs={{0,1},{1,2},{2,3},{3,4},{4,5},{5,6},{6,7},{7,8},{8,9},{9,10},{10,1... | collective-permute-start | bytes 61448 | tf_op jit(solution)/shard_map/ppermute | solution.py:675
  23.0 0.7 collective-permute-done.from_east
  23.7 0.2 collective-permute-done.1.from_west
  23.9 0.3 sides.1
  24.2 5.3 %all-to-all-done = f32[128,1,1152]{2,1,0:T(1,128)S(1)} async-done(((f32[128,1,1152]{2,1,0:T(1,128)}), f32[128,1,1152]{2,1,0:T(1,128)S(1)}, u32[]{:S(2)}, u32[]{:S(2)}) %all-to-all-start) | async-done | bytes 589856 | tf_op jit(solution)/shard_map/all_to_all | solution.py:692
  29.5 0.5 force.1
  30.0 0.1 collective-permute-start.2
  30.1 0.0 copy-start.6
  30.1 3.6 %collective-permute-start.3 = (f32[15,8,128]{2,1,0:T(8,128)S(1)}, f32[15,8,128]{2,1,0:T(8,128)S(1)}, u32[]{:S(2)}, u32[]{:S(2)}) collective-permute-start(f32[15,8,128]{2,1,0:T(8,128)S(1)} %get-tuple-element.21), channel_id=1, source_target_pairs={{0,112},{16,0},{32,16},{48,32},{64,48},{80,64},{96,80},{112,96},{1... | collective-permute-start | bytes 184328 | tf_op jit(solution)/shard_map/ppermute | solution.py:675
  33.7 1.6 %collective-permute-done.2.from_north = f32[15,8,128]{2,1,0:T(8,128)S(1)} collective-permute-done((f32[15,8,128]{2,1,0:T(8,128)S(1)}, f32[15,8,128]{2,1,0:T(8,128)S(1)}, u32[]{:S(2)}, u32[]{:S(2)}) %collective-permute-start.2) | collective-permute-done | bytes 61472 | tf_op jit(solution)/shard_map/ppermute | solution.py:675
  35.3 0.0 collective-permute-done.3.from_south
  35.3 0.0 copy-done.5
  35.3 0.0 copy-done.6
  35.3 1.8 %first_patch.1 = (f32[3,4,144,128]{3,2,1,0:T(8,128)S(1)}, f32[3,3,144,128]{3,2,1,0:T(8,128)S(1)}, f32[256,128]{1,0:T(8,128)}) custom-call(s32[8]{0:T(128)S(1)} %copy-done.6, f32[2,128,256]{2,1,0:T(8,128)S(1)} %copy-done, f32[2,128,256]{2,1,0:T(8,128)S(1)} %copy-done.1, f32[128,256]{1,0:T(8,128)S(1)} %copy-done.2, f32[5,128,128]{2,1,0:T(8,128)S(1)} %sides.1, ...), custom_call_target="tpu_custom_call" | custom-call | tf_op jit(solution)/shard_map/first_patch/pallas_call | solution.py:77
  37.1 8.3 %all-to-all-start.1 = ((f32[128,1,256]{2,1,0:T(1,128)}), f32[128,1,256]{2,1,0:T(1,128)S(1)}, u32[]{:S(2)}, u32[]{:S(2)}) async-start(f32[128,1,256]{2,1,0:T(1,128)} %bitcast.7), calls=%async_computation.1 | async-start | bytes 262144 | tf_op jit(solution)/shard_map/all_to_all | solution.py:692
  45.4 0.4 tables.1
  45.8 0.7 first_step.1
  46.6 0.9 %copy-done.3 = f32[3,4,144,128]{3,2,1,0:T(8,128)} copy-done((f32[3,4,144,128]{3,2,1,0:T(8,128)}, f32[3,4,144,128]{3,2,1,0:T(8,128)S(1)}, u32[]{:S(2)}) %copy-start.3) | copy-done | bytes 884760
  47.5 7.8 %all-to-all-done.1 = f32[128,1,256]{2,1,0:T(1,128)S(1)} async-done(((f32[128,1,256]{2,1,0:T(1,128)}), f32[128,1,256]{2,1,0:T(1,128)S(1)}, u32[]{:S(2)}, u32[]{:S(2)}) %all-to-all-start.1) | async-done | bytes 131104 | tf_op jit(solution)/shard_map/all_to_all | solution.py:692
  55.3 1.2 %copy-done.4 = f32[3,4,144,128]{3,2,1,0:T(8,128)S(1)} copy-done((f32[3,4,144,128]{3,2,1,0:T(8,128)S(1)}, f32[3,4,144,128]{3,2,1,0:T(8,128)}, u32[]{:S(2)}) %copy-start.4) | copy-done | bytes 884760
  56.5 4.4 %first_steps.1 = (f32[3,4,144,128]{3,2,1,0:T(8,128)S(1)}, f32[256,128]{1,0:T(8,128)}) custom-call(s32[8]{0:T(128)S(1)} %copy-done.6, f32[3,4,144,128]{3,2,1,0:T(8,128)S(1)} %copy-done.4, f32[3,3,144,128]{3,2,1,0:T(8,128)S(1)} %get-tuple-element.26.coef, f32[3,3,144,128]{3,2,1,0:T(8,128)S(1)} %get-tuple-element.24.rest, f32[256,128]{1,0:T(8,128)S(1)} %bitcast.14, ...), custom_call_target="tpu_custom_call" | custom-call | tf_op jit(solution)/shard_map/first_steps/pallas_call | solution.py:77
  60.9 4.3 %all-to-all-start.2 = ((f32[128,1,256]{2,1,0:T(1,128)}), f32[128,1,256]{2,1,0:T(1,128)S(1)}, u32[]{:S(2)}, u32[]{:S(2)}) async-start(f32[128,1,256]{2,1,0:T(1,128)} %bitcast.9), calls=%async_computation.2 | async-start | bytes 262144 | tf_op jit(solution)/shard_map/all_to_all | solution.py:692
  65.2 0.7 free_step.1.ahead
  65.9 9.2 %all-to-all-done.2 = f32[128,1,256]{2,1,0:T(1,128)S(1)} async-done(((f32[128,1,256]{2,1,0:T(1,128)}), f32[128,1,256]{2,1,0:T(1,128)S(1)}, u32[]{:S(2)}, u32[]{:S(2)}) %all-to-all-start.2) | async-done | bytes 131104 | tf_op jit(solution)/shard_map/all_to_all | solution.py:692
  75.1 3.2 %last_steps.1 = (f32[2,128,256]{2,1,0:T(8,128)}, f32[2,128,256]{2,1,0:T(8,128)}) custom-call(f32[3,4,144,128]{3,2,1,0:T(8,128)S(1)} %free_step.1.ahead, f32[3,3,144,128]{3,2,1,0:T(8,128)S(1)} %get-tuple-element.26.coef, f32[256,128]{1,0:T(8,128)S(1)} %bitcast.15, f32[24,128]{1,0:T(8,128)S(1)} %get-tuple-element.28.ports, ...), custom_call_target="tpu_custom_call" | custom-call | tf_op jit(solution)/shard_map/last_steps/pallas_call | solution.py:77
  (6 shorter events, 0.0 us)
Async XLA Ops:
  3.9 11.5 %copy-start = (f32[2,128,256]{2,1,0:T(8,128)S(1)}, f32[2,128,256]{2,1,0:T(8,128)}, u32[]{:S(2)}) copy-start(f32[2,128,256]{2,1,0:T(8,128)} %ca.5) | copy-start | bytes 786436
  3.9 11.5 %copy-start.1 = (f32[2,128,256]{2,1,0:T(8,128)S(1)}, f32[2,128,256]{2,1,0:T(8,128)}, u32[]{:S(2)}) copy-start(f32[2,128,256]{2,1,0:T(8,128)} %vo.5) | copy-start | bytes 786436
  3.9 11.5 %copy-start.2 = (f32[128,256]{1,0:T(8,128)S(1)}, f32[128,256]{1,0:T(8,128)}, u32[]{:S(2)}) copy-start(f32[128,256]{1,0:T(8,128)} %co.5) | copy-start | bytes 393220
  3.9 25.6 %all-to-all-start = ((f32[128,1,1152]{2,1,0:T(1,128)}), f32[128,1,1152]{2,1,0:T(1,128)S(1)}, u32[]{:S(2)}, u32[]{:S(2)}) async-start(f32[128,1,1152]{2,1,0:T(1,128)} %bitcast.5), calls=%async_computation | async-start | bytes 1179648 | tf_op jit(solution)/shard_map/all_to_all | solution.py:692
  15.7 8.0 %collective-permute-start = (f32[40,128]{1,0:T(8,128)S(1)}, f32[40,128]{1,0:T(8,128)S(1)}, u32[]{:S(2)}, u32[]{:S(2)}) collective-permute-start(f32[40,128]{1,0:T(8,128)S(1)} %get-tuple-element.18), channel_id=1, source_target_pairs={{1,0},{2,1},{3,2},{4,3},{5,4},{6,5},{7,6},{8,7},{9,8},{10,9},{11,1... | collective-permute-start | bytes 61448 | tf_op jit(solution)/shard_map/ppermute | solution.py:675
  18.6 5.3 %collective-permute-start.1 = (f32[40,128]{1,0:T(8,128)S(1)}, f32[40,128]{1,0:T(8,128)S(1)}, u32[]{:S(2)}, u32[]{:S(2)}) collective-permute-start(f32[40,128]{1,0:T(8,128)S(1)} %get-tuple-element.19), channel_id=1, source_target_pairs={{0,1},{1,2},{2,3},{3,4},{4,5},{5,6},{6,7},{7,8},{8,9},{9,10},{10,1... | collective-permute-start | bytes 61448 | tf_op jit(solution)/shard_map/ppermute | solution.py:675
  29.5 5.8 %copy-start.5 = (s32[8,256]{1,0:T(8,128)S(1)}, s32[8,256]{1,0:T(8,128)}, u32[]{:S(2)}) copy-start(s32[8,256]{1,0:T(8,128)} %constant.2.clone.table) | copy-start | bytes 24580
  30.0 5.3 %collective-permute-start.2 = (f32[15,8,128]{2,1,0:T(8,128)S(1)}, f32[15,8,128]{2,1,0:T(8,128)S(1)}, u32[]{:S(2)}, u32[]{:S(2)}) collective-permute-start(f32[15,8,128]{2,1,0:T(8,128)S(1)} %get-tuple-element.20), channel_id=1, source_target_pairs={{0,16},{16,32},{32,48},{48,64},{64,80},{80,96},{96,112},{112,0},{1... | collective-permute-start | bytes 184328 | tf_op jit(solution)/shard_map/ppermute | solution.py:675
  30.1 5.2 %copy-start.6 = (s32[8]{0:T(128)S(1)}, s32[8]{0:T(128)}, u32[]{:S(2)}) copy-start(s32[8]{0:T(128)} %cells.5) | copy-start | bytes 100
  30.1 5.2 %collective-permute-start.3 = (f32[15,8,128]{2,1,0:T(8,128)S(1)}, f32[15,8,128]{2,1,0:T(8,128)S(1)}, u32[]{:S(2)}, u32[]{:S(2)}) collective-permute-start(f32[15,8,128]{2,1,0:T(8,128)S(1)} %get-tuple-element.21), channel_id=1, source_target_pairs={{0,112},{16,0},{32,16},{48,32},{64,48},{80,64},{96,80},{112,96},{1... | collective-permute-start | bytes 184328 | tf_op jit(solution)/shard_map/ppermute | solution.py:675
  37.1 18.2 %all-to-all-start.1 = ((f32[128,1,256]{2,1,0:T(1,128)}), f32[128,1,256]{2,1,0:T(1,128)S(1)}, u32[]{:S(2)}, u32[]{:S(2)}) async-start(f32[128,1,256]{2,1,0:T(1,128)} %bitcast.7), calls=%async_computation.1 | async-start | bytes 262144 | tf_op jit(solution)/shard_map/all_to_all | solution.py:692
  46.5 0.9 %copy-start.3 = (f32[3,4,144,128]{3,2,1,0:T(8,128)}, f32[3,4,144,128]{3,2,1,0:T(8,128)S(1)}, u32[]{:S(2)}) copy-start(f32[3,4,144,128]{3,2,1,0:T(8,128)S(1)} %get-tuple-element.25.ahead) | copy-start | bytes 2654212
  55.3 1.2 %copy-start.4 = (f32[3,4,144,128]{3,2,1,0:T(8,128)S(1)}, f32[3,4,144,128]{3,2,1,0:T(8,128)}, u32[]{:S(2)}) copy-start(f32[3,4,144,128]{3,2,1,0:T(8,128)} %copy-done.3) | copy-start | bytes 2654212
  60.9 14.2 %all-to-all-start.2 = ((f32[128,1,256]{2,1,0:T(1,128)}), f32[128,1,256]{2,1,0:T(1,128)S(1)}, u32[]{:S(2)}, u32[]{:S(2)}) async-start(f32[128,1,256]{2,1,0:T(1,128)} %bitcast.9), calls=%async_computation.2 | async-start | bytes 262144 | tf_op jit(solution)/shard_map/all_to_all | solution.py:692
